TPU v7x, 512 devices: a whole 4x4x16 slice. The times are simulated.
512 devices in a mesh: row: 16 (over z), col: 32 (over y, x, core).
Axes of the slice: x: 4, y: 4, z: 16, core: 2. Of those that a mesh axis runs over, the one named last changes fastest.
Arguments:
- velocity: float32 [3, 256, 256, 256], P(None, 'row', 'col'), may hold values from -6 to 6
- positions: bfloat16 [16384, 3, 128], P(('row', 'col')), may hold values from -4 to 4
- weights: bfloat16 [16384, 3, 8, 128], P(('row', 'col')), may hold values from 0 to 0.5
- stiffness: bfloat16 [16384], P(('row', 'col')), may hold values from 0.099609375 to 1
- rest_sq: bfloat16 [16384], P(('row', 'col')), may hold values from 1 to 8
- owner_column: int32 [16384, 1], P(('row', 'col')), may hold values from 0 to 31; in each aligned block of 32 rows (0 to 31, 32 to 63, ...) at most 3 rows name the same one
- brick_index: int32 [16384], P(('row', 'col')), may hold values from 0 to 63
Outputs:
- new_velocity: float32 [3, 256, 256, 256], P(None, 'row', 'col')
- marker_velocity: float32 [16384, 3, 128], P(('row', 'col'))
Inputs may be any that keep to these rules, and one draw needn't show every extreme that they name: `owner_column`: A block's brick lies on the device in the block's own device row and in this column; no device's 32 blocks name one column more than 3 times, and that many is reached.
All inputs are finite; a program needn't handle non-finite values.
Results may differ from a plain program's by a relative error of at most 0.0003.
Values may be sent and summed in bfloat16 or wider, within the bound.
No kernel may reach another device: no remote copies, remote signals or barrier semaphores. Data moves between devices by JAX's collectives and lax.ppermute only.
A program may use at most 64 MiB of HBM per device.

v0:
```python
import jax
import jax.numpy as jnp
import numpy as np
from jax import lax
from jax.experimental import pallas as pl
from jax.experimental.pallas import tpu as pltpu
from jax.sharding import PartitionSpec as P


DT_STEP = 0.5
VISCOSITY = 0.1
N = 256
FIRST = np.array([k for r in range(16) for k in ((0, 16) if r == 0 else (r, 32 - r))])
F32 = jnp.float32
BF16 = jnp.bfloat16
TURN = 2.0 * np.pi


def split_table(table):
    table = np.asarray(table, np.float32)
    high = table.astype(BF16)
    low = (table - high.astype(np.float32)).astype(BF16)
    return np.stack([high, low])


def rotation(angle):
    rows, cols = angle.shape
    out = np.zeros((rows, 2, 4, cols, 2, 4))
    for j in range(4):
        out[:, 0, j, :, 0, j] = np.cos(angle)
        out[:, 0, j, :, 1, j] = np.sin(angle)
        out[:, 1, j, :, 0, j] = -np.sin(angle)
        out[:, 1, j, :, 1, j] = np.cos(angle)
    return out.reshape(rows * 8, cols * 8)


def z_tables():
    z = np.arange(N)
    fore = np.zeros((32, 2, 4, N))
    back = np.zeros((32, 2, 4, N))
    for k in range(128):
        angle = TURN / N * (k * z % N)
        twice = 2.0 if k else 1.0
        sine = np.sin(angle) if k else -np.cos(np.pi * z)
        fore[k // 4, 0, k % 4] = np.cos(angle)
        fore[k // 4, 1, k % 4] = -sine
        back[k // 4, 0, k % 4] = twice * np.cos(angle) / N
        back[k // 4, 1, k % 4] = -twice * sine / N
    return split_table(fore.reshape(N, N)), split_table(back.reshape(N, N))


def y_tables():
    angle = TURN / 32 * np.outer(FIRST, np.arange(32))
    fore = split_table(rotation(angle))
    back = split_table(rotation(-angle.T) / N)
    small = TURN / 8 * np.outer(np.arange(8), np.arange(8))
    cosine, sine = (np.kron(np.eye(16), f(small)) for f in (np.cos, np.sin))
    lanes_fore = split_table(np.concatenate([cosine, sine], 1))
    lanes_back = split_table(np.concatenate([cosine, -sine], 1))
    phase = TURN / N * np.outer(FIRST, np.tile(np.arange(8), 16))
    twiddle = np.stack([np.cos(phase), np.sin(phase)]).astype(np.float32)[:, :, None, :]
    return fore, back, lanes_fore, lanes_back, twiddle


def x_tables():
    angle = TURN / 16 * np.outer(np.arange(16), np.arange(16))
    pair = np.eye(2)

    def both(turn):
        grid = np.zeros((16, 2, 8, 16, 2, 8))
        base = rotation(turn).reshape(16, 8, 16, 8)
        for p in range(2):
            grid[:, p, :, :, p, :] = base
        return grid

    main = both(angle).reshape(256, 256)
    extra = both(angle).reshape(8, 2, 2, 2, 4, 16, 2, 2, 4)[:, :, :, :, 0]
    extra = extra.transpose(0, 3, 1, 2, 4, 5, 6, 7).copy()
    extra[..., 1:] = 0.0
    extra = extra.reshape(64, 256)
    back_main = both(-angle).reshape(256, 256) / N
    back_extra = both(-angle).reshape(16, 2, 2, 4, 8, 2, 2, 2, 4)[..., 0]
    back_extra = back_extra.transpose(0, 1, 2, 3, 4, 7, 5, 6).copy()
    back_extra[:, :, :, 1:] = 0.0
    back_extra = back_extra.reshape(256, 64) / N
    back = np.concatenate([back_main, back_extra], 1)
    cosine, sine = (np.kron(f(angle), np.eye(8)) for f in (np.cos, np.sin))
    lanes_fore = split_table(np.concatenate([cosine, sine], 1))
    lanes_back = split_table(np.concatenate([cosine, -sine], 1))
    phase = TURN / N * np.outer(np.arange(16), np.repeat(np.arange(16), 8))
    wide = np.zeros((2, 320, 128), np.float32)
    k_main = np.repeat(np.arange(16), 16)
    k_extra = (2 * np.arange(8)[:, None, None, None] + np.arange(2)[None, None, :, None]
               + np.zeros((8, 2, 2, 2), int)).reshape(64)
    p_main = np.tile(np.repeat(np.arange(2), 8), 16)
    p_extra = np.tile(np.arange(2), 32)
    j_main = np.tile(np.arange(4), 64)
    first = np.concatenate([k_main, k_extra])
    wide[0] = np.cos(phase)[first]
    wide[1] = np.sin(phase)[first]
    marks = (first, np.concatenate([p_main, p_extra]), np.concatenate([j_main, np.zeros(64, int)]))
    reverse = np.kron(np.eye(16), np.eye(8)[(7 - np.arange(8))])
    negate = np.kron(np.eye(16), np.eye(8)[(-np.arange(8)) % 8])
    flips = np.concatenate([reverse, negate], 1).astype(BF16)
    return (split_table(main), split_table(extra), split_table(back), lanes_fore, lanes_back,
            wide.reshape(2, 40, 8, 128), marks, flips)


def dot(a, b, dims=((1,), (0,))):
    return lax.dot_general(a, b, (dims, ((), ())), preferred_element_type=F32)


def halves(x):
    high = x.astype(BF16)
    return high, (x - high.astype(F32)).astype(BF16)


def table_left(table, x, dims=((1,), (0,))):
    high, low = halves(x)
    return dot(table[0], high, dims) + dot(table[0], low, dims) + dot(table[1], high, dims)


def table_right(x, table, dims=((1,), (0,))):
    high, low = halves(x)
    return dot(high, table[0], dims) + dot(low, table[0], dims) + dot(high, table[1], dims)


def signs(shape):
    at = lax.broadcasted_iota(jnp.int32, shape, len(shape) - 2)
    return jnp.where(at % 8 < 4, 1.0, -1.0).astype(F32)


def swapped(x):
    return pltpu.roll(x, 4, 1) * signs((1, 8, 128))


def lane_pass(x, table):
    both = table_right(x, table)
    rows = x.shape[0]
    cosine = both[:, :128].reshape(rows // 8, 8, 128)
    sine = both[:, 128:].reshape(rows // 8, 8, 128)
    return cosine + swapped(sine)


def stacked(x):
    return jnp.concatenate([x[:, 128 * c:128 * c + 128] for c in range(3)], 0)


def unstacked(x):
    rows = x.shape[0] // 3
    return jnp.concatenate([x[rows * c:rows * c + rows] for c in range(3)], 1)


def twiddled(x, cosine, sine):
    groups = cosine.shape[0]
    turned = swapped(x)
    parts = [x[groups * c:groups * c + groups] * cosine + turned[groups * c:groups * c + groups] * sine
             for c in range(3)]
    return jnp.concatenate(parts, 0)


def tile_place(slot, c):
    at = 3 * slot + c
    return at >> 1, at & 1


def lane_half(shape=(8, 128)):
    return lax.broadcasted_iota(jnp.int32, shape, len(shape) - 1) // 64


def spread_kernel(params, owner, brick, positions, weights, out, slots, count, cubes):
    out[...] = jnp.zeros(out.shape, F32)
    for d in range(32):
        count[d] = 0
    for n in range(32):
        place = positions[n].astype(F32)
        segment = pltpu.roll(place, 127, 1) - place
        stretch = jnp.sum(segment * segment, axis=0, keepdims=True) / params[1, n]
        tension = 0.5 * params[0, n] * (stretch - 1.0) * segment
        force = tension - pltpu.roll(tension, 1, 1)
        w0, w1, w2 = (weights[n, a].astype(F32) for a in range(3))
        cells = (w0[:, None, :] * w1[None, :, :]).reshape(64, 128)
        cells = jnp.concatenate([cells, cells], 0)
        pushed = (force[:, None, :] * w2[None, :, :]).reshape(24, 128)
        cells_high, cells_low = halves(cells)
        pushed_high, pushed_low = halves(pushed)
        both = ((1,), (1,))
        cubes[n] = (dot(pushed_high, cells_high, both) + dot(pushed_low, cells_high, both)
                    + dot(pushed_high, cells_low, both))
    half = lane_half()
    lane = lax.broadcasted_iota(jnp.int32, (8, 128), 1)

    @pl.loop(0, 32)
    def _(n):
        d = owner[n, 0]
        s = count[d]
        count[d] = s + 1
        slots[n] = s
        for c in range(3):
            tile, side = tile_place(s, c)
            out[d, tile] += jnp.where(half == side, cubes[n, 8 * c:8 * c + 8, :], 0.0)
        out[d, 4] += jnp.where(lane == 64 + s, brick[n].astype(F32), 0.0)


def advect_kernel(table, velocity, x_low, x_high, y_low, y_high, spectrum, turned):
    u = [velocity[c].reshape(128, 256) for c in range(3)]
    sub = lax.broadcasted_iota(jnp.int32, (16, 8, 256), 1)
    rows = []
    for c in range(3):
        v = velocity[c]
        turned[c] = jnp.transpose(u[c]).reshape(32, 8, 128)
        ahead = jnp.concatenate([v[1:], x_high[c]], 0)
        behind = jnp.concatenate([x_low[c], v[:-1]], 0)
        total = u[0] * (ahead - behind).reshape(128, 256)
        ahead = jnp.where(sub == 7, y_high[c], pltpu.roll(v, 7, 1))
        behind = jnp.where(sub == 0, y_low[c], pltpu.roll(v, 1, 1))
        total = total + u[1] * (ahead - behind).reshape(128, 256)
        total = total + u[2] * (pltpu.roll(u[c], 255, 1) - pltpu.roll(u[c], 1, 1))
        rows.append(u[c] - (0.5 * DT_STEP) * total)
    star = jnp.concatenate(rows, 0)
    spectrum[...] = table_left(table, star, ((1,), (1,)))


def gather_kernel(ids, table, pushes, spectrum, out, force0, force1, force2):
    forces = (force0, force1, force2)
    for force in forces:
        force[...] = jnp.zeros(force.shape, F32)
    half = lane_half()

    @pl.loop(0, 32, unroll=4)
    def _(src):
        tiles = [pushes[src, t] for t in range(5)]
        turned = [pltpu.roll(tile, 64, 1) for tile in tiles]
        for slot in range(3):
            brick = ids[src, slot]
            x_half, z_block = brick >> 5, brick & 31
            for c in range(3):
                tile, side = tile_place(slot, c)
                wide = jnp.where(half == side, tiles[tile], turned[tile])
                forces[c][z_block] += jnp.where(half == x_half, wide, 0.0)

    field = jnp.concatenate([force[...].reshape(256, 128) for force in forces], 1)
    total = spectrum[...] + table_left(table, DT_STEP * field)
    out[...] = total.reshape(32, 8, 384)


def reply_kernel(ids, turned, out):
    half = lane_half()

    @pl.loop(0, 32, unroll=4)
    def _(src):
        wides = []
        for slot in range(3):
            brick = ids[src, slot]
            x_half, z_block = brick >> 5, brick & 31
            for c in range(3):
                tile = turned[c, z_block]
                wides.append(jnp.where(half == x_half, tile, pltpu.roll(tile, 64, 1)))
        wides.append(wides[0])
        for t in range(5):
            out[src, t] = jnp.where(half == 0, wides[2 * t], wides[2 * t + 1])


def interpolate_kernel(owner, slots, replies, weights, out):
    half = lane_half()
    for n in range(32):
        d, s = owner[n, 0], slots[n]
        parts = []
        for c in range(3):
            tile, side = tile_place(s, c)
            cube = replies[d, tile]
            parts.append(jnp.where(half == side, cube, pltpu.roll(cube, 64, 1)))
        cube_high, cube_low = halves(jnp.concatenate(parts, 0)[:, :64])
        w0, w1, w2 = (weights[n, a].astype(F32) for a in range(3))
        cells_high, cells_low = halves((w0[:, None, :] * w1[None, :, :]).reshape(64, 128))
        partial = dot(cube_high, cells_high) + dot(cube_low, cells_high) + dot(cube_high, cells_low)
        out[n] = jnp.sum(partial.reshape(3, 8, 128) * w2[None], axis=1)


def y_kernel(left, lanes, twiddle, values, out):
    spectrum = table_left(left, values[...].reshape(256, 384))
    spectrum = stacked(spectrum).reshape(96, 8, 128)
    spectrum = twiddled(spectrum, twiddle[0], twiddle[1])
    spectrum = lane_pass(spectrum.reshape(768, 128), lanes)
    out[...] = unstacked(spectrum.reshape(768, 128)).reshape(16, 16, 384)


def x_kernel(flags, left, left_extra, back, lanes, lanes_back, twiddle, flips, waves, damping, values, out):
    packed = stacked(values[...].reshape(256, 384))
    high, low = halves(packed)
    flipped = dot(high, flips[...]) + dot(low, flips[...])
    by_pair = (3, 16, 2, 8, 128)
    reverse = flipped[:, :128].reshape(by_pair)
    negate = flipped[:, 128:].reshape(by_pair)
    packed = packed.reshape(by_pair)
    own = flags[0] == 1
    first = jnp.where(own, negate[:, :, 0:1], reverse[:, :, 1:2])
    second = jnp.where(own, reverse[:, :, 1:2], reverse[:, :, 0:1])
    mirrored = jnp.concatenate([first, second], 2) * signs((1, 1, 1, 8, 128))
    sub = lax.broadcasted_iota(jnp.int32, (1, 1, 1, 8, 128), 3)
    lowest = (sub % 4 == 0) & (flags[1] == 1)
    main = jnp.where(lowest, 0.5 * (packed + mirrored), packed)
    extra = jnp.where(lowest, 0.5 * (packed - mirrored), 0.0)
    main = table_left(left, unstacked(main.reshape(768, 128)))
    extra = table_left(left_extra, unstacked(extra.reshape(768, 128)))
    spectrum = stacked(jnp.concatenate([main, extra], 0)).reshape(120, 8, 128)
    spectrum = twiddled(spectrum, twiddle[0], twiddle[1])
    spectrum = lane_pass(spectrum.reshape(960, 128), lanes).reshape(3, 320, 128)
    normal = waves[0] * spectrum[0] + waves[1] * spectrum[1] + waves[2] * spectrum[2]
    damp = damping[...]
    projected = jnp.concatenate([(spectrum[c] - waves[c] * normal) * damp for c in range(3)], 0)
    projected = lane_pass(projected, lanes_back)
    projected = twiddled(projected, twiddle[0], -twiddle[1])
    projected = unstacked(projected.reshape(960, 128))
    out[...] = table_left(back, projected).reshape(16, 16, 384)


def y_back_kernel(back, lanes, twiddle, values, out):
    spectrum = lane_pass(stacked(values[...].reshape(256, 384)), lanes)
    spectrum = twiddled(spectrum, twiddle[0], -twiddle[1])
    spectrum = table_left(back, unstacked(spectrum.reshape(768, 128)))
    out[...] = spectrum.reshape(32, 8, 384)


def z_back_kernel(back, values, out):
    spectrum = values[...].reshape(256, 384)
    field = table_right(jnp.transpose(spectrum), back)
    out[...] = field.reshape(3, 16, 8, 256)


VMEM = pl.BlockSpec(memory_space=pltpu.VMEM)
SMEM = pl.BlockSpec(memory_space=pltpu.SMEM)


def call(kernel, specs, shapes, scratch=(), out_specs=None):
    single = not isinstance(shapes, tuple)
    structs = [jax.ShapeDtypeStruct(s, F32) if isinstance(s, list) else s
               for s in ((shapes,) if single else shapes)]
    outs = out_specs or [VMEM] * len(structs)
    return pl.pallas_call(
        kernel,
        out_shape=structs[0] if single else structs,
        in_specs=specs,
        out_specs=outs[0] if single else outs,
        scratch_shapes=list(scratch),
        compiler_params=pltpu.CompilerParams(vmem_limit_bytes=48 << 20),
    )


def signed(indices):
    return jnp.where(indices <= (N - 1) // 2, indices, indices - N)


def wave_tables(marks, row, col):
    first, pair, slot = (jnp.asarray(m, jnp.int32)[:, None] for m in marks)
    lane = jnp.arange(128, dtype=jnp.int32)[None, :]
    nyquist = jnp.arange(320, dtype=jnp.int32)[:, None] >= 256
    second = jnp.where(row == 0, 16, 32 - row)
    index_x = first + 16 * (lane // 8)
    index_y = jnp.where(pair == 0, row, second) + 32 * (lane % 8)
    index_z = jnp.where(nyquist, N // 2, 4 * col + slot) + 0 * lane
    scale = 2.0 * jnp.pi / N
    full_sq, waves = 0.0, []
    for index in (index_x, index_y, index_z):
        full = scale * signed(index).astype(F32)
        full_sq = full_sq + full * full
        waves.append(jnp.where(2 * index == N, 0.0, full))
    wave_sq = waves[0] * waves[0] + waves[1] * waves[1] + waves[2] * waves[2]
    still = wave_sq == 0.0
    inverse = jnp.where(still, 0.0, lax.rsqrt(jnp.where(still, 1.0, wave_sq)))
    units = jnp.stack([w * inverse for w in waves])
    return units, 1.0 / (1.0 + DT_STEP * VISCOSITY * full_sq)


def moved(x, axis):
    return lax.all_to_all(x, axis, split_axis=0, concat_axis=0, tiled=True)


def neighbours(plane_low, plane_high, axis):
    count = lax.axis_size(axis)
    up = [(i, (i + 1) % count) for i in range(count)]
    down = [((i + 1) % count, i) for i in range(count)]
    return lax.ppermute(plane_high, axis, up), lax.ppermute(plane_low, axis, down)


def local(velocity, positions, weights, stiffness, rest_sq, owner_column, brick_index):
    row, col = lax.axis_index("row"), lax.axis_index("col")
    z_fore, z_back = z_tables()
    y_fore, y_back, y_lanes, y_lanes_back, y_twiddle = y_tables()
    x_fore, x_extra, x_back, x_lanes, x_lanes_back, x_twiddle, marks, flips = x_tables()
    flags = jnp.stack([row == 0, col == 0]).astype(jnp.int32)
    units, damping = wave_tables(marks, row, col)

    params = jnp.stack([stiffness, rest_sq]).astype(F32)
    pushes, slots = call(
        spread_kernel, [SMEM, SMEM, SMEM, VMEM, VMEM],
        ([32, 5, 8, 128], jax.ShapeDtypeStruct((32,), jnp.int32)),
        [pltpu.SMEM((32,), jnp.int32), pltpu.VMEM((32, 24, 128), F32)], [VMEM, SMEM],
    )(params, owner_column, brick_index, positions, weights)
    x_low, x_high = neighbours(velocity[:, :1], velocity[:, 15:], "row")
    y_low, y_high = neighbours(velocity[:, :, :1], velocity[:, :, 7:], "col")
    pushes = moved(pushes, "col")
    ids = pushes[:, 4, 0, 64:67].astype(jnp.int32)

    spectrum, turned = call(advect_kernel, [VMEM] * 6, ([256, 384], [3, 32, 8, 128]))(
        z_fore, velocity, x_low, x_high, y_low, y_high)
    spectrum = call(gather_kernel, [SMEM, VMEM, VMEM, VMEM], [32, 8, 384],
                    [pltpu.VMEM((32, 8, 128), F32)] * 3)(ids, z_fore, pushes, spectrum)
    spectrum = moved(spectrum, "col")
    spectrum = call(y_kernel, [VMEM] * 4, [16, 16, 384])(y_fore, y_lanes, y_twiddle, spectrum)
    spectrum = moved(spectrum, "row")
    spectrum = call(x_kernel, [SMEM] + [VMEM] * 10, [16, 16, 384])(
        flags, x_fore, x_extra, x_back, x_lanes, x_lanes_back, x_twiddle, flips, units, damping, spectrum)
    spectrum = moved(spectrum, "row")
    spectrum = call(y_back_kernel, [VMEM] * 4, [32, 8, 384])(y_back, y_lanes_back, y_twiddle, spectrum)
    spectrum = moved(spectrum, "col")
    new_velocity = call(z_back_kernel, [VMEM] * 2, [3, 16, 8, 256])(z_back, spectrum)

    replies = moved(call(reply_kernel, [SMEM, VMEM], [32, 5, 8, 128])(ids, turned), "col")
    marker_velocity = call(interpolate_kernel, [SMEM, SMEM, VMEM, VMEM], [32, 3, 128])(
        owner_column, slots, replies, weights)
    return new_velocity, marker_velocity


def solution(mesh):
    both = ("row", "col")
    placed = (
        P(None, "row", "col", None),
        P(both, None, None),
        P(both, None, None, None),
        P(both),
        P(both),
        P(both, None),
        P(both),
    )
    return jax.shard_map(
        local,
        mesh=mesh,
        in_specs=placed,
        out_specs=(P(None, "row", "col", None), P(both, None, None)),
        check_vma=False,
    )
```

profile of v0, /device:TPU:1, one launch (start us, length us, event | category | flops | bytes accessed | tf_op | source)
XLA Modules:
  0.0 162.7 jit_solution(7376133967031623727)
XLA Ops:
  4.4 4.2 %shard_map.239 = (f32[32,5,8,128]{3,2,1,0:T(8,128)}, s32[32]{0:T(128)S(1)}) custom-call(f32[2,32]{1,0:T(2,128)S(1)} %maximum_convert_fusion.params, s32[32,1]{1,0:T(8,128)S(1)} %copy.33.owner, s32[32]{0:T(128)S(1)} %copy-done.17, bf16[32,3,128]{2,1,0:T(4,128)(2,1)S(1)} %copy.34.positions, bf16[32,3,8,128]{3,2,1,0:T(8,128)(2,1)S(1)} %copy-done.1), custom_call_target="tpu_custom_call" | custom-call | tf_op jit(solution)/shard_map/pallas_call | solution.py:395
  8.6 10.6 %all-to-all-start = ((f32[32,5,8,128]{3,2,1,0:T(8,128)}), f32[32,5,8,128]{3,2,1,0:T(8,128)S(1)}, u32[]{:S(2)}, u32[]{:S(2)}) async-start(f32[32,5,8,128]{3,2,1,0:T(8,128)} %get-tuple-element.6), calls=%async_computation | async-start | bytes 1310720 | tf_op jit(solution)/shard_map/all_to_all | solution.py:376
  19.3 2.3 %collective-permute-start.3 = (f32[3,16,1,256]{3,2,1,0:T(1,128)S(1)}, f32[3,16,1,256]{3,2,1,0:T(1,128)S(1)}, u32[]{:S(2)}, u32[]{:S(2)}) collective-permute-start(f32[3,16,1,256]{3,2,1,0:T(1,128)S(1)} %get-tuple-element.14), channel_id=1, source_target_pairs={{1,0},{2,1},{3,2},{4,3},{5,4},{6,5},{7,6},{8,7},{9,8},{10,9},{11,1... | collective-permute-start | bytes 147464 | tf_op jit(solution)/shard_map/ppermute | solution.py:383
  21.6 3.3 %collective-permute-start.2 = (f32[3,16,1,256]{3,2,1,0:T(1,128)S(1)}, f32[3,16,1,256]{3,2,1,0:T(1,128)S(1)}, u32[]{:S(2)}, u32[]{:S(2)}) collective-permute-start(f32[3,16,1,256]{3,2,1,0:T(1,128)S(1)} %get-tuple-element.15), channel_id=1, source_target_pairs={{0,1},{1,2},{2,3},{3,4},{4,5},{5,6},{6,7},{7,8},{8,9},{9,10},{10,1... | collective-permute-start | bytes 147464 | tf_op jit(solution)/shard_map/ppermute | solution.py:383
  24.9 9.3 %collective-permute-start.1 = (f32[3,1,8,256]{3,2,1,0:T(8,128)S(1)}, f32[3,1,8,256]{3,2,1,0:T(8,128)S(1)}, u32[]{:S(2)}, u32[]{:S(2)}) collective-permute-start(f32[3,1,8,256]{3,2,1,0:T(8,128)S(1)} %get-tuple-element.16), channel_id=1, source_target_pairs={{32,0},{64,32},{96,64},{128,96},{160,128},{192,160},{224,192},{256... | collective-permute-start | bytes 73736 | tf_op jit(solution)/shard_map/ppermute | solution.py:383
  34.2 1.9 %collective-permute-start = (f32[3,1,8,256]{3,2,1,0:T(8,128)S(1)}, f32[3,1,8,256]{3,2,1,0:T(8,128)S(1)}, u32[]{:S(2)}, u32[]{:S(2)}) collective-permute-start(f32[3,1,8,256]{3,2,1,0:T(8,128)S(1)} %get-tuple-element.17), channel_id=1, source_target_pairs={{0,32},{32,64},{64,96},{96,128},{128,160},{160,192},{192,224},{224... | collective-permute-start | bytes 73736 | tf_op jit(solution)/shard_map/ppermute | solution.py:383
  36.1 3.8 %collective-permute-done.x_low = f32[3,1,8,256]{3,2,1,0:T(8,128)S(1)} collective-permute-done((f32[3,1,8,256]{3,2,1,0:T(8,128)S(1)}, f32[3,1,8,256]{3,2,1,0:T(8,128)S(1)}, u32[]{:S(2)}, u32[]{:S(2)}) %collective-permute-start) | collective-permute-done | bytes 24608 | tf_op jit(solution)/shard_map/ppermute | solution.py:383
  40.7 3.1 %shard_map.241 = f32[32,8,384]{2,1,0:T(8,128)} custom-call(s32[32,3]{1,0:T(8,128)S(1)} %bitcast.5, bf16[2,256,256]{2,1,0:T(8,128)(2,1)S(1)} %copy-done, f32[32,5,8,128]{3,2,1,0:T(8,128)S(1)} %all-to-all-done.pushes, f32[256,384]{1,0:T(8,128)S(1)} %get-tuple-element.7.spectrum), custom_call_target="tpu_custom_call" | custom-call | tf_op jit(solution)/shard_map/pallas_call | solution.py:407
  43.8 10.1 %all-to-all-start.1 = ((f32[32,8,384]{2,1,0:T(8,128)}), f32[32,8,384]{2,1,0:T(8,128)S(1)}, u32[]{:S(2)}, u32[]{:S(2)}) async-start(f32[32,8,384]{2,1,0:T(8,128)} %shard_map.241), calls=%async_computation.1 | async-start | bytes 786432 | tf_op jit(solution)/shard_map/all_to_all | solution.py:376
  53.9 10.2 %all-to-all-done.1.values = f32[32,8,384]{2,1,0:T(8,128)S(1)} async-done(((f32[32,8,384]{2,1,0:T(8,128)}), f32[32,8,384]{2,1,0:T(8,128)S(1)}, u32[]{:S(2)}, u32[]{:S(2)}) %all-to-all-start.1) | async-done | bytes 393248 | tf_op jit(solution)/shard_map/all_to_all | solution.py:376
  64.1 1.5 shard_map.242
  65.6 5.7 %all-to-all-start.2 = ((f32[16,16,384]{2,1,0:T(8,128)}), f32[16,16,384]{2,1,0:T(8,128)S(1)}, u32[]{:S(2)}, u32[]{:S(2)}) async-start(f32[16,16,384]{2,1,0:T(8,128)} %shard_map.242), calls=%async_computation.2 | async-start | bytes 786432 | tf_op jit(solution)/shard_map/all_to_all | solution.py:376
  74.2 14.3 %all-to-all-done.2.values = f32[16,16,384]{2,1,0:T(8,128)S(1)} async-done(((f32[16,16,384]{2,1,0:T(8,128)}), f32[16,16,384]{2,1,0:T(8,128)S(1)}, u32[]{:S(2)}, u32[]{:S(2)}) %all-to-all-start.2) | async-done | bytes 393248 | tf_op jit(solution)/shard_map/all_to_all | solution.py:376
  88.6 4.4 %shard_map.243 = f32[16,16,384]{2,1,0:T(8,128)} custom-call(s32[2]{0:T(128)S(1)} %add_convert_fusion.flags, bf16[2,256,256]{2,1,0:T(8,128)(2,1)S(1)} %copy-done.7, bf16[2,64,256]{2,1,0:T(8,128)(2,1)S(1)} %copy-done.16, bf16[2,256,320]{2,1,0:T(8,128)(2,1)S(1)} %copy-done.4, bf16[2,128,256]{2,1,0:T(8,128)(2,1)S(1)} %copy-done.12, ...), custom_call_target="tpu_custom_call" | custom-call | tf_op jit(solution)/shard_map/pallas_call | solution.py:412
  92.9 12.8 %all-to-all-start.3 = ((f32[16,16,384]{2,1,0:T(8,128)}), f32[16,16,384]{2,1,0:T(8,128)S(1)}, u32[]{:S(2)}, u32[]{:S(2)}) async-start(f32[16,16,384]{2,1,0:T(8,128)} %shard_map.243), calls=%async_computation.3 | async-start | bytes 786432 | tf_op jit(solution)/shard_map/all_to_all | solution.py:376
  105.7 2.5 %shard_map.246 = f32[32,5,8,128]{3,2,1,0:T(8,128)} custom-call(s32[32,3]{1,0:T(8,128)S(1)} %bitcast.6, f32[3,32,8,128]{3,2,1,0:T(8,128)S(1)} %get-tuple-element.9.turned), custom_call_target="tpu_custom_call" | custom-call | tf_op jit(solution)/shard_map/pallas_call | solution.py:419
  108.2 15.1 %all-to-all-done.3.values = f32[16,16,384]{2,1,0:T(8,128)S(1)} async-done(((f32[16,16,384]{2,1,0:T(8,128)}), f32[16,16,384]{2,1,0:T(8,128)S(1)}, u32[]{:S(2)}, u32[]{:S(2)}) %all-to-all-start.3) | async-done | bytes 393248 | tf_op jit(solution)/shard_map/all_to_all | solution.py:376
  123.3 11.0 %all-to-all-start.5 = ((f32[32,5,8,128]{3,2,1,0:T(8,128)}), f32[32,5,8,128]{3,2,1,0:T(8,128)S(1)}, u32[]{:S(2)}, u32[]{:S(2)}) async-start(f32[32,5,8,128]{3,2,1,0:T(8,128)} %shard_map.246), calls=%async_computation.5 | async-start | bytes 1310720 | tf_op jit(solution)/shard_map/all_to_all | solution.py:376
  134.3 1.9 %shard_map.244 = f32[32,8,384]{2,1,0:T(8,128)} custom-call(bf16[2,256,256]{2,1,0:T(8,128)(2,1)S(1)} %copy-done.6, bf16[2,128,256]{2,1,0:T(8,128)(2,1)S(1)} %copy-done.10, f32[2,32,1,128]{3,2,1,0:T(1,128)S(1)} %copy-done.14, f32[16,16,384]{2,1,0:T(8,128)S(1)} %all-to-all-done.3.values), custom_call_target="tpu_custom_call" | custom-call | tf_op jit(solution)/shard_map/pallas_call | solution.py:415
  136.2 11.0 %all-to-all-done.5.replies = f32[32,5,8,128]{3,2,1,0:T(8,128)S(1)} async-done(((f32[32,5,8,128]{3,2,1,0:T(8,128)}), f32[32,5,8,128]{3,2,1,0:T(8,128)S(1)}, u32[]{:S(2)}, u32[]{:S(2)}) %all-to-all-start.5) | async-done | bytes 655392 | tf_op jit(solution)/shard_map/all_to_all | solution.py:376
  147.2 4.1 %all-to-all-start.4 = ((f32[32,8,384]{2,1,0:T(8,128)}), f32[32,8,384]{2,1,0:T(8,128)S(1)}, u32[]{:S(2)}, u32[]{:S(2)}) async-start(f32[32,8,384]{2,1,0:T(8,128)} %shard_map.244), calls=%async_computation.4 | async-start | bytes 786432 | tf_op jit(solution)/shard_map/all_to_all | solution.py:376
  151.3 1.4 shard_map.247
  153.4 8.2 %all-to-all-done.4.values = f32[32,8,384]{2,1,0:T(8,128)S(1)} async-done(((f32[32,8,384]{2,1,0:T(8,128)}), f32[32,8,384]{2,1,0:T(8,128)S(1)}, u32[]{:S(2)}, u32[]{:S(2)}) %all-to-all-start.4) | async-done | bytes 393248 | tf_op jit(solution)/shard_map/all_to_all | solution.py:376
  161.6 1.1 shard_map.245
  (66 shorter events, 8.0 us)
Async XLA Ops:
  8.6 32.0 %all-to-all-start = ((f32[32,5,8,128]{3,2,1,0:T(8,128)}), f32[32,5,8,128]{3,2,1,0:T(8,128)S(1)}, u32[]{:S(2)}, u32[]{:S(2)}) async-start(f32[32,5,8,128]{3,2,1,0:T(8,128)} %get-tuple-element.6), calls=%async_computation | async-start | bytes 1310720 | tf_op jit(solution)/shard_map/all_to_all | solution.py:376
  19.2 20.8 %copy-start = (bf16[2,256,256]{2,1,0:T(8,128)(2,1)S(1)}, bf16[2,256,256]{2,1,0:T(8,128)(2,1)}, u32[]{:S(2)}) copy-start(bf16[2,256,256]{2,1,0:T(8,128)(2,1)} %constant.110.clone.table) | copy-start | bytes 786436
  19.3 20.7 %collective-permute-start.3 = (f32[3,16,1,256]{3,2,1,0:T(1,128)S(1)}, f32[3,16,1,256]{3,2,1,0:T(1,128)S(1)}, u32[]{:S(2)}, u32[]{:S(2)}) collective-permute-start(f32[3,16,1,256]{3,2,1,0:T(1,128)S(1)} %get-tuple-element.14), channel_id=1, source_target_pairs={{1,0},{2,1},{3,2},{4,3},{5,4},{6,5},{7,6},{8,7},{9,8},{10,9},{11,1... | collective-permute-start | bytes 147464 | tf_op jit(solution)/shard_map/ppermute | solution.py:383
  21.6 18.4 %collective-permute-start.2 = (f32[3,16,1,256]{3,2,1,0:T(1,128)S(1)}, f32[3,16,1,256]{3,2,1,0:T(1,128)S(1)}, u32[]{:S(2)}, u32[]{:S(2)}) collective-permute-start(f32[3,16,1,256]{3,2,1,0:T(1,128)S(1)} %get-tuple-element.15), channel_id=1, source_target_pairs={{0,1},{1,2},{2,3},{3,4},{4,5},{5,6},{6,7},{7,8},{8,9},{9,10},{10,1... | collective-permute-start | bytes 147464 | tf_op jit(solution)/shard_map/ppermute | solution.py:383
  24.9 11.2 %collective-permute-start.1 = (f32[3,1,8,256]{3,2,1,0:T(8,128)S(1)}, f32[3,1,8,256]{3,2,1,0:T(8,128)S(1)}, u32[]{:S(2)}, u32[]{:S(2)}) collective-permute-start(f32[3,1,8,256]{3,2,1,0:T(8,128)S(1)} %get-tuple-element.16), channel_id=1, source_target_pairs={{32,0},{64,32},{96,64},{128,96},{160,128},{192,160},{224,192},{256... | collective-permute-start | bytes 73736 | tf_op jit(solution)/shard_map/ppermute | solution.py:383
  34.2 5.8 %collective-permute-start = (f32[3,1,8,256]{3,2,1,0:T(8,128)S(1)}, f32[3,1,8,256]{3,2,1,0:T(8,128)S(1)}, u32[]{:S(2)}, u32[]{:S(2)}) collective-permute-start(f32[3,1,8,256]{3,2,1,0:T(8,128)S(1)} %get-tuple-element.17), channel_id=1, source_target_pairs={{0,32},{32,64},{64,96},{96,128},{128,160},{160,192},{192,224},{224... | collective-permute-start | bytes 73736 | tf_op jit(solution)/shard_map/ppermute | solution.py:383
  43.8 20.3 %copy-start.8 = (bf16[2,256,256]{2,1,0:T(8,128)(2,1)S(1)}, bf16[2,256,256]{2,1,0:T(8,128)(2,1)}, u32[]{:S(2)}) copy-start(bf16[2,256,256]{2,1,0:T(8,128)(2,1)} %constant.111.clone.left) | copy-start | bytes 786436
  43.8 20.3 %copy-start.13 = (bf16[2,128,256]{2,1,0:T(8,128)(2,1)S(1)}, bf16[2,128,256]{2,1,0:T(8,128)(2,1)}, u32[]{:S(2)}) copy-start(bf16[2,128,256]{2,1,0:T(8,128)(2,1)} %constant.112.clone.lanes) | copy-start | bytes 393220
  43.8 20.3 %copy-start.14 = (f32[2,32,1,128]{3,2,1,0:T(1,128)S(1)}, f32[2,32,1,128]{3,2,1,0:T(1,128)}, u32[]{:S(2)}) copy-start(f32[2,32,1,128]{3,2,1,0:T(1,128)} %constant.113.clone.twiddle) | copy-start | bytes 98308
  43.8 20.3 %all-to-all-start.1 = ((f32[32,8,384]{2,1,0:T(8,128)}), f32[32,8,384]{2,1,0:T(8,128)S(1)}, u32[]{:S(2)}, u32[]{:S(2)}) async-start(f32[32,8,384]{2,1,0:T(8,128)} %shard_map.241), calls=%async_computation.1 | async-start | bytes 786432 | tf_op jit(solution)/shard_map/all_to_all | solution.py:376
  65.6 22.9 %all-to-all-start.2 = ((f32[16,16,384]{2,1,0:T(8,128)}), f32[16,16,384]{2,1,0:T(8,128)S(1)}, u32[]{:S(2)}, u32[]{:S(2)}) async-start(f32[16,16,384]{2,1,0:T(8,128)} %shard_map.242), calls=%async_computation.2 | async-start | bytes 786432 | tf_op jit(solution)/shard_map/all_to_all | solution.py:376
  73.5 15.1 %copy-start.12 = (bf16[2,128,256]{2,1,0:T(8,128)(2,1)S(1)}, bf16[2,128,256]{2,1,0:T(8,128)(2,1)}, u32[]{:S(2)}) copy-start(bf16[2,128,256]{2,1,0:T(8,128)(2,1)} %constant.117.clone.lanes) | copy-start | bytes 393220
  73.5 15.1 %copy-start.15 = (bf16[128,256]{1,0:T(8,128)(2,1)S(1)}, bf16[128,256]{1,0:T(8,128)(2,1)}, u32[]{:S(2)}) copy-start(bf16[128,256]{1,0:T(8,128)(2,1)} %constant.120.clone.flips) | copy-start | bytes 196612
  73.5 15.1 %copy-start.16 = (bf16[2,64,256]{2,1,0:T(8,128)(2,1)S(1)}, bf16[2,64,256]{2,1,0:T(8,128)(2,1)}, u32[]{:S(2)}) copy-start(bf16[2,64,256]{2,1,0:T(8,128)(2,1)} %constant.115.clone.left_extra) | copy-start | bytes 196612
  73.8 14.7 %copy-start.4 = (bf16[2,256,320]{2,1,0:T(8,128)(2,1)S(1)}, bf16[2,256,320]{2,1,0:T(8,128)(2,1)}, u32[]{:S(2)}) copy-start(bf16[2,256,320]{2,1,0:T(8,128)(2,1)} %constant.116.clone.back) | copy-start | bytes 983044
  73.8 14.7 %copy-start.5 = (f32[2,40,8,128]{3,2,1,0:T(8,128)S(1)}, f32[2,40,8,128]{3,2,1,0:T(8,128)}, u32[]{:S(2)}) copy-start(f32[2,40,8,128]{3,2,1,0:T(8,128)} %constant.119.clone.twiddle) | copy-start | bytes 983044
  73.8 14.7 %copy-start.7 = (bf16[2,256,256]{2,1,0:T(8,128)(2,1)S(1)}, bf16[2,256,256]{2,1,0:T(8,128)(2,1)}, u32[]{:S(2)}) copy-start(bf16[2,256,256]{2,1,0:T(8,128)(2,1)} %constant.114.clone.left) | copy-start | bytes 786436
  73.9 14.7 %copy-start.11 = (bf16[2,128,256]{2,1,0:T(8,128)(2,1)S(1)}, bf16[2,128,256]{2,1,0:T(8,128)(2,1)}, u32[]{:S(2)}) copy-start(bf16[2,128,256]{2,1,0:T(8,128)(2,1)} %constant.118.clone.lanes_back) | copy-start | bytes 393220
  92.9 30.4 %all-to-all-start.3 = ((f32[16,16,384]{2,1,0:T(8,128)}), f32[16,16,384]{2,1,0:T(8,128)S(1)}, u32[]{:S(2)}, u32[]{:S(2)}) async-start(f32[16,16,384]{2,1,0:T(8,128)} %shard_map.243), calls=%async_computation.3 | async-start | bytes 786432 | tf_op jit(solution)/shard_map/all_to_all | solution.py:376
  108.2 26.1 %copy-start.6 = (bf16[2,256,256]{2,1,0:T(8,128)(2,1)S(1)}, bf16[2,256,256]{2,1,0:T(8,128)(2,1)}, u32[]{:S(2)}) copy-start(bf16[2,256,256]{2,1,0:T(8,128)(2,1)} %constant.121.clone.back) | copy-start | bytes 786436
  108.2 26.1 %copy-start.10 = (bf16[2,128,256]{2,1,0:T(8,128)(2,1)S(1)}, bf16[2,128,256]{2,1,0:T(8,128)(2,1)}, u32[]{:S(2)}) copy-start(bf16[2,128,256]{2,1,0:T(8,128)(2,1)} %constant.122.clone.lanes) | copy-start | bytes 393220
  123.3 23.9 %all-to-all-start.5 = ((f32[32,5,8,128]{3,2,1,0:T(8,128)}), f32[32,5,8,128]{3,2,1,0:T(8,128)S(1)}, u32[]{:S(2)}, u32[]{:S(2)}) async-start(f32[32,5,8,128]{3,2,1,0:T(8,128)} %shard_map.246), calls=%async_computation.5 | async-start | bytes 1310720 | tf_op jit(solution)/shard_map/all_to_all | solution.py:376
  136.2 15.1 %copy-start.2 = (bf16[32,3,8,128]{3,2,1,0:T(8,128)(2,1)S(1)}, bf16[32,3,8,128]{3,2,1,0:T(8,128)(2,1)}, u32[]{:S(2)}) copy-start(bf16[32,3,8,128]{3,2,1,0:T(8,128)(2,1)} %weights.3) | copy-start | bytes 589828
  147.2 14.4 %all-to-all-start.4 = ((f32[32,8,384]{2,1,0:T(8,128)}), f32[32,8,384]{2,1,0:T(8,128)S(1)}, u32[]{:S(2)}, u32[]{:S(2)}) async-start(f32[32,8,384]{2,1,0:T(8,128)} %shard_map.244), calls=%async_computation.4 | async-start | bytes 786432 | tf_op jit(solution)/shard_map/all_to_all | solution.py:376
  (9 other events, 25.8 us)
where the time goes:
time: 164 us; the launch traced here: 163 us
  starting transfers between devices  71 us (43%)
  waiting for transfers between devices  62.7 us (38%)
  Pallas kernels  20.7 us (13%)
  local copies, waits for them, and re-layouts  6.5 us (4%)
    all_to_all x6, waiting for transfers between devices, moved(): return lax.all_to_all(x, axis, split_axis=0, concat_axis=0, tiled=True)  58.8 us
    all_to_all x6, starting transfers between devices, moved(): return lax.all_to_all(x, axis, split_axis=0, concat_axis=0, tiled=True)  54.2 us
    ppermute x2, starting transfers between devices, neighbours(): lax.ppermute(plane_low, axis, down)  11.5 us
    unnamed x49, local copies, waits for them, and re-layouts  6.43 us
    ppermute x2, starting transfers between devices, neighbours(): lax.ppermute(plane_high, axis, up)  5.23 us
    pallas_call x1, Pallas kernels, local(): call(x_kernel, [SMEM] + [VMEM] * 10, [16, 16, 384])  4.36 us
    pallas_call x1, Pallas kernels, local(): call(spread_kernel, [SMEM, SMEM, SMEM, VMEM, VMEM], ([32, 5, 8, 128], jax...  4.23 us
    ppermute x2, waiting for transfers between devices, neighbours(): lax.ppermute(plane_high, axis, up)  3.85 us
  transfers between devices with their start and end apart: 10, of which 6 were waited for; matrix products, arithmetic and copies ran while one was open for 1% of the time, Pallas kernels for 4%

commit v1 on v0

--- a/solution.py
+++ b/solution.py
@@ -168,38 +168,110 @@
     return lax.broadcasted_iota(jnp.int32, shape, len(shape) - 1) // 64
 
 
-def spread_kernel(params, owner, brick, positions, weights, out, slots, count, cubes):
-    out[...] = jnp.zeros(out.shape, F32)
+def to_exponent(largest):
+    return jnp.ceil(16.0 * jnp.log(jnp.maximum(largest, 1e-36)))
+
+
+def steps_per_unit(exponent):
+    return 32767.0 * jnp.exp(exponent * (-1.0 / 16.0))
+
+
+def step(exponent):
+    return jnp.exp(exponent * (1.0 / 16.0)) * (1.0 / 32767.0)
+
+
+def narrow(codes):
+    return codes.astype(jnp.int32).astype(jnp.int16)
+
+
+def wide(codes):
+    return codes.astype(jnp.int32).astype(F32)
+
+
+def row_largest(x):
+    return jnp.max(jnp.abs(x), axis=-1, keepdims=True)
+
+
+def encoded(x):
+    largest = jnp.maximum(jnp.maximum(jnp.abs(x[0]), jnp.abs(x[1])), jnp.abs(x[2]))
+    largest = jnp.broadcast_to(jnp.max(largest, axis=-1, keepdims=True), largest.shape)
+    exponent = to_exponent(largest)
+    return jnp.round(x * steps_per_unit(exponent)[None]), exponent
+
+
+def put_pairs(out, spectrum):
+    codes, exponent = encoded(spectrum)
+    codes = narrow(codes).reshape(3, 16, 2, 8, 128)
+    exponent = exponent.reshape(16, 2, 8, 128)
+    for p in range(2):
+        for c in range(3):
+            out[:, 3 * p + c] = codes[c, :, p]
+    half = lane_half((1, 8, 128))
+    out[:, 6] = narrow(jnp.where(half == 0, exponent[:, 0], exponent[:, 1]))
+
+
+def take_pairs(values):
+    half = lane_half((1, 8, 128))
+    steps = step(wide(values[:, 6]))
+    turned = pltpu.roll(steps, 64, 2)
+    steps = (jnp.where(half == 0, steps, turned), jnp.where(half == 0, turned, steps))
+    parts = []
+    for c in range(3):
+        pair = [wide(values[:, 3 * p + c]) * steps[p] for p in range(2)]
+        parts.append(jnp.stack(pair, 1).reshape(256, 128))
+    return jnp.concatenate(parts, 0)
+
+
+def to_column(row):
+    size = row.shape[1]
+    same = (lax.broadcasted_iota(jnp.int32, (size, size), 0)
+            == lax.broadcasted_iota(jnp.int32, (size, size), 1))
+    return jnp.sum(jnp.where(same, row, 0.0), axis=1, keepdims=True)
+
+
+def spread_kernel(owner, brick, stiffness, rest_sq, positions, weights, out, slots, count, cubes, marks, total):
+    total[...] = jnp.zeros(total.shape, F32)
     for d in range(32):
         count[d] = 0
+    place = [positions[c].astype(F32) for c in range(3)]
+    segment = [pltpu.roll(p, 127, 1) - p for p in place]
+    stretch = (segment[0] * segment[0] + segment[1] * segment[1] + segment[2] * segment[2])
+    stretch = stretch / to_column(rest_sq[...].astype(F32))
+    pull = 0.5 * to_column(stiffness[...].astype(F32)) * (stretch - 1.0)
+    force = []
+    for c in range(3):
+        tension = pull * segment[c]
+        force.append(tension - pltpu.roll(tension, 1, 1))
     for n in range(32):
-        place = positions[n].astype(F32)
-        segment = pltpu.roll(place, 127, 1) - place
-        stretch = jnp.sum(segment * segment, axis=0, keepdims=True) / params[1, n]
-        tension = 0.5 * params[0, n] * (stretch - 1.0) * segment
-        force = tension - pltpu.roll(tension, 1, 1)
         w0, w1, w2 = (weights[n, a].astype(F32) for a in range(3))
         cells = (w0[:, None, :] * w1[None, :, :]).reshape(64, 128)
         cells = jnp.concatenate([cells, cells], 0)
-        pushed = (force[:, None, :] * w2[None, :, :]).reshape(24, 128)
+        pushed = jnp.concatenate([force[c][n:n + 1] * w2 for c in range(3)], 0)
         cells_high, cells_low = halves(cells)
         pushed_high, pushed_low = halves(pushed)
         both = ((1,), (1,))
-        cubes[n] = (dot(pushed_high, cells_high, both) + dot(pushed_low, cells_high, both)
-                    + dot(pushed_high, cells_low, both))
+        cube = (dot(pushed_high, cells_high, both) + dot(pushed_low, cells_high, both)
+                + dot(pushed_high, cells_low, both))
+        exponent = to_exponent(jnp.broadcast_to(row_largest(cube), cube.shape))
+        marks[n] = exponent
+        cubes[n] = jnp.round(cube * steps_per_unit(exponent))
     half = lane_half()
     lane = lax.broadcasted_iota(jnp.int32, (8, 128), 1)
 
     @pl.loop(0, 32)
     def _(n):
-        d = owner[n, 0]
+        d = owner[n]
         s = count[d]
         count[d] = s + 1
         slots[n] = s
+        last = jnp.where(lane == 73 + s, brick[n].astype(F32), 0.0)
         for c in range(3):
             tile, side = tile_place(s, c)
-            out[d, tile] += jnp.where(half == side, cubes[n, 8 * c:8 * c + 8, :], 0.0)
-        out[d, 4] += jnp.where(lane == 64 + s, brick[n].astype(F32), 0.0)
+            total[d, tile] += jnp.where(half == side, cubes[n, 8 * c:8 * c + 8, :], 0.0)
+            last = jnp.where(lane == 64 + 3 * s + c, marks[n, 8 * c:8 * c + 8, :], last)
+        total[d, 4] += last
+
+    out[...] = narrow(total[...])
 
 
 def advect_kernel(table, velocity, x_low, x_high, y_low, y_high, spectrum, turned):
@@ -229,64 +301,85 @@
 
     @pl.loop(0, 32, unroll=4)
     def _(src):
-        tiles = [pushes[src, t] for t in range(5)]
+        tiles = [wide(pushes[src, t]) for t in range(5)]
         turned = [pltpu.roll(tile, 64, 1) for tile in tiles]
+        steps = step(tiles[4])
         for slot in range(3):
             brick = ids[src, slot]
             x_half, z_block = brick >> 5, brick & 31
             for c in range(3):
+                at = 3 * slot + c
                 tile, side = tile_place(slot, c)
-                wide = jnp.where(half == side, tiles[tile], turned[tile])
-                forces[c][z_block] += jnp.where(half == x_half, wide, 0.0)
+                codes = jnp.where(half == side, tiles[tile], turned[tile])
+                cube = codes * jnp.broadcast_to(steps[:, 64 + at:65 + at], (8, 128))
+                forces[c][z_block] += jnp.where(half == x_half, cube, 0.0)
 
     field = jnp.concatenate([force[...].reshape(256, 128) for force in forces], 1)
     total = spectrum[...] + table_left(table, DT_STEP * field)
-    out[...] = total.reshape(32, 8, 384)
+    codes, exponent = encoded(stacked(total).reshape(3, 32, 8, 128))
+    for c in range(3):
+        out[:, c] = narrow(codes[c])
+    out[:, 3] = narrow(exponent)
 
 
 def reply_kernel(ids, turned, out):
     half = lane_half()
+    lane = lax.broadcasted_iota(jnp.int32, (8, 128), 1)
 
     @pl.loop(0, 32, unroll=4)
     def _(src):
-        wides = []
+        cubes = []
+        largest = jnp.ones((8, 128), F32)
         for slot in range(3):
             brick = ids[src, slot]
             x_half, z_block = brick >> 5, brick & 31
             for c in range(3):
                 tile = turned[c, z_block]
-                wides.append(jnp.where(half == x_half, tile, pltpu.roll(tile, 64, 1)))
-        wides.append(wides[0])
+                cube = jnp.where(half == x_half, tile, pltpu.roll(tile, 64, 1))
+                largest = jnp.where(lane == 64 + len(cubes), row_largest(cube), largest)
+                cubes.append(cube)
+        exponent = to_exponent(largest)
+        steps = steps_per_unit(exponent)
+        codes = [jnp.round(cube * jnp.broadcast_to(steps[:, 64 + at:65 + at], (8, 128)))
+                 for at, cube in enumerate(cubes)]
+        codes.append(exponent)
         for t in range(5):
-            out[src, t] = jnp.where(half == 0, wides[2 * t], wides[2 * t + 1])
+            out[src, t] = narrow(jnp.where(half == 0, codes[2 * t], codes[2 * t + 1]))
 
 
 def interpolate_kernel(owner, slots, replies, weights, out):
     half = lane_half()
+    lane = lax.broadcasted_iota(jnp.int32, (8, 128), 1)
     for n in range(32):
-        d, s = owner[n, 0], slots[n]
+        d, s = owner[n], slots[n]
+        steps = step(wide(replies[d, 7]))
         parts = []
         for c in range(3):
             tile, side = tile_place(s, c)
-            cube = replies[d, tile]
-            parts.append(jnp.where(half == side, cube, pltpu.roll(cube, 64, 1)))
+            cube = wide(replies[d, 3 + tile])
+            cube = jnp.where(half == side, cube, pltpu.roll(cube, 64, 1))
+            own = jnp.sum(jnp.where(lane == 64 + 3 * s + c, steps, 0.0), axis=1, keepdims=True)
+            parts.append(cube * own)
         cube_high, cube_low = halves(jnp.concatenate(parts, 0)[:, :64])
         w0, w1, w2 = (weights[n, a].astype(F32) for a in range(3))
         cells_high, cells_low = halves((w0[:, None, :] * w1[None, :, :]).reshape(64, 128))
         partial = dot(cube_high, cells_high) + dot(cube_low, cells_high) + dot(cube_high, cells_low)
-        out[n] = jnp.sum(partial.reshape(3, 8, 128) * w2[None], axis=1)
+        for c in range(3):
+            out[c, n:n + 1] = jnp.sum(partial[8 * c:8 * c + 8] * w2, axis=0, keepdims=True)
 
 
 def y_kernel(left, lanes, twiddle, values, out):
-    spectrum = table_left(left, values[...].reshape(256, 384))
+    steps = step(wide(values[:, 3]))
+    spectrum = [(wide(values[:, c]) * steps).reshape(256, 128) for c in range(3)]
+    spectrum = table_left(left, jnp.concatenate(spectrum, 1))
     spectrum = stacked(spectrum).reshape(96, 8, 128)
     spectrum = twiddled(spectrum, twiddle[0], twiddle[1])
     spectrum = lane_pass(spectrum.reshape(768, 128), lanes)
-    out[...] = unstacked(spectrum.reshape(768, 128)).reshape(16, 16, 384)
+    put_pairs(out, spectrum.reshape(3, 32, 8, 128))
 
 
 def x_kernel(flags, left, left_extra, back, lanes, lanes_back, twiddle, flips, waves, damping, values, out):
-    packed = stacked(values[...].reshape(256, 384))
+    packed = take_pairs(values)
     high, low = halves(packed)
     flipped = dot(high, flips[...]) + dot(low, flips[...])
     by_pair = (3, 16, 2, 8, 128)
@@ -312,19 +405,26 @@
     projected = lane_pass(projected, lanes_back)
     projected = twiddled(projected, twiddle[0], -twiddle[1])
     projected = unstacked(projected.reshape(960, 128))
-    out[...] = table_left(back, projected).reshape(16, 16, 384)
-
-
-def y_back_kernel(back, lanes, twiddle, values, out):
-    spectrum = lane_pass(stacked(values[...].reshape(256, 384)), lanes)
+    put_pairs(out, stacked(table_left(back, projected)).reshape(3, 32, 8, 128))
+
+
+def y_back_kernel(back, lanes, twiddle, values, replies, out):
+    spectrum = lane_pass(take_pairs(values), lanes)
     spectrum = twiddled(spectrum, twiddle[0], -twiddle[1])
     spectrum = table_left(back, unstacked(spectrum.reshape(768, 128)))
-    out[...] = spectrum.reshape(32, 8, 384)
+    codes, exponent = encoded(stacked(spectrum).reshape(3, 32, 8, 128))
+    for c in range(3):
+        out[:, c] = narrow(codes[c])
+    for t in range(4):
+        out[:, 3 + t] = replies[:, t]
+    lane = lax.broadcasted_iota(jnp.int32, (1, 8, 128), 2)
+    out[:, 7] = narrow(jnp.where(lane == 76, exponent, wide(replies[:, 4])))
 
 
 def z_back_kernel(back, values, out):
-    spectrum = values[...].reshape(256, 384)
-    field = table_right(jnp.transpose(spectrum), back)
+    steps = step(wide(values[:, 7])[:, :, 76:77])
+    spectrum = [(wide(values[:, c]) * steps).reshape(256, 128) for c in range(3)]
+    field = table_right(jnp.transpose(jnp.concatenate(spectrum, 1)), back)
     out[...] = field.reshape(3, 16, 8, 256)
 
 
@@ -345,6 +445,10 @@
         scratch_shapes=list(scratch),
         compiler_params=pltpu.CompilerParams(vmem_limit_bytes=48 << 20),
     )
+
+
+def codes_of(count, tiles):
+    return jax.ShapeDtypeStruct((count, tiles, 8, 128), jnp.int16)
 
 
 def signed(indices):
@@ -391,35 +495,36 @@
     flags = jnp.stack([row == 0, col == 0]).astype(jnp.int32)
     units, damping = wave_tables(marks, row, col)
 
-    params = jnp.stack([stiffness, rest_sq]).astype(F32)
+    owner = owner_column.reshape(32)
+    spread_outs = (jax.ShapeDtypeStruct((32, 5, 8, 128), jnp.int16), jax.ShapeDtypeStruct((32,), jnp.int32))
     pushes, slots = call(
-        spread_kernel, [SMEM, SMEM, SMEM, VMEM, VMEM],
-        ([32, 5, 8, 128], jax.ShapeDtypeStruct((32,), jnp.int32)),
-        [pltpu.SMEM((32,), jnp.int32), pltpu.VMEM((32, 24, 128), F32)], [VMEM, SMEM],
-    )(params, owner_column, brick_index, positions, weights)
+        spread_kernel, [SMEM, SMEM, VMEM, VMEM, VMEM, VMEM], spread_outs,
+        [pltpu.SMEM((32,), jnp.int32), pltpu.VMEM((32, 24, 128), F32), pltpu.VMEM((32, 24, 128), F32),
+         pltpu.VMEM((32, 5, 8, 128), F32)], [VMEM, SMEM],
+    )(owner, brick_index, stiffness.reshape(1, 32), rest_sq.reshape(1, 32), positions.transpose(1, 0, 2), weights)
     x_low, x_high = neighbours(velocity[:, :1], velocity[:, 15:], "row")
     y_low, y_high = neighbours(velocity[:, :, :1], velocity[:, :, 7:], "col")
     pushes = moved(pushes, "col")
-    ids = pushes[:, 4, 0, 64:67].astype(jnp.int32)
+    ids = pushes[:, 4, 0, 73:76].astype(jnp.int32)
 
     spectrum, turned = call(advect_kernel, [VMEM] * 6, ([256, 384], [3, 32, 8, 128]))(
         z_fore, velocity, x_low, x_high, y_low, y_high)
-    spectrum = call(gather_kernel, [SMEM, VMEM, VMEM, VMEM], [32, 8, 384],
+    spectrum = call(gather_kernel, [SMEM, VMEM, VMEM, VMEM], codes_of(32, 4),
                     [pltpu.VMEM((32, 8, 128), F32)] * 3)(ids, z_fore, pushes, spectrum)
     spectrum = moved(spectrum, "col")
-    spectrum = call(y_kernel, [VMEM] * 4, [16, 16, 384])(y_fore, y_lanes, y_twiddle, spectrum)
+    spectrum = call(y_kernel, [VMEM] * 4, codes_of(16, 7))(y_fore, y_lanes, y_twiddle, spectrum)
     spectrum = moved(spectrum, "row")
-    spectrum = call(x_kernel, [SMEM] + [VMEM] * 10, [16, 16, 384])(
+    spectrum = call(x_kernel, [SMEM] + [VMEM] * 10, codes_of(16, 7))(
         flags, x_fore, x_extra, x_back, x_lanes, x_lanes_back, x_twiddle, flips, units, damping, spectrum)
     spectrum = moved(spectrum, "row")
-    spectrum = call(y_back_kernel, [VMEM] * 4, [32, 8, 384])(y_back, y_lanes_back, y_twiddle, spectrum)
+    replies = call(reply_kernel, [SMEM, VMEM], codes_of(32, 5))(ids, turned)
+    spectrum = call(y_back_kernel, [VMEM] * 5, codes_of(32, 8))(
+        y_back, y_lanes_back, y_twiddle, spectrum, replies)
     spectrum = moved(spectrum, "col")
     new_velocity = call(z_back_kernel, [VMEM] * 2, [3, 16, 8, 256])(z_back, spectrum)
-
-    replies = moved(call(reply_kernel, [SMEM, VMEM], [32, 5, 8, 128])(ids, turned), "col")
-    marker_velocity = call(interpolate_kernel, [SMEM, SMEM, VMEM, VMEM], [32, 3, 128])(
-        owner_column, slots, replies, weights)
-    return new_velocity, marker_velocity
+    marker_velocity = call(interpolate_kernel, [SMEM, SMEM, VMEM, VMEM], [3, 32, 128])(
+        owner, slots, spectrum, weights)
+    return new_velocity, marker_velocity.transpose(1, 0, 2)
 
 
 def solution(mesh):

time: 164 us -> 137 us (0.84)
  waiting for transfers between devices: 62.7 us -> 24.2 us
  blocking collectives: 0 us -> 19.8 us
  starting transfers between devices: 71 us -> 54.1 us
  Pallas kernels: 20.7 us -> 31.6 us
  local copies, waits for them, and re-layouts: 6.5 us -> 4.51 us
    all_to_all x6 -> x4, waiting for transfers between devices: 58.8 us -> 20.7 us  [moved(): return lax.all_to_all(x, axis, split_axis=0, concat_axis=0, tiled=True)]
    all_to_all x0 -> x1, blocking collectives: none -> 19.8 us  [moved(): return lax.all_to_all(x, axis, split_axis=0, concat_axis=0, tiled=True)]
    all_to_all x6 -> x4, starting transfers between devices: 54.2 us -> 34.7 us  [moved(): return lax.all_to_all(x, axis, split_axis=0, concat_axis=0, tiled=True)]
    pallas_call x7, Pallas kernels: 19 us -> 29.7 us  [the longest x1 12.8 us: local(): replies = call(reply_kernel, [SMEM, VMEM], codes_of(32, 5))(ids, turned)]
    unnamed x49 -> x50, local copies, waits for them, and re-layouts: 6.43 us -> 3.68 us
    ppermute x2, starting transfers between devices: 11.5 us -> 14.1 us  [neighbours(): lax.ppermute(plane_low, axis, down)]
  transfers between devices with their start and end apart: 10 -> 8, of which waited for: 6 -> 5; matrix products, arithmetic and copies ran while one was open for 1% -> 1% of each run, Pallas kernels for 4% -> 13%
where the time goes in v1:
time: 137 us; the launch traced here: 136 us
  starting transfers between devices  54.1 us (39%)
  Pallas kernels  31.6 us (23%)
  waiting for transfers between devices  24.2 us (18%)
  blocking collectives  19.8 us (14%)
  local copies, waits for them, and re-layouts  4.51 us (3%)
    all_to_all x4, starting transfers between devices, moved(): return lax.all_to_all(x, axis, split_axis=0, concat_axis=0, tiled=True)  34.7 us
    all_to_all x4, waiting for transfers between devices, moved(): return lax.all_to_all(x, axis, split_axis=0, concat_axis=0, tiled=True)  20.7 us
    all_to_all x1, blocking collectives, moved(): return lax.all_to_all(x, axis, split_axis=0, concat_axis=0, tiled=True)  19.8 us
    ppermute x2, starting transfers between devices, neighbours(): lax.ppermute(plane_low, axis, down)  14.1 us
    pallas_call x1, Pallas kernels, local(): replies = call(reply_kernel, [SMEM, VMEM], codes_of(32, 5))(ids, turned)  12.8 us
    ppermute x2, starting transfers between devices, neighbours(): lax.ppermute(plane_high, axis, up)  5.34 us
    pallas_call x1, Pallas kernels, local(): call(x_kernel, [SMEM] + [VMEM] * 10, codes_of(16, 7))  4.51 us
    pallas_call x1, Pallas kernels, local(): call(spread_kernel, [SMEM, SMEM, VMEM, VMEM, VMEM, VMEM], spread_outs, [p...  4.03 us
  transfers between devices with their start and end apart: 8, of which 5 were waited for; matrix products, arithmetic and copies ran while one was open for 1% of the time, Pallas kernels for 13%

profile of v1, /device:TPU:1, one launch (start us, length us, event | category | flops | bytes accessed | tf_op | source)
XLA Modules:
  0.0 136.0 jit_solution(9298710206050062000)
XLA Ops:
  0.6 0.8 fusion.26
  1.4 11.9 %collective-permute-start.1 = (f32[3,1,8,256]{3,2,1,0:T(8,128)S(1)}, f32[3,1,8,256]{3,2,1,0:T(8,128)S(1)}, u32[]{:S(2)}, u32[]{:S(2)}) collective-permute-start(f32[3,1,8,256]{3,2,1,0:T(8,128)S(1)} %get-tuple-element.12), channel_id=1, source_target_pairs={{32,0},{64,32},{96,64},{128,96},{160,128},{192,160},{224,192},{256... | collective-permute-start | bytes 73736 | tf_op jit(solution)/shard_map/ppermute | solution.py:487
  13.4 1.9 %collective-permute-start = (f32[3,1,8,256]{3,2,1,0:T(8,128)S(1)}, f32[3,1,8,256]{3,2,1,0:T(8,128)S(1)}, u32[]{:S(2)}, u32[]{:S(2)}) collective-permute-start(f32[3,1,8,256]{3,2,1,0:T(8,128)S(1)} %get-tuple-element.13), channel_id=1, source_target_pairs={{0,32},{32,64},{64,96},{96,128},{128,160},{160,192},{192,224},{224... | collective-permute-start | bytes 73736 | tf_op jit(solution)/shard_map/ppermute | solution.py:487
  16.0 0.9 copy-done.1
  16.9 4.0 %shard_map.239 = (s16[32,5,8,128]{3,2,1,0:T(8,128)(2,1)}, s32[32]{0:T(128)S(1)}) custom-call(s32[32]{0:T(128)S(1)} %bitcast.11, s32[32]{0:T(128)S(1)} %copy-done.19, bf16[1,32]{1,0:T(2,128)(2,1)S(1)} %bitcast.13, bf16[1,32]{1,0:T(2,128)(2,1)S(1)} %bitcast.14, bf16[3,32,128]{2,1,0:T(8,128)(2,1)S(1)} %bitcast.10, bf16[32,3,8,128]{3,2,1,0:T(8,128)(2,1)S(1)} %copy-done.1), custom_call_target="tpu_custom_call" | custom-call | tf_op jit(solution)/shard_map/pallas_call | solution.py:500
  21.0 8.2 %all-to-all-start = ((s16[32,5,8,128]{3,2,1,0:T(8,128)(2,1)}), s16[32,5,8,128]{3,2,1,0:T(8,128)(2,1)S(1)}, u32[]{:S(2)}, u32[]{:S(2)}) async-start(s16[32,5,8,128]{3,2,1,0:T(8,128)(2,1)} %get-tuple-element.6), calls=%async_computation | async-start | bytes 655360 | tf_op jit(solution)/shard_map/all_to_all | solution.py:480
  29.2 2.1 %collective-permute-start.3 = (f32[3,16,1,256]{3,2,1,0:T(1,128)S(1)}, f32[3,16,1,256]{3,2,1,0:T(1,128)S(1)}, u32[]{:S(2)}, u32[]{:S(2)}) collective-permute-start(f32[3,16,1,256]{3,2,1,0:T(1,128)S(1)} %get-tuple-element.10), channel_id=1, source_target_pairs={{1,0},{2,1},{3,2},{4,3},{5,4},{6,5},{7,6},{8,7},{9,8},{10,9},{11,1... | collective-permute-start | bytes 147464 | tf_op jit(solution)/shard_map/ppermute | solution.py:487
  31.4 3.4 %collective-permute-start.2 = (f32[3,16,1,256]{3,2,1,0:T(1,128)S(1)}, f32[3,16,1,256]{3,2,1,0:T(1,128)S(1)}, u32[]{:S(2)}, u32[]{:S(2)}) collective-permute-start(f32[3,16,1,256]{3,2,1,0:T(1,128)S(1)} %get-tuple-element.11), channel_id=1, source_target_pairs={{0,1},{1,2},{2,3},{3,4},{4,5},{5,6},{6,7},{7,8},{8,9},{9,10},{10,1... | collective-permute-start | bytes 147464 | tf_op jit(solution)/shard_map/ppermute | solution.py:487
  35.9 3.0 %collective-permute-done.2.y_low = f32[3,16,1,256]{3,2,1,0:T(1,128)S(1)} collective-permute-done((f32[3,16,1,256]{3,2,1,0:T(1,128)S(1)}, f32[3,16,1,256]{3,2,1,0:T(1,128)S(1)}, u32[]{:S(2)}, u32[]{:S(2)}) %collective-permute-start.2) | collective-permute-done | bytes 49184 | tf_op jit(solution)/shard_map/ppermute | solution.py:487
  39.7 3.5 %shard_map.241 = s16[32,4,8,128]{3,2,1,0:T(8,128)(2,1)} custom-call(s32[32,3]{1,0:T(8,128)S(1)} %bitcast.8, bf16[2,256,256]{2,1,0:T(8,128)(2,1)S(1)} %copy-done, s16[32,5,8,128]{3,2,1,0:T(8,128)(2,1)S(1)} %all-to-all-done.pushes, f32[256,384]{1,0:T(8,128)S(1)} %get-tuple-element.7.spectrum), custom_call_target="tpu_custom_call" | custom-call | tf_op jit(solution)/shard_map/pallas_call | solution.py:512
  43.2 9.8 %all-to-all-start.1 = ((s16[32,4,8,128]{3,2,1,0:T(8,128)(2,1)}), s16[32,4,8,128]{3,2,1,0:T(8,128)(2,1)S(1)}, u32[]{:S(2)}, u32[]{:S(2)}) async-start(s16[32,4,8,128]{3,2,1,0:T(8,128)(2,1)} %shard_map.241), calls=%async_computation.1 | async-start | bytes 524288 | tf_op jit(solution)/shard_map/all_to_all | solution.py:480
  53.0 0.7 copy-done.23
  53.7 8.3 %all-to-all-done.1.values = s16[32,4,8,128]{3,2,1,0:T(8,128)(2,1)S(1)} async-done(((s16[32,4,8,128]{3,2,1,0:T(8,128)(2,1)}), s16[32,4,8,128]{3,2,1,0:T(8,128)(2,1)S(1)}, u32[]{:S(2)}, u32[]{:S(2)}) %all-to-all-start.1) | async-done | bytes 262176 | tf_op jit(solution)/shard_map/all_to_all | solution.py:480
  62.0 1.7 %shard_map.242 = s16[16,7,8,128]{3,2,1,0:T(8,128)(2,1)} custom-call(bf16[2,256,256]{2,1,0:T(8,128)(2,1)S(1)} %copy-done.6, bf16[2,128,256]{2,1,0:T(8,128)(2,1)S(1)} %copy-done.11, f32[2,32,1,128]{3,2,1,0:T(1,128)S(1)} %copy-done.12, s16[32,4,8,128]{3,2,1,0:T(8,128)(2,1)S(1)} %all-to-all-done.1.values), custom_call_target="tpu_custom_call" | custom-call | tf_op jit(solution)/shard_map/pallas_call | solution.py:515
  63.7 7.4 %all-to-all-start.2 = ((s16[16,7,8,128]{3,2,1,0:T(8,128)(2,1)}), s16[16,7,8,128]{3,2,1,0:T(8,128)(2,1)S(1)}, u32[]{:S(2)}, u32[]{:S(2)}) async-start(s16[16,7,8,128]{3,2,1,0:T(8,128)(2,1)} %shard_map.242), calls=%async_computation.2 | async-start | bytes 458752 | tf_op jit(solution)/shard_map/all_to_all | solution.py:480
  71.2 0.7 copy-done.22
  72.6 12.0 %all-to-all-done.2.values = s16[16,7,8,128]{3,2,1,0:T(8,128)(2,1)S(1)} async-done(((s16[16,7,8,128]{3,2,1,0:T(8,128)(2,1)}), s16[16,7,8,128]{3,2,1,0:T(8,128)(2,1)S(1)}, u32[]{:S(2)}, u32[]{:S(2)}) %all-to-all-start.2) | async-done | bytes 229408 | tf_op jit(solution)/shard_map/all_to_all | solution.py:480
  84.7 4.5 %shard_map.243 = s16[16,7,8,128]{3,2,1,0:T(8,128)(2,1)} custom-call(s32[2]{0:T(128)S(1)} %add_convert_fusion.flags, bf16[2,256,256]{2,1,0:T(8,128)(2,1)S(1)} %copy-done.9, bf16[2,64,256]{2,1,0:T(8,128)(2,1)S(1)} %copy-done.16, bf16[2,256,320]{2,1,0:T(8,128)(2,1)S(1)} %copy-done.4, bf16[2,128,256]{2,1,0:T(8,128)(2,1)S(1)} %copy-done.14, ...), custom_call_target="tpu_custom_call" | custom-call | tf_op jit(solution)/shard_map/pallas_call | solution.py:517
  89.2 9.3 %all-to-all-start.3 = ((s16[16,7,8,128]{3,2,1,0:T(8,128)(2,1)}), s16[16,7,8,128]{3,2,1,0:T(8,128)(2,1)S(1)}, u32[]{:S(2)}, u32[]{:S(2)}) async-start(s16[16,7,8,128]{3,2,1,0:T(8,128)(2,1)} %shard_map.243), calls=%async_computation.3 | async-start | bytes 458752 | tf_op jit(solution)/shard_map/all_to_all | solution.py:480
  98.6 12.8 %shard_map.244.replies = s16[32,5,8,128]{3,2,1,0:T(8,128)(2,1)S(1)} custom-call(s32[32,3]{1,0:T(8,128)S(1)} %bitcast.9, f32[3,32,8,128]{3,2,1,0:T(8,128)S(1)} %get-tuple-element.8.turned), custom_call_target="tpu_custom_call" | custom-call | tf_op jit(solution)/shard_map/pallas_call | solution.py:520
  111.7 1.4 shard_map.245
  113.1 19.8 %all_to_all.25.values.replies = s16[32,8,8,128]{3,2,1,0:T(8,128)(2,1)S(1)} all-to-all(s16[32,8,8,128]{3,2,1,0:T(8,128)(2,1)S(1)} %shard_map.245), channel_id=1, replica_groups=mesh['row'=16,'col'=32] {'col'}, dimensions={0} | all-to-all | bytes 1048576 | tf_op jit(solution)/shard_map/all_to_all | solution.py:480
  132.9 1.9 %shard_map.247 = f32[3,32,128]{2,1,0:T(8,128)} custom-call(s32[32]{0:T(128)S(1)} %bitcast.12, s32[32]{0:T(128)S(1)} %get-tuple-element.9.slots, s16[32,8,8,128]{3,2,1,0:T(8,128)(2,1)S(1)} %all_to_all.25.values.replies, bf16[32,3,8,128]{3,2,1,0:T(8,128)(2,1)S(1)} %copy-done.2), custom_call_target="tpu_custom_call" | custom-call | tf_op jit(solution)/shard_map/pallas_call | solution.py:525
  134.8 1.2 shard_map.246
  (63 shorter events, 3.7 us)
Async XLA Ops:
  0.6 14.7 %copy-start.17 = (bf16[32,3,128]{2,0,1:T(8,128)(2,1)S(1)}, bf16[32,3,128]{2,0,1:T(8,128)(2,1)}, u32[]{:S(2)}) copy-start(bf16[32,3,128]{2,0,1:T(8,128)(2,1)} %param.25) | copy-start | bytes 73732
  1.4 34.1 %collective-permute-start.1 = (f32[3,1,8,256]{3,2,1,0:T(8,128)S(1)}, f32[3,1,8,256]{3,2,1,0:T(8,128)S(1)}, u32[]{:S(2)}, u32[]{:S(2)}) collective-permute-start(f32[3,1,8,256]{3,2,1,0:T(8,128)S(1)} %get-tuple-element.12), channel_id=1, source_target_pairs={{32,0},{64,32},{96,64},{128,96},{160,128},{192,160},{224,192},{256... | collective-permute-start | bytes 73736 | tf_op jit(solution)/shard_map/ppermute | solution.py:487
  13.4 22.1 %collective-permute-start = (f32[3,1,8,256]{3,2,1,0:T(8,128)S(1)}, f32[3,1,8,256]{3,2,1,0:T(8,128)S(1)}, u32[]{:S(2)}, u32[]{:S(2)}) collective-permute-start(f32[3,1,8,256]{3,2,1,0:T(8,128)S(1)} %get-tuple-element.13), channel_id=1, source_target_pairs={{0,32},{32,64},{64,96},{96,128},{128,160},{160,192},{192,224},{224... | collective-permute-start | bytes 73736 | tf_op jit(solution)/shard_map/ppermute | solution.py:487
  16.9 12.3 %copy-start.3 = (f32[3,16,8,256]{3,2,1,0:T(8,128)S(1)}, f32[3,16,8,256]{3,2,1,0:T(8,128)}, u32[]{:S(2)}) copy-start(f32[3,16,8,256]{3,2,1,0:T(8,128)} %velocity.1) | copy-start | bytes 1179652
  21.0 18.0 %copy-start = (bf16[2,256,256]{2,1,0:T(8,128)(2,1)S(1)}, bf16[2,256,256]{2,1,0:T(8,128)(2,1)}, u32[]{:S(2)}) copy-start(bf16[2,256,256]{2,1,0:T(8,128)(2,1)} %constant.110.clone.table) | copy-start | bytes 786436
  21.0 18.6 %all-to-all-start = ((s16[32,5,8,128]{3,2,1,0:T(8,128)(2,1)}), s16[32,5,8,128]{3,2,1,0:T(8,128)(2,1)S(1)}, u32[]{:S(2)}, u32[]{:S(2)}) async-start(s16[32,5,8,128]{3,2,1,0:T(8,128)(2,1)} %get-tuple-element.6), calls=%async_computation | async-start | bytes 655360 | tf_op jit(solution)/shard_map/all_to_all | solution.py:480
  29.2 6.7 %collective-permute-start.3 = (f32[3,16,1,256]{3,2,1,0:T(1,128)S(1)}, f32[3,16,1,256]{3,2,1,0:T(1,128)S(1)}, u32[]{:S(2)}, u32[]{:S(2)}) collective-permute-start(f32[3,16,1,256]{3,2,1,0:T(1,128)S(1)} %get-tuple-element.10), channel_id=1, source_target_pairs={{1,0},{2,1},{3,2},{4,3},{5,4},{6,5},{7,6},{8,7},{9,8},{10,9},{11,1... | collective-permute-start | bytes 147464 | tf_op jit(solution)/shard_map/ppermute | solution.py:487
  31.4 7.6 %collective-permute-start.2 = (f32[3,16,1,256]{3,2,1,0:T(1,128)S(1)}, f32[3,16,1,256]{3,2,1,0:T(1,128)S(1)}, u32[]{:S(2)}, u32[]{:S(2)}) collective-permute-start(f32[3,16,1,256]{3,2,1,0:T(1,128)S(1)} %get-tuple-element.11), channel_id=1, source_target_pairs={{0,1},{1,2},{2,3},{3,4},{4,5},{5,6},{6,7},{7,8},{8,9},{9,10},{10,1... | collective-permute-start | bytes 147464 | tf_op jit(solution)/shard_map/ppermute | solution.py:487
  43.2 18.8 %copy-start.6 = (bf16[2,256,256]{2,1,0:T(8,128)(2,1)S(1)}, bf16[2,256,256]{2,1,0:T(8,128)(2,1)}, u32[]{:S(2)}) copy-start(bf16[2,256,256]{2,1,0:T(8,128)(2,1)} %constant.111.clone.left) | copy-start | bytes 786436
  43.2 18.8 %copy-start.11 = (bf16[2,128,256]{2,1,0:T(8,128)(2,1)S(1)}, bf16[2,128,256]{2,1,0:T(8,128)(2,1)}, u32[]{:S(2)}) copy-start(bf16[2,128,256]{2,1,0:T(8,128)(2,1)} %constant.112.clone.lanes) | copy-start | bytes 393220
  43.2 18.8 %copy-start.12 = (f32[2,32,1,128]{3,2,1,0:T(1,128)S(1)}, f32[2,32,1,128]{3,2,1,0:T(1,128)}, u32[]{:S(2)}) copy-start(f32[2,32,1,128]{3,2,1,0:T(1,128)} %constant.113.clone.twiddle) | copy-start | bytes 98308
  43.2 18.8 %all-to-all-start.1 = ((s16[32,4,8,128]{3,2,1,0:T(8,128)(2,1)}), s16[32,4,8,128]{3,2,1,0:T(8,128)(2,1)S(1)}, u32[]{:S(2)}, u32[]{:S(2)}) async-start(s16[32,4,8,128]{3,2,1,0:T(8,128)(2,1)} %shard_map.241), calls=%async_computation.1 | async-start | bytes 524288 | tf_op jit(solution)/shard_map/all_to_all | solution.py:480
  63.7 21.0 %all-to-all-start.2 = ((s16[16,7,8,128]{3,2,1,0:T(8,128)(2,1)}), s16[16,7,8,128]{3,2,1,0:T(8,128)(2,1)S(1)}, u32[]{:S(2)}, u32[]{:S(2)}) async-start(s16[16,7,8,128]{3,2,1,0:T(8,128)(2,1)} %shard_map.242), calls=%async_computation.2 | async-start | bytes 458752 | tf_op jit(solution)/shard_map/all_to_all | solution.py:480
  71.9 12.8 %copy-start.14 = (bf16[2,128,256]{2,1,0:T(8,128)(2,1)S(1)}, bf16[2,128,256]{2,1,0:T(8,128)(2,1)}, u32[]{:S(2)}) copy-start(bf16[2,128,256]{2,1,0:T(8,128)(2,1)} %constant.117.clone.lanes) | copy-start | bytes 393220
  71.9 12.8 %copy-start.15 = (bf16[128,256]{1,0:T(8,128)(2,1)S(1)}, bf16[128,256]{1,0:T(8,128)(2,1)}, u32[]{:S(2)}) copy-start(bf16[128,256]{1,0:T(8,128)(2,1)} %constant.120.clone.flips) | copy-start | bytes 196612
  71.9 12.8 %copy-start.16 = (bf16[2,64,256]{2,1,0:T(8,128)(2,1)S(1)}, bf16[2,64,256]{2,1,0:T(8,128)(2,1)}, u32[]{:S(2)}) copy-start(bf16[2,64,256]{2,1,0:T(8,128)(2,1)} %constant.115.clone.left_extra) | copy-start | bytes 196612
  72.2 12.4 %copy-start.4 = (bf16[2,256,320]{2,1,0:T(8,128)(2,1)S(1)}, bf16[2,256,320]{2,1,0:T(8,128)(2,1)}, u32[]{:S(2)}) copy-start(bf16[2,256,320]{2,1,0:T(8,128)(2,1)} %constant.116.clone.back) | copy-start | bytes 983044
  72.3 12.4 %copy-start.5 = (f32[2,40,8,128]{3,2,1,0:T(8,128)S(1)}, f32[2,40,8,128]{3,2,1,0:T(8,128)}, u32[]{:S(2)}) copy-start(f32[2,40,8,128]{3,2,1,0:T(8,128)} %constant.119.clone.twiddle) | copy-start | bytes 983044
  72.3 12.4 %copy-start.9 = (bf16[2,256,256]{2,1,0:T(8,128)(2,1)S(1)}, bf16[2,256,256]{2,1,0:T(8,128)(2,1)}, u32[]{:S(2)}) copy-start(bf16[2,256,256]{2,1,0:T(8,128)(2,1)} %constant.114.clone.left) | copy-start | bytes 786436
  72.3 12.4 %copy-start.13 = (bf16[2,128,256]{2,1,0:T(8,128)(2,1)S(1)}, bf16[2,128,256]{2,1,0:T(8,128)(2,1)}, u32[]{:S(2)}) copy-start(bf16[2,128,256]{2,1,0:T(8,128)(2,1)} %constant.118.clone.lanes_back) | copy-start | bytes 393220
  89.2 22.5 %all-to-all-start.3 = ((s16[16,7,8,128]{3,2,1,0:T(8,128)(2,1)}), s16[16,7,8,128]{3,2,1,0:T(8,128)(2,1)S(1)}, u32[]{:S(2)}, u32[]{:S(2)}) async-start(s16[16,7,8,128]{3,2,1,0:T(8,128)(2,1)} %shard_map.243), calls=%async_computation.3 | async-start | bytes 458752 | tf_op jit(solution)/shard_map/all_to_all | solution.py:480
  98.6 13.2 %copy-start.8 = (bf16[2,256,256]{2,1,0:T(8,128)(2,1)S(1)}, bf16[2,256,256]{2,1,0:T(8,128)(2,1)}, u32[]{:S(2)}) copy-start(bf16[2,256,256]{2,1,0:T(8,128)(2,1)} %constant.121.clone.back) | copy-start | bytes 786436
  98.6 13.2 %copy-start.10 = (bf16[2,128,256]{2,1,0:T(8,128)(2,1)S(1)}, bf16[2,128,256]{2,1,0:T(8,128)(2,1)}, u32[]{:S(2)}) copy-start(bf16[2,128,256]{2,1,0:T(8,128)(2,1)} %constant.122.clone.lanes) | copy-start | bytes 393220
  113.1 19.8 %copy-start.2 = (bf16[32,3,8,128]{3,2,1,0:T(8,128)(2,1)S(1)}, bf16[32,3,8,128]{3,2,1,0:T(8,128)(2,1)}, u32[]{:S(2)}) copy-start(bf16[32,3,8,128]{3,2,1,0:T(8,128)(2,1)} %weights.3) | copy-start | bytes 589828
  (9 other events, 7.5 us)

commit v2 on v1

--- a/solution.py
+++ b/solution.py
@@ -135,7 +135,9 @@
 
 
 def lane_pass(x, table):
-    both = table_right(x, table)
+    high, low = halves(x)
+    twice = jnp.concatenate([table[0], table[0]], 0)
+    both = dot(jnp.concatenate([high, low], 1), twice) + dot(high, table[1])
     rows = x.shape[0]
     cosine = both[:, :128].reshape(rows // 8, 8, 128)
     sine = both[:, 128:].reshape(rows // 8, 8, 128)
@@ -229,10 +231,18 @@
     return jnp.sum(jnp.where(same, row, 0.0), axis=1, keepdims=True)
 
 
-def spread_kernel(owner, brick, stiffness, rest_sq, positions, weights, out, slots, count, cubes, marks, total):
+def spread_kernel(owner_in, brick_in, stiffness_in, rest_in, positions_in, weights_in, out, slots,
+                  owner, brick, stiffness, rest_sq, positions, weights, count, cubes, marks, total, arrived):
+    pairs = ((weights_in, weights), (positions_in, positions), (rest_in, rest_sq),
+             (stiffness_in, stiffness), (owner_in, owner), (brick_in, brick))
+    copies = [pltpu.make_async_copy(a, b, arrived.at[i]) for i, (a, b) in enumerate(pairs)]
+    for copy in copies:
+        copy.start()
     total[...] = jnp.zeros(total.shape, F32)
     for d in range(32):
         count[d] = 0
+    for copy in copies:
+        copy.wait()
     place = [positions[c].astype(F32) for c in range(3)]
     segment = [pltpu.roll(p, 127, 1) - p for p in place]
     stretch = (segment[0] * segment[0] + segment[1] * segment[1] + segment[2] * segment[2])
@@ -328,26 +338,28 @@
 
     @pl.loop(0, 32, unroll=4)
     def _(src):
-        cubes = []
-        largest = jnp.ones((8, 128), F32)
+        cubes, largest = [], []
         for slot in range(3):
             brick = ids[src, slot]
             x_half, z_block = brick >> 5, brick & 31
             for c in range(3):
                 tile = turned[c, z_block]
                 cube = jnp.where(half == x_half, tile, pltpu.roll(tile, 64, 1))
-                largest = jnp.where(lane == 64 + len(cubes), row_largest(cube), largest)
+                largest.append(jnp.max(jnp.abs(cube), axis=0, keepdims=True))
                 cubes.append(cube)
-        exponent = to_exponent(largest)
+        largest = jnp.concatenate(largest + largest[:7], 0)
+        exponent = to_exponent(jnp.broadcast_to(row_largest(largest), (16, 128)))
         steps = steps_per_unit(exponent)
-        codes = [jnp.round(cube * jnp.broadcast_to(steps[:, 64 + at:65 + at], (8, 128)))
-                 for at, cube in enumerate(cubes)]
-        codes.append(exponent)
+        codes = [jnp.round(cube * steps[at:at + 1]) for at, cube in enumerate(cubes)]
+        last = jnp.zeros((8, 128), F32)
+        for at in range(9):
+            last = jnp.where(lane == 64 + at, exponent[at:at + 1], last)
+        codes.append(last)
         for t in range(5):
             out[src, t] = narrow(jnp.where(half == 0, codes[2 * t], codes[2 * t + 1]))
 
 
-def interpolate_kernel(owner, slots, replies, weights, out):
+def interpolate(owner, slots, replies, weights, out):
     half = lane_half()
     lane = lax.broadcasted_iota(jnp.int32, (8, 128), 1)
     for n in range(32):
@@ -381,7 +393,7 @@
 def x_kernel(flags, left, left_extra, back, lanes, lanes_back, twiddle, flips, waves, damping, values, out):
     packed = take_pairs(values)
     high, low = halves(packed)
-    flipped = dot(high, flips[...]) + dot(low, flips[...])
+    flipped = dot(jnp.concatenate([high, low], 1), jnp.concatenate([flips[...], flips[...]], 0))
     by_pair = (3, 16, 2, 8, 128)
     reverse = flipped[:, :128].reshape(by_pair)
     negate = flipped[:, 128:].reshape(by_pair)
@@ -421,7 +433,8 @@
     out[:, 7] = narrow(jnp.where(lane == 76, exponent, wide(replies[:, 4])))
 
 
-def z_back_kernel(back, values, out):
+def last_kernel(owner, slots, back, values, weights, out, markers):
+    interpolate(owner, slots, values, weights, markers)
     steps = step(wide(values[:, 7])[:, :, 76:77])
     spectrum = [(wide(values[:, c]) * steps).reshape(256, 128) for c in range(3)]
     field = table_right(jnp.transpose(jnp.concatenate(spectrum, 1)), back)
@@ -430,6 +443,7 @@
 
 VMEM = pl.BlockSpec(memory_space=pltpu.VMEM)
 SMEM = pl.BlockSpec(memory_space=pltpu.SMEM)
+HBM = pl.BlockSpec(memory_space=pltpu.HBM)
 
 
 def call(kernel, specs, shapes, scratch=(), out_specs=None):
@@ -498,12 +512,16 @@
     owner = owner_column.reshape(32)
     spread_outs = (jax.ShapeDtypeStruct((32, 5, 8, 128), jnp.int16), jax.ShapeDtypeStruct((32,), jnp.int32))
     pushes, slots = call(
-        spread_kernel, [SMEM, SMEM, VMEM, VMEM, VMEM, VMEM], spread_outs,
-        [pltpu.SMEM((32,), jnp.int32), pltpu.VMEM((32, 24, 128), F32), pltpu.VMEM((32, 24, 128), F32),
-         pltpu.VMEM((32, 5, 8, 128), F32)], [VMEM, SMEM],
+        spread_kernel, [HBM] * 6, spread_outs,
+        [pltpu.SMEM((32,), jnp.int32), pltpu.SMEM((32,), jnp.int32), pltpu.VMEM((1, 32), BF16),
+         pltpu.VMEM((1, 32), BF16), pltpu.VMEM((3, 32, 128), BF16), pltpu.VMEM((32, 3, 8, 128), BF16),
+         pltpu.SMEM((32,), jnp.int32), pltpu.VMEM((32, 24, 128), F32), pltpu.VMEM((32, 24, 128), F32),
+         pltpu.VMEM((32, 5, 8, 128), F32), pltpu.SemaphoreType.DMA((6,))], [VMEM, SMEM],
     )(owner, brick_index, stiffness.reshape(1, 32), rest_sq.reshape(1, 32), positions.transpose(1, 0, 2), weights)
-    x_low, x_high = neighbours(velocity[:, :1], velocity[:, 15:], "row")
-    y_low, y_high = neighbours(velocity[:, :, :1], velocity[:, :, 7:], "col")
+    planes = (velocity[:, :1], velocity[:, 15:], velocity[:, :, :1], velocity[:, :, 7:])
+    planes, pushes, slots = lax.optimization_barrier((planes, pushes, slots))
+    x_low, x_high = neighbours(planes[0], planes[1], "row")
+    y_low, y_high = neighbours(planes[2], planes[3], "col")
     pushes = moved(pushes, "col")
     ids = pushes[:, 4, 0, 73:76].astype(jnp.int32)
 
@@ -521,9 +539,9 @@
     spectrum = call(y_back_kernel, [VMEM] * 5, codes_of(32, 8))(
         y_back, y_lanes_back, y_twiddle, spectrum, replies)
     spectrum = moved(spectrum, "col")
-    new_velocity = call(z_back_kernel, [VMEM] * 2, [3, 16, 8, 256])(z_back, spectrum)
-    marker_velocity = call(interpolate_kernel, [SMEM, SMEM, VMEM, VMEM], [3, 32, 128])(
-        owner, slots, spectrum, weights)
+    new_velocity, marker_velocity = call(
+        last_kernel, [SMEM, SMEM, VMEM, VMEM, VMEM], ([3, 16, 8, 256], [3, 32, 128]))(
+        owner, slots, z_back, spectrum, weights)
     return new_velocity, marker_velocity.transpose(1, 0, 2)
 
 

time: 137 us -> 133 us (0.971)
  Pallas kernels: 31.6 us -> 20.2 us
  waiting for transfers between devices: 24.2 us -> 30.8 us
    pallas_call x1, Pallas kernels: 12.8 us -> 2.87 us  [local(): replies = call(reply_kernel, [SMEM, VMEM], codes_of(32, 5))(ids, turned)]
    all_to_all x4, waiting for transfers between devices: 20.7 us -> 30.5 us  [moved(): return lax.all_to_all(x, axis, split_axis=0, concat_axis=0, tiled=True)]
    all_to_all x4, starting transfers between devices: 34.7 us -> 37.8 us  [moved(): return lax.all_to_all(x, axis, split_axis=0, concat_axis=0, tiled=True)]
    ppermute x2, waiting for transfers between devices: 3.05 us -> 0.01 us  [neighbours(): lax.ppermute(plane_high, axis, up)]
    ppermute x2, starting transfers between devices: 14.1 us -> 11.2 us  [neighbours(): lax.ppermute(plane_low, axis, down)]
    unnamed x50 -> x48, local copies, waits for them, and re-layouts: 3.68 us -> 2.76 us
    pallas_call x3 -> x2, Pallas kernels: 7.1 us -> 6.62 us  [the longest x1 4.35 us: local(): call(spread_kernel, [HBM] * 6, spread_outs, [pltpu.SMEM((32,), jnp.int32)...]
  transfers between devices with their start and end apart: 8 -> 8, of which waited for: 5 -> 4; matrix products, arithmetic and copies ran while one was open for 1% -> 1% of each run, Pallas kernels for 13% -> 3%
where the time goes in v2:
time: 133 us; the launch traced here: 132 us
  starting transfers between devices  54.5 us (41%)
  waiting for transfers between devices  30.8 us (23%)
  Pallas kernels  20.2 us (15%)
  blocking collectives  19.9 us (15%)
  local copies, waits for them, and re-layouts  4.75 us (4%)
    all_to_all x4, starting transfers between devices, moved(): return lax.all_to_all(x, axis, split_axis=0, concat_axis=0, tiled=True)  37.8 us
    all_to_all x4, waiting for transfers between devices, moved(): return lax.all_to_all(x, axis, split_axis=0, concat_axis=0, tiled=True)  30.5 us
    all_to_all x1, blocking collectives, moved(): return lax.all_to_all(x, axis, split_axis=0, concat_axis=0, tiled=True)  19.9 us
    ppermute x2, starting transfers between devices, neighbours(): lax.ppermute(plane_low, axis, down)  11.2 us
    ppermute x2, starting transfers between devices, neighbours(): lax.ppermute(plane_high, axis, up)  5.47 us
    pallas_call x1, Pallas kernels, local(): call(spread_kernel, [HBM] * 6, spread_outs, [pltpu.SMEM((32,), jnp.int32)...  4.35 us
    pallas_call x1, Pallas kernels, local(): call(x_kernel, [SMEM] + [VMEM] * 10, codes_of(16, 7))  3.79 us
    pallas_call x1, Pallas kernels, local(): call(gather_kernel, [SMEM, VMEM, VMEM, VMEM], codes_of(32, 4), [pltpu.VME...  3.55 us
  transfers between devices with their start and end apart: 8, of which 4 were waited for; matrix products, arithmetic and copies ran while one was open for 1% of the time, Pallas kernels for 3%

profile of v2, /device:TPU:1, one launch (start us, length us, event | category | flops | bytes accessed | tf_op | source)
XLA Modules:
  0.0 132.0 jit_solution(7072662377640698834)
XLA Ops:
  0.6 1.2 fusion.25
  1.9 0.8 fusion.26
  3.3 4.3 %shard_map.239 = (s16[32,5,8,128]{3,2,1,0:T(8,128)(2,1)}, s32[32]{0:T(128)S(1)}) custom-call(s32[32]{0:T(128)S(1)} %bitcast.11, s32[32]{0:T(128)S(1)} %copy-done.18, bf16[1,32]{1,0:T(2,128)(2,1)S(1)} %bitcast.13, bf16[1,32]{1,0:T(2,128)(2,1)S(1)} %bitcast.14, bf16[3,32,128]{2,1,0:T(8,128)(2,1)S(1)} %bitcast.10, bf16[32,3,8,128]{3,2,1,0:T(8,128)(2,1)S(1)} %copy-done.1), custom_call_target="tpu_custom_call" | custom-call | tf_op jit(solution)/shard_map/pallas_call | solution.py:514
  7.7 10.6 %all-to-all-start = ((s16[32,5,8,128]{3,2,1,0:T(8,128)(2,1)}), s16[32,5,8,128]{3,2,1,0:T(8,128)(2,1)S(1)}, u32[]{:S(2)}, u32[]{:S(2)}) async-start(s16[32,5,8,128]{3,2,1,0:T(8,128)(2,1)} %get-tuple-element.17), calls=%async_computation | async-start | bytes 655360 | tf_op jit(solution)/shard_map/all_to_all | solution.py:494
  18.3 3.5 %collective-permute-start.2 = (f32[3,16,1,256]{3,2,1,0:T(1,128)S(1)}, f32[3,16,1,256]{3,2,1,0:T(1,128)S(1)}, u32[]{:S(2)}, u32[]{:S(2)}) collective-permute-start(f32[3,16,1,256]{3,2,1,0:T(1,128)S(1)} %get-tuple-element.20), channel_id=1, source_target_pairs={{0,1},{1,2},{2,3},{3,4},{4,5},{5,6},{6,7},{7,8},{8,9},{9,10},{10,1... | collective-permute-start | bytes 147464 | tf_op jit(solution)/shard_map/ppermute | solution.py:501
  21.8 1.9 %collective-permute-start.3 = (f32[3,16,1,256]{3,2,1,0:T(1,128)S(1)}, f32[3,16,1,256]{3,2,1,0:T(1,128)S(1)}, u32[]{:S(2)}, u32[]{:S(2)}) collective-permute-start(f32[3,16,1,256]{3,2,1,0:T(1,128)S(1)} %get-tuple-element.21), channel_id=1, source_target_pairs={{1,0},{2,1},{3,2},{4,3},{5,4},{6,5},{7,6},{8,7},{9,8},{10,9},{11,1... | collective-permute-start | bytes 147464 | tf_op jit(solution)/shard_map/ppermute | solution.py:501
  23.8 1.9 %collective-permute-start = (f32[3,1,8,256]{3,2,1,0:T(8,128)S(1)}, f32[3,1,8,256]{3,2,1,0:T(8,128)S(1)}, u32[]{:S(2)}, u32[]{:S(2)}) collective-permute-start(f32[3,1,8,256]{3,2,1,0:T(8,128)S(1)} %get-tuple-element.18), channel_id=1, source_target_pairs={{0,32},{32,64},{64,96},{96,128},{128,160},{160,192},{192,224},{224... | collective-permute-start | bytes 73736 | tf_op jit(solution)/shard_map/ppermute | solution.py:501
  25.7 9.3 %collective-permute-start.1 = (f32[3,1,8,256]{3,2,1,0:T(8,128)S(1)}, f32[3,1,8,256]{3,2,1,0:T(8,128)S(1)}, u32[]{:S(2)}, u32[]{:S(2)}) collective-permute-start(f32[3,1,8,256]{3,2,1,0:T(8,128)S(1)} %get-tuple-element.19), channel_id=1, source_target_pairs={{32,0},{64,32},{96,64},{128,96},{160,128},{192,160},{224,192},{256... | collective-permute-start | bytes 73736 | tf_op jit(solution)/shard_map/ppermute | solution.py:501
  35.0 0.6 copy-done.23
  36.7 3.6 %shard_map.241 = s16[32,4,8,128]{3,2,1,0:T(8,128)(2,1)} custom-call(s32[32,3]{1,0:T(8,128)S(1)} %bitcast.8, bf16[2,256,256]{2,1,0:T(8,128)(2,1)S(1)} %copy-done, s16[32,5,8,128]{3,2,1,0:T(8,128)(2,1)S(1)} %all-to-all-done.pushes, f32[256,384]{1,0:T(8,128)S(1)} %get-tuple-element.22.spectrum), custom_call_target="tpu_custom_call" | custom-call | tf_op jit(solution)/shard_map/pallas_call | solution.py:530
  40.2 8.5 %all-to-all-start.1 = ((s16[32,4,8,128]{3,2,1,0:T(8,128)(2,1)}), s16[32,4,8,128]{3,2,1,0:T(8,128)(2,1)S(1)}, u32[]{:S(2)}, u32[]{:S(2)}) async-start(s16[32,4,8,128]{3,2,1,0:T(8,128)(2,1)} %shard_map.241), calls=%async_computation.1 | async-start | bytes 524288 | tf_op jit(solution)/shard_map/all_to_all | solution.py:494
  48.7 0.7 copy-done.22
  49.4 8.2 %all-to-all-done.1.values = s16[32,4,8,128]{3,2,1,0:T(8,128)(2,1)S(1)} async-done(((s16[32,4,8,128]{3,2,1,0:T(8,128)(2,1)}), s16[32,4,8,128]{3,2,1,0:T(8,128)(2,1)S(1)}, u32[]{:S(2)}, u32[]{:S(2)}) %all-to-all-start.1) | async-done | bytes 262176 | tf_op jit(solution)/shard_map/all_to_all | solution.py:494
  57.6 1.6 %shard_map.242 = s16[16,7,8,128]{3,2,1,0:T(8,128)(2,1)} custom-call(bf16[2,256,256]{2,1,0:T(8,128)(2,1)S(1)} %copy-done.6, bf16[2,128,256]{2,1,0:T(8,128)(2,1)S(1)} %copy-done.10, f32[2,32,1,128]{3,2,1,0:T(1,128)S(1)} %copy-done.11, s16[32,4,8,128]{3,2,1,0:T(8,128)(2,1)S(1)} %all-to-all-done.1.values), custom_call_target="tpu_custom_call" | custom-call | tf_op jit(solution)/shard_map/pallas_call | solution.py:533
  59.2 9.5 %all-to-all-start.2 = ((s16[16,7,8,128]{3,2,1,0:T(8,128)(2,1)}), s16[16,7,8,128]{3,2,1,0:T(8,128)(2,1)S(1)}, u32[]{:S(2)}, u32[]{:S(2)}) async-start(s16[16,7,8,128]{3,2,1,0:T(8,128)(2,1)} %shard_map.242), calls=%async_computation.2 | async-start | bytes 458752 | tf_op jit(solution)/shard_map/all_to_all | solution.py:494
  68.8 0.7 copy-done.21
  70.2 12.0 %all-to-all-done.2.values = s16[16,7,8,128]{3,2,1,0:T(8,128)(2,1)S(1)} async-done(((s16[16,7,8,128]{3,2,1,0:T(8,128)(2,1)}), s16[16,7,8,128]{3,2,1,0:T(8,128)(2,1)S(1)}, u32[]{:S(2)}, u32[]{:S(2)}) %all-to-all-start.2) | async-done | bytes 229408 | tf_op jit(solution)/shard_map/all_to_all | solution.py:494
  82.3 3.8 %shard_map.243 = s16[16,7,8,128]{3,2,1,0:T(8,128)(2,1)} custom-call(s32[2]{0:T(128)S(1)} %add_convert_fusion.flags, bf16[2,256,256]{2,1,0:T(8,128)(2,1)S(1)} %copy-done.8, bf16[2,64,256]{2,1,0:T(8,128)(2,1)S(1)} %copy-done.14, bf16[2,256,320]{2,1,0:T(8,128)(2,1)S(1)} %copy-done.3, bf16[2,128,256]{2,1,0:T(8,128)(2,1)S(1)} %copy-done.12, ...), custom_call_target="tpu_custom_call" | custom-call | tf_op jit(solution)/shard_map/pallas_call | solution.py:535
  86.1 9.3 %all-to-all-start.3 = ((s16[16,7,8,128]{3,2,1,0:T(8,128)(2,1)}), s16[16,7,8,128]{3,2,1,0:T(8,128)(2,1)S(1)}, u32[]{:S(2)}, u32[]{:S(2)}) async-start(s16[16,7,8,128]{3,2,1,0:T(8,128)(2,1)} %shard_map.243), calls=%async_computation.3 | async-start | bytes 458752 | tf_op jit(solution)/shard_map/all_to_all | solution.py:494
  95.4 2.9 %shard_map.244.replies = s16[32,5,8,128]{3,2,1,0:T(8,128)(2,1)S(1)} custom-call(s32[32,3]{1,0:T(8,128)S(1)} %bitcast.9, f32[3,32,8,128]{3,2,1,0:T(8,128)S(1)} %get-tuple-element.23.turned), custom_call_target="tpu_custom_call" | custom-call | tf_op jit(solution)/shard_map/pallas_call | solution.py:538
  98.3 10.3 %all-to-all-done.3.values = s16[16,7,8,128]{3,2,1,0:T(8,128)(2,1)S(1)} async-done(((s16[16,7,8,128]{3,2,1,0:T(8,128)(2,1)}), s16[16,7,8,128]{3,2,1,0:T(8,128)(2,1)S(1)}, u32[]{:S(2)}, u32[]{:S(2)}) %all-to-all-start.3) | async-done | bytes 229408 | tf_op jit(solution)/shard_map/all_to_all | solution.py:494
  108.6 1.2 shard_map.245
  109.8 19.9 %all_to_all.25.values = s16[32,8,8,128]{3,2,1,0:T(8,128)(2,1)S(1)} all-to-all(s16[32,8,8,128]{3,2,1,0:T(8,128)(2,1)S(1)} %shard_map.245), channel_id=1, replica_groups=mesh['row'=16,'col'=32] {'col'}, dimensions={0} | all-to-all | bytes 1048576 | tf_op jit(solution)/shard_map/all_to_all | solution.py:494
  129.7 2.3 %shard_map.246 = (f32[3,16,8,256]{3,2,1,0:T(8,128)}, f32[3,32,128]{2,1,0:T(8,128)}) custom-call(s32[32]{0:T(128)S(1)} %bitcast.12, s32[32]{0:T(128)S(1)} %get-tuple-element.16.slots, bf16[2,256,256]{2,1,0:T(8,128)(2,1)S(1)} %copy-done.5, s16[32,8,8,128]{3,2,1,0:T(8,128)(2,1)S(1)} %all_to_all.25.values, bf16[32,3,8,128]{3,2,1,0:T(8,128)(2,1)S(1)} %copy-done.1), custom_call_target="tpu_custom_call" | custom-call | tf_op jit(solution)/shard_map/pallas_call | solution.py:542
  (60 shorter events, 2.5 us)
Async XLA Ops:
  0.6 2.0 %copy-start.1 = (bf16[32,3,8,128]{3,2,1,0:T(8,128)(2,1)S(1)}, bf16[32,3,8,128]{3,2,1,0:T(8,128)(2,1)}, u32[]{:S(2)}) copy-start(bf16[32,3,8,128]{3,2,1,0:T(8,128)(2,1)} %weights.1) | copy-start | bytes 589828
  7.7 28.2 %copy-start.2 = (f32[3,16,8,256]{3,2,1,0:T(8,128)S(1)}, f32[3,16,8,256]{3,2,1,0:T(8,128)}, u32[]{:S(2)}) copy-start(f32[3,16,8,256]{3,2,1,0:T(8,128)} %velocity.1) | copy-start | bytes 1179652
  7.7 28.2 %copy-start = (bf16[2,256,256]{2,1,0:T(8,128)(2,1)S(1)}, bf16[2,256,256]{2,1,0:T(8,128)(2,1)}, u32[]{:S(2)}) copy-start(bf16[2,256,256]{2,1,0:T(8,128)(2,1)} %constant.110.clone.table) | copy-start | bytes 786436
  7.7 28.8 %all-to-all-start = ((s16[32,5,8,128]{3,2,1,0:T(8,128)(2,1)}), s16[32,5,8,128]{3,2,1,0:T(8,128)(2,1)S(1)}, u32[]{:S(2)}, u32[]{:S(2)}) async-start(s16[32,5,8,128]{3,2,1,0:T(8,128)(2,1)} %get-tuple-element.17), calls=%async_computation | async-start | bytes 655360 | tf_op jit(solution)/shard_map/all_to_all | solution.py:494
  18.3 17.6 %collective-permute-start.2 = (f32[3,16,1,256]{3,2,1,0:T(1,128)S(1)}, f32[3,16,1,256]{3,2,1,0:T(1,128)S(1)}, u32[]{:S(2)}, u32[]{:S(2)}) collective-permute-start(f32[3,16,1,256]{3,2,1,0:T(1,128)S(1)} %get-tuple-element.20), channel_id=1, source_target_pairs={{0,1},{1,2},{2,3},{3,4},{4,5},{5,6},{6,7},{7,8},{8,9},{9,10},{10,1... | collective-permute-start | bytes 147464 | tf_op jit(solution)/shard_map/ppermute | solution.py:501
  21.8 14.1 %collective-permute-start.3 = (f32[3,16,1,256]{3,2,1,0:T(1,128)S(1)}, f32[3,16,1,256]{3,2,1,0:T(1,128)S(1)}, u32[]{:S(2)}, u32[]{:S(2)}) collective-permute-start(f32[3,16,1,256]{3,2,1,0:T(1,128)S(1)} %get-tuple-element.21), channel_id=1, source_target_pairs={{1,0},{2,1},{3,2},{4,3},{5,4},{6,5},{7,6},{8,7},{9,8},{10,9},{11,1... | collective-permute-start | bytes 147464 | tf_op jit(solution)/shard_map/ppermute | solution.py:501
  23.8 11.9 %collective-permute-start = (f32[3,1,8,256]{3,2,1,0:T(8,128)S(1)}, f32[3,1,8,256]{3,2,1,0:T(8,128)S(1)}, u32[]{:S(2)}, u32[]{:S(2)}) collective-permute-start(f32[3,1,8,256]{3,2,1,0:T(8,128)S(1)} %get-tuple-element.18), channel_id=1, source_target_pairs={{0,32},{32,64},{64,96},{96,128},{128,160},{160,192},{192,224},{224... | collective-permute-start | bytes 73736 | tf_op jit(solution)/shard_map/ppermute | solution.py:501
  25.7 10.2 %collective-permute-start.1 = (f32[3,1,8,256]{3,2,1,0:T(8,128)S(1)}, f32[3,1,8,256]{3,2,1,0:T(8,128)S(1)}, u32[]{:S(2)}, u32[]{:S(2)}) collective-permute-start(f32[3,1,8,256]{3,2,1,0:T(8,128)S(1)} %get-tuple-element.19), channel_id=1, source_target_pairs={{32,0},{64,32},{96,64},{128,96},{160,128},{192,160},{224,192},{256... | collective-permute-start | bytes 73736 | tf_op jit(solution)/shard_map/ppermute | solution.py:501
  40.2 17.4 %copy-start.6 = (bf16[2,256,256]{2,1,0:T(8,128)(2,1)S(1)}, bf16[2,256,256]{2,1,0:T(8,128)(2,1)}, u32[]{:S(2)}) copy-start(bf16[2,256,256]{2,1,0:T(8,128)(2,1)} %constant.111.clone.left) | copy-start | bytes 786436
  40.2 17.4 %copy-start.10 = (bf16[2,128,256]{2,1,0:T(8,128)(2,1)S(1)}, bf16[2,128,256]{2,1,0:T(8,128)(2,1)}, u32[]{:S(2)}) copy-start(bf16[2,128,256]{2,1,0:T(8,128)(2,1)} %constant.112.clone.lanes) | copy-start | bytes 393220
  40.2 17.4 %copy-start.11 = (f32[2,32,1,128]{3,2,1,0:T(1,128)S(1)}, f32[2,32,1,128]{3,2,1,0:T(1,128)}, u32[]{:S(2)}) copy-start(f32[2,32,1,128]{3,2,1,0:T(1,128)} %constant.113.clone.twiddle) | copy-start | bytes 98308
  40.2 17.4 %all-to-all-start.1 = ((s16[32,4,8,128]{3,2,1,0:T(8,128)(2,1)}), s16[32,4,8,128]{3,2,1,0:T(8,128)(2,1)S(1)}, u32[]{:S(2)}, u32[]{:S(2)}) async-start(s16[32,4,8,128]{3,2,1,0:T(8,128)(2,1)} %shard_map.241), calls=%async_computation.1 | async-start | bytes 524288 | tf_op jit(solution)/shard_map/all_to_all | solution.py:494
  59.2 23.1 %all-to-all-start.2 = ((s16[16,7,8,128]{3,2,1,0:T(8,128)(2,1)}), s16[16,7,8,128]{3,2,1,0:T(8,128)(2,1)S(1)}, u32[]{:S(2)}, u32[]{:S(2)}) async-start(s16[16,7,8,128]{3,2,1,0:T(8,128)(2,1)} %shard_map.242), calls=%async_computation.2 | async-start | bytes 458752 | tf_op jit(solution)/shard_map/all_to_all | solution.py:494
  69.5 12.8 %copy-start.13 = (bf16[2,128,256]{2,1,0:T(8,128)(2,1)S(1)}, bf16[2,128,256]{2,1,0:T(8,128)(2,1)}, u32[]{:S(2)}) copy-start(bf16[2,128,256]{2,1,0:T(8,128)(2,1)} %constant.118.clone.lanes_back) | copy-start | bytes 393220
  69.5 12.8 %copy-start.14 = (bf16[2,64,256]{2,1,0:T(8,128)(2,1)S(1)}, bf16[2,64,256]{2,1,0:T(8,128)(2,1)}, u32[]{:S(2)}) copy-start(bf16[2,64,256]{2,1,0:T(8,128)(2,1)} %constant.115.clone.left_extra) | copy-start | bytes 196612
  69.5 12.8 %copy-start.15 = (bf16[128,256]{1,0:T(8,128)(2,1)S(1)}, bf16[128,256]{1,0:T(8,128)(2,1)}, u32[]{:S(2)}) copy-start(bf16[128,256]{1,0:T(8,128)(2,1)} %constant.120.clone.flips) | copy-start | bytes 196612
  69.8 12.4 %copy-start.3 = (bf16[2,256,320]{2,1,0:T(8,128)(2,1)S(1)}, bf16[2,256,320]{2,1,0:T(8,128)(2,1)}, u32[]{:S(2)}) copy-start(bf16[2,256,320]{2,1,0:T(8,128)(2,1)} %constant.116.clone.back) | copy-start | bytes 983044
  69.8 12.4 %copy-start.4 = (f32[2,40,8,128]{3,2,1,0:T(8,128)S(1)}, f32[2,40,8,128]{3,2,1,0:T(8,128)}, u32[]{:S(2)}) copy-start(f32[2,40,8,128]{3,2,1,0:T(8,128)} %constant.119.clone.twiddle) | copy-start | bytes 983044
  69.8 12.4 %copy-start.8 = (bf16[2,256,256]{2,1,0:T(8,128)(2,1)S(1)}, bf16[2,256,256]{2,1,0:T(8,128)(2,1)}, u32[]{:S(2)}) copy-start(bf16[2,256,256]{2,1,0:T(8,128)(2,1)} %constant.114.clone.left) | copy-start | bytes 786436
  69.9 12.4 %copy-start.12 = (bf16[2,128,256]{2,1,0:T(8,128)(2,1)S(1)}, bf16[2,128,256]{2,1,0:T(8,128)(2,1)}, u32[]{:S(2)}) copy-start(bf16[2,128,256]{2,1,0:T(8,128)(2,1)} %constant.117.clone.lanes) | copy-start | bytes 393220
  86.1 22.5 %all-to-all-start.3 = ((s16[16,7,8,128]{3,2,1,0:T(8,128)(2,1)}), s16[16,7,8,128]{3,2,1,0:T(8,128)(2,1)S(1)}, u32[]{:S(2)}, u32[]{:S(2)}) async-start(s16[16,7,8,128]{3,2,1,0:T(8,128)(2,1)} %shard_map.243), calls=%async_computation.3 | async-start | bytes 458752 | tf_op jit(solution)/shard_map/all_to_all | solution.py:494
  95.4 13.2 %copy-start.7 = (bf16[2,256,256]{2,1,0:T(8,128)(2,1)S(1)}, bf16[2,256,256]{2,1,0:T(8,128)(2,1)}, u32[]{:S(2)}) copy-start(bf16[2,256,256]{2,1,0:T(8,128)(2,1)} %constant.121.clone.back) | copy-start | bytes 786436
  95.4 13.2 %copy-start.9 = (bf16[2,128,256]{2,1,0:T(8,128)(2,1)S(1)}, bf16[2,128,256]{2,1,0:T(8,128)(2,1)}, u32[]{:S(2)}) copy-start(bf16[2,128,256]{2,1,0:T(8,128)(2,1)} %constant.122.clone.lanes) | copy-start | bytes 393220
  109.8 19.9 %copy-start.5 = (bf16[2,256,256]{2,1,0:T(8,128)(2,1)S(1)}, bf16[2,256,256]{2,1,0:T(8,128)(2,1)}, u32[]{:S(2)}) copy-start(bf16[2,256,256]{2,1,0:T(8,128)(2,1)} %constant.123.clone.back) | copy-start | bytes 786436
  (8 other events, 5.5 us)

commit v3 on v2

--- a/solution.py
+++ b/solution.py
@@ -195,7 +195,7 @@
 
 
 def encoded(x):
-    largest = jnp.maximum(jnp.maximum(jnp.abs(x[0]), jnp.abs(x[1])), jnp.abs(x[2]))
+    largest = jnp.max(jnp.abs(x), axis=0)
     largest = jnp.broadcast_to(jnp.max(largest, axis=-1, keepdims=True), largest.shape)
     exponent = to_exponent(largest)
     return jnp.round(x * steps_per_unit(exponent)[None]), exponent
@@ -231,8 +231,8 @@
     return jnp.sum(jnp.where(same, row, 0.0), axis=1, keepdims=True)
 
 
-def spread_kernel(owner_in, brick_in, stiffness_in, rest_in, positions_in, weights_in, out, slots,
-                  owner, brick, stiffness, rest_sq, positions, weights, count, cubes, marks, total, arrived):
+def spread_kernel(owner_in, brick_in, stiffness_in, rest_in, positions_in, weights_in, velocity,
+                  out, slots, x_first, x_last, y_last, owner, brick, stiffness, rest_sq, positions, weights, count, cubes, marks, total, arrived):
     pairs = ((weights_in, weights), (positions_in, positions), (rest_in, rest_sq),
              (stiffness_in, stiffness), (owner_in, owner), (brick_in, brick))
     copies = [pltpu.make_async_copy(a, b, arrived.at[i]) for i, (a, b) in enumerate(pairs)]
@@ -241,6 +241,10 @@
     total[...] = jnp.zeros(total.shape, F32)
     for d in range(32):
         count[d] = 0
+    for c in range(3):
+        x_first[c] = velocity[c, 0:1]
+        x_last[c] = velocity[c, 15:16]
+        y_last[c] = velocity[c, :, 7:8, :]
     for copy in copies:
         copy.wait()
     place = [positions[c].astype(F32) for c in range(3)]
@@ -252,6 +256,7 @@
     for c in range(3):
         tension = pull * segment[c]
         force.append(tension - pltpu.roll(tension, 1, 1))
+    largest = []
     for n in range(32):
         w0, w1, w2 = (weights[n, a].astype(F32) for a in range(3))
         cells = (w0[:, None, :] * w1[None, :, :]).reshape(64, 128)
@@ -260,11 +265,17 @@
         cells_high, cells_low = halves(cells)
         pushed_high, pushed_low = halves(pushed)
         both = ((1,), (1,))
-        cube = (dot(pushed_high, cells_high, both) + dot(pushed_low, cells_high, both)
-                + dot(pushed_high, cells_low, both))
-        exponent = to_exponent(jnp.broadcast_to(row_largest(cube), cube.shape))
-        marks[n] = exponent
-        cubes[n] = jnp.round(cube * steps_per_unit(exponent))
+        cube = dot(jnp.concatenate([pushed_high, pushed_low], 1), jnp.concatenate([cells_high, cells_high], 1), both)
+        cube = cube + dot(pushed_high, cells_low, both)
+        cubes[n] = cube
+        largest += [jnp.max(jnp.abs(cube[8 * c:8 * c + 8]), axis=0, keepdims=True) for c in range(3)]
+    largest = jnp.concatenate(largest, 0)
+    exponent = to_exponent(jnp.broadcast_to(row_largest(largest), (96, 128)))
+    marks[...] = exponent
+    steps = steps_per_unit(exponent)
+    for n in range(32):
+        for c in range(3):
+            cubes[n, 8 * c:8 * c + 8] = jnp.round(cubes[n, 8 * c:8 * c + 8] * steps[3 * n + c:3 * n + c + 1])
     half = lane_half()
     lane = lax.broadcasted_iota(jnp.int32, (8, 128), 1)
 
@@ -278,28 +289,31 @@
         for c in range(3):
             tile, side = tile_place(s, c)
             total[d, tile] += jnp.where(half == side, cubes[n, 8 * c:8 * c + 8, :], 0.0)
-            last = jnp.where(lane == 64 + 3 * s + c, marks[n, 8 * c:8 * c + 8, :], last)
+            last = jnp.where(lane == 64 + 3 * s + c, marks[pl.ds(3 * n + c, 1), :], last)
         total[d, 4] += last
 
     out[...] = narrow(total[...])
 
 
-def advect_kernel(table, velocity, x_low, x_high, y_low, y_high, spectrum, turned):
+def advect_kernel(table, velocity, x_low, x_high, y_low, spectrum, turned):
     u = [velocity[c].reshape(128, 256) for c in range(3)]
     sub = lax.broadcasted_iota(jnp.int32, (16, 8, 256), 1)
     rows = []
+    beyond = jnp.zeros((16, 8, 256), F32)
     for c in range(3):
         v = velocity[c]
+        beyond = jnp.where(sub == c, v[:, 0:1, :], beyond)
         turned[c] = jnp.transpose(u[c]).reshape(32, 8, 128)
         ahead = jnp.concatenate([v[1:], x_high[c]], 0)
         behind = jnp.concatenate([x_low[c], v[:-1]], 0)
         total = u[0] * (ahead - behind).reshape(128, 256)
-        ahead = jnp.where(sub == 7, y_high[c], pltpu.roll(v, 7, 1))
+        ahead = jnp.where(sub == 7, 0.0, pltpu.roll(v, 7, 1))
         behind = jnp.where(sub == 0, y_low[c], pltpu.roll(v, 1, 1))
         total = total + u[1] * (ahead - behind).reshape(128, 256)
         total = total + u[2] * (pltpu.roll(u[c], 255, 1) - pltpu.roll(u[c], 1, 1))
         rows.append(u[c] - (0.5 * DT_STEP) * total)
-    star = jnp.concatenate(rows, 0)
+    beyond = (-0.5 * DT_STEP) * y_low[1] * beyond
+    star = jnp.concatenate(rows + [beyond.reshape(128, 256)], 0)
     spectrum[...] = table_left(table, star, ((1,), (1,)))
 
 
@@ -325,11 +339,12 @@
                 forces[c][z_block] += jnp.where(half == x_half, cube, 0.0)
 
     field = jnp.concatenate([force[...].reshape(256, 128) for force in forces], 1)
-    total = spectrum[...] + table_left(table, DT_STEP * field)
-    codes, exponent = encoded(stacked(total).reshape(3, 32, 8, 128))
-    for c in range(3):
-        out[:, c] = narrow(codes[c])
-    out[:, 3] = narrow(exponent)
+    total = spectrum[:, :384] + table_left(table, DT_STEP * field)
+    total = jnp.concatenate([stacked(total), spectrum[:, 384:]], 0)
+    codes, exponent = encoded(total.reshape(4, 32, 8, 128))
+    for t in range(4):
+        out[:, t] = narrow(codes[t])
+    out[:, 4] = narrow(exponent)
 
 
 def reply_kernel(ids, turned, out):
@@ -381,8 +396,14 @@
 
 
 def y_kernel(left, lanes, twiddle, values, out):
-    steps = step(wide(values[:, 3]))
-    spectrum = [(wide(values[:, c]) * steps).reshape(256, 128) for c in range(3)]
+    steps = step(wide(values[:, 4]))
+    beyond = wide(values[:, 3]) * steps
+    beyond = jnp.concatenate([beyond[1:], beyond[:1]], 0)
+    last = lax.broadcasted_iota(jnp.int32, (1, 8, 128), 2) % 8 == 7
+    spectrum = []
+    for c in range(3):
+        part = wide(values[:, c]) * steps + jnp.where(last, pltpu.roll(beyond, 7 - c, 2), 0.0)
+        spectrum.append(part.reshape(256, 128))
     spectrum = table_left(left, jnp.concatenate(spectrum, 1))
     spectrum = stacked(spectrum).reshape(96, 8, 128)
     spectrum = twiddled(spectrum, twiddle[0], twiddle[1])
@@ -494,11 +515,9 @@
     return lax.all_to_all(x, axis, split_axis=0, concat_axis=0, tiled=True)
 
 
-def neighbours(plane_low, plane_high, axis):
+def shifted(plane, axis, by):
     count = lax.axis_size(axis)
-    up = [(i, (i + 1) % count) for i in range(count)]
-    down = [((i + 1) % count, i) for i in range(count)]
-    return lax.ppermute(plane_high, axis, up), lax.ppermute(plane_low, axis, down)
+    return lax.ppermute(plane, axis, [(i, (i + by) % count) for i in range(count)])
 
 
 def local(velocity, positions, weights, stiffness, rest_sq, owner_column, brick_index):
@@ -510,24 +529,24 @@
     units, damping = wave_tables(marks, row, col)
 
     owner = owner_column.reshape(32)
-    spread_outs = (jax.ShapeDtypeStruct((32, 5, 8, 128), jnp.int16), jax.ShapeDtypeStruct((32,), jnp.int32))
-    pushes, slots = call(
-        spread_kernel, [HBM] * 6, spread_outs,
+    spread_outs = (codes_of(32, 5), jax.ShapeDtypeStruct((32,), jnp.int32), [3, 1, 8, 256], [3, 1, 8, 256], [3, 16, 1, 256])
+    pushes, slots, x_first, x_last, y_last = call(
+        spread_kernel, [HBM] * 6 + [VMEM], spread_outs,
         [pltpu.SMEM((32,), jnp.int32), pltpu.SMEM((32,), jnp.int32), pltpu.VMEM((1, 32), BF16),
          pltpu.VMEM((1, 32), BF16), pltpu.VMEM((3, 32, 128), BF16), pltpu.VMEM((32, 3, 8, 128), BF16),
-         pltpu.SMEM((32,), jnp.int32), pltpu.VMEM((32, 24, 128), F32), pltpu.VMEM((32, 24, 128), F32),
-         pltpu.VMEM((32, 5, 8, 128), F32), pltpu.SemaphoreType.DMA((6,))], [VMEM, SMEM],
-    )(owner, brick_index, stiffness.reshape(1, 32), rest_sq.reshape(1, 32), positions.transpose(1, 0, 2), weights)
-    planes = (velocity[:, :1], velocity[:, 15:], velocity[:, :, :1], velocity[:, :, 7:])
-    planes, pushes, slots = lax.optimization_barrier((planes, pushes, slots))
-    x_low, x_high = neighbours(planes[0], planes[1], "row")
-    y_low, y_high = neighbours(planes[2], planes[3], "col")
+         pltpu.SMEM((32,), jnp.int32), pltpu.VMEM((32, 24, 128), F32), pltpu.VMEM((96, 128), F32),
+         pltpu.VMEM((32, 5, 8, 128), F32), pltpu.SemaphoreType.DMA((6,))], [VMEM, SMEM, VMEM, VMEM, VMEM],
+    )(owner, brick_index, stiffness.reshape(1, 32), rest_sq.reshape(1, 32), positions.transpose(1, 0, 2), weights,
+      velocity)
+    y_low = shifted(y_last, "col", 1)
+    x_low = shifted(x_last, "row", 1)
+    x_high = shifted(x_first, "row", -1)
     pushes = moved(pushes, "col")
     ids = pushes[:, 4, 0, 73:76].astype(jnp.int32)
 
-    spectrum, turned = call(advect_kernel, [VMEM] * 6, ([256, 384], [3, 32, 8, 128]))(
-        z_fore, velocity, x_low, x_high, y_low, y_high)
-    spectrum = call(gather_kernel, [SMEM, VMEM, VMEM, VMEM], codes_of(32, 4),
+    spectrum, turned = call(advect_kernel, [VMEM] * 5, ([256, 512], [3, 32, 8, 128]))(
+        z_fore, velocity, x_low, x_high, y_low)
+    spectrum = call(gather_kernel, [SMEM, VMEM, VMEM, VMEM], codes_of(32, 5),
                     [pltpu.VMEM((32, 8, 128), F32)] * 3)(ids, z_fore, pushes, spectrum)
     spectrum = moved(spectrum, "col")
     spectrum = call(y_kernel, [VMEM] * 4, codes_of(16, 7))(y_fore, y_lanes, y_twiddle, spectrum)

time: 133 us -> 131 us (0.985)
  starting transfers between devices: 54.5 us -> 51.9 us
  waiting for transfers between devices: 30.8 us -> 32.2 us
    unnamed x48 -> x52, local copies, waits for them, and re-layouts: 2.76 us -> 4.75 us
    slice x2 -> x0, local copies, waits for them, and re-layouts: 1.99 us -> none  [the longest x1 1.22 us: local(): velocity[:, :, 7:]]
    ppermute x4 -> x3, starting transfers between devices: 16.7 us -> 15 us  [shifted(): lax.ppermute(plane, axis, [(i, (i + by) % count) for i in range(count)])]
  transfers between devices with their start and end apart: 8 -> 7, of which waited for: 4 -> 4; matrix products, arithmetic and copies ran while one was open for 1% -> 1% of each run, Pallas kernels for 3% -> 3%
where the time goes in v3:
time: 131 us; the launch traced here: 130 us
  starting transfers between devices  51.9 us (40%)
  waiting for transfers between devices  32.2 us (25%)
  blocking collectives  19.9 us (15%)
  Pallas kernels  19.8 us (15%)
  local copies, waits for them, and re-layouts  4.75 us (4%)
    all_to_all x4, starting transfers between devices, moved(): return lax.all_to_all(x, axis, split_axis=0, concat_axis=0, tiled=True)  36.8 us
    all_to_all x4, waiting for transfers between devices, moved(): return lax.all_to_all(x, axis, split_axis=0, concat_axis=0, tiled=True)  31.7 us
    all_to_all x1, blocking collectives, moved(): return lax.all_to_all(x, axis, split_axis=0, concat_axis=0, tiled=True)  19.9 us
    ppermute x3, starting transfers between devices, shifted(): lax.ppermute(plane, axis, [(i, (i + by) % count) for i in range(count)])  15 us
    unnamed x52, local copies, waits for them, and re-layouts  4.75 us
    pallas_call x1, Pallas kernels, local(): call(spread_kernel, [HBM] * 6 + [VMEM], spread_outs, [pltpu.SMEM((32,), j...  3.81 us
    pallas_call x1, Pallas kernels, local(): call(x_kernel, [SMEM] + [VMEM] * 10, codes_of(16, 7))  3.79 us
    pallas_call x1, Pallas kernels, local(): call(gather_kernel, [SMEM, VMEM, VMEM, VMEM], codes_of(32, 5), [pltpu.VME...  3.57 us
  transfers between devices with their start and end apart: 7, of which 4 were waited for; matrix products, arithmetic and copies ran while one was open for 1% of the time, Pallas kernels for 3%

profile of v3, /device:TPU:1, one launch (start us, length us, event | category | flops | bytes accessed | tf_op | source)
XLA Modules:
  0.0 130.3 jit_solution(16283168949280530888)
XLA Ops:
  1.3 1.0 copy-done
  2.3 0.9 copy-done.3
  3.3 0.7 copy-done.18
  4.0 3.8 %shard_map.239 = (s16[32,5,8,128]{3,2,1,0:T(8,128)(2,1)}, s32[32]{0:T(128)S(1)}, f32[3,1,8,256]{3,2,1,0:T(8,128)S(1)}, f32[3,1,8,256]{3,2,1,0:T(8,128)S(1)}, f32[3,16,1,256]{3,2,1,0:T(1,128)S(1)}) custom-call(s32[32]{0:T(128)S(1)} %bitcast.11, s32[32]{0:T(128)S(1)} %copy-done.20, bf16[1,32]{1,0:T(2,128)(2,1)S(1)} %bitcast.13, bf16[1,32]{1,0:T(2,128)(2,1)S(1)} %bitcast.14, ...), custom_call_target="tpu_custom_call" | custom-call | tf_op jit(solution)/shard_map/pallas_call | solution.py:533
  7.8 10.6 %all-to-all-start = ((s16[32,5,8,128]{3,2,1,0:T(8,128)(2,1)}), s16[32,5,8,128]{3,2,1,0:T(8,128)(2,1)S(1)}, u32[]{:S(2)}, u32[]{:S(2)}) async-start(s16[32,5,8,128]{3,2,1,0:T(8,128)(2,1)} %get-tuple-element.12), calls=%async_computation | async-start | bytes 655360 | tf_op jit(solution)/shard_map/all_to_all | solution.py:515
  18.4 1.9 %collective-permute-start = (f32[3,1,8,256]{3,2,1,0:T(8,128)S(1)}, f32[3,1,8,256]{3,2,1,0:T(8,128)S(1)}, u32[]{:S(2)}, u32[]{:S(2)}) collective-permute-start(f32[3,1,8,256]{3,2,1,0:T(8,128)S(1)} %get-tuple-element.13), channel_id=1, source_target_pairs={{0,32},{32,64},{64,96},{96,128},{128,160},{160,192},{192,224},{224... | collective-permute-start | bytes 73736 | tf_op jit(solution)/shard_map/ppermute | solution.py:520
  20.3 9.3 %collective-permute-start.1 = (f32[3,1,8,256]{3,2,1,0:T(8,128)S(1)}, f32[3,1,8,256]{3,2,1,0:T(8,128)S(1)}, u32[]{:S(2)}, u32[]{:S(2)}) collective-permute-start(f32[3,1,8,256]{3,2,1,0:T(8,128)S(1)} %get-tuple-element.14), channel_id=1, source_target_pairs={{0,480},{32,0},{64,32},{96,64},{128,96},{160,128},{192,160},{224,1... | collective-permute-start | bytes 73736 | tf_op jit(solution)/shard_map/ppermute | solution.py:520
  29.6 3.8 %collective-permute-start.2 = (f32[3,16,1,256]{3,2,1,0:T(1,128)S(1)}, f32[3,16,1,256]{3,2,1,0:T(1,128)S(1)}, u32[]{:S(2)}, u32[]{:S(2)}) collective-permute-start(f32[3,16,1,256]{3,2,1,0:T(1,128)S(1)} %get-tuple-element.15), channel_id=1, source_target_pairs={{0,1},{1,2},{2,3},{3,4},{4,5},{5,6},{6,7},{7,8},{8,9},{9,10},{10,1... | collective-permute-start | bytes 147464 | tf_op jit(solution)/shard_map/ppermute | solution.py:520
  33.5 0.6 copy-done.25
  34.6 0.6 shard_map.240
  35.4 3.6 %shard_map.241 = s16[32,5,8,128]{3,2,1,0:T(8,128)(2,1)} custom-call(s32[32,3]{1,0:T(8,128)S(1)} %bitcast.8, bf16[2,256,256]{2,1,0:T(8,128)(2,1)S(1)} %copy-done.2, s16[32,5,8,128]{3,2,1,0:T(8,128)(2,1)S(1)} %all-to-all-done.pushes, f32[256,512]{1,0:T(8,128)S(1)} %get-tuple-element.16.spectrum), custom_call_target="tpu_custom_call" | custom-call | tf_op jit(solution)/shard_map/pallas_call | solution.py:549
  39.0 8.2 %all-to-all-start.1 = ((s16[32,5,8,128]{3,2,1,0:T(8,128)(2,1)}), s16[32,5,8,128]{3,2,1,0:T(8,128)(2,1)S(1)}, u32[]{:S(2)}, u32[]{:S(2)}) async-start(s16[32,5,8,128]{3,2,1,0:T(8,128)(2,1)} %shard_map.241), calls=%async_computation.1 | async-start | bytes 655360 | tf_op jit(solution)/shard_map/all_to_all | solution.py:515
  47.2 9.5 %all-to-all-done.1.values = s16[32,5,8,128]{3,2,1,0:T(8,128)(2,1)S(1)} async-done(((s16[32,5,8,128]{3,2,1,0:T(8,128)(2,1)}), s16[32,5,8,128]{3,2,1,0:T(8,128)(2,1)S(1)}, u32[]{:S(2)}, u32[]{:S(2)}) %all-to-all-start.1) | async-done | bytes 327712 | tf_op jit(solution)/shard_map/all_to_all | solution.py:515
  56.8 1.6 %shard_map.242 = s16[16,7,8,128]{3,2,1,0:T(8,128)(2,1)} custom-call(bf16[2,256,256]{2,1,0:T(8,128)(2,1)S(1)} %copy-done.9, bf16[2,128,256]{2,1,0:T(8,128)(2,1)S(1)} %copy-done.12, f32[2,32,1,128]{3,2,1,0:T(1,128)S(1)} %copy-done.13, s16[32,5,8,128]{3,2,1,0:T(8,128)(2,1)S(1)} %all-to-all-done.1.values), custom_call_target="tpu_custom_call" | custom-call | tf_op jit(solution)/shard_map/pallas_call | solution.py:552
  58.4 8.6 %all-to-all-start.2 = ((s16[16,7,8,128]{3,2,1,0:T(8,128)(2,1)}), s16[16,7,8,128]{3,2,1,0:T(8,128)(2,1)S(1)}, u32[]{:S(2)}, u32[]{:S(2)}) async-start(s16[16,7,8,128]{3,2,1,0:T(8,128)(2,1)} %shard_map.242), calls=%async_computation.2 | async-start | bytes 458752 | tf_op jit(solution)/shard_map/all_to_all | solution.py:515
  67.1 0.7 copy-done.23
  68.5 11.9 %all-to-all-done.2.values = s16[16,7,8,128]{3,2,1,0:T(8,128)(2,1)S(1)} async-done(((s16[16,7,8,128]{3,2,1,0:T(8,128)(2,1)}), s16[16,7,8,128]{3,2,1,0:T(8,128)(2,1)S(1)}, u32[]{:S(2)}, u32[]{:S(2)}) %all-to-all-start.2) | async-done | bytes 229408 | tf_op jit(solution)/shard_map/all_to_all | solution.py:515
  80.5 3.8 %shard_map.243 = s16[16,7,8,128]{3,2,1,0:T(8,128)(2,1)} custom-call(s32[2]{0:T(128)S(1)} %add_convert_fusion.flags, bf16[2,256,256]{2,1,0:T(8,128)(2,1)S(1)} %copy-done.10, bf16[2,64,256]{2,1,0:T(8,128)(2,1)S(1)} %copy-done.17, bf16[2,256,320]{2,1,0:T(8,128)(2,1)S(1)} %copy-done.5, bf16[2,128,256]{2,1,0:T(8,128)(2,1)S(1)} %copy-done.15, ...), custom_call_target="tpu_custom_call" | custom-call | tf_op jit(solution)/shard_map/pallas_call | solution.py:554
  84.3 9.4 %all-to-all-start.3 = ((s16[16,7,8,128]{3,2,1,0:T(8,128)(2,1)}), s16[16,7,8,128]{3,2,1,0:T(8,128)(2,1)S(1)}, u32[]{:S(2)}, u32[]{:S(2)}) async-start(s16[16,7,8,128]{3,2,1,0:T(8,128)(2,1)} %shard_map.243), calls=%async_computation.3 | async-start | bytes 458752 | tf_op jit(solution)/shard_map/all_to_all | solution.py:515
  93.7 2.9 %shard_map.244.replies = s16[32,5,8,128]{3,2,1,0:T(8,128)(2,1)S(1)} custom-call(s32[32,3]{1,0:T(8,128)S(1)} %bitcast.9, f32[3,32,8,128]{3,2,1,0:T(8,128)S(1)} %get-tuple-element.17.turned), custom_call_target="tpu_custom_call" | custom-call | tf_op jit(solution)/shard_map/pallas_call | solution.py:557
  96.6 10.3 %all-to-all-done.3.values = s16[16,7,8,128]{3,2,1,0:T(8,128)(2,1)S(1)} async-done(((s16[16,7,8,128]{3,2,1,0:T(8,128)(2,1)}), s16[16,7,8,128]{3,2,1,0:T(8,128)(2,1)S(1)}, u32[]{:S(2)}, u32[]{:S(2)}) %all-to-all-start.3) | async-done | bytes 229408 | tf_op jit(solution)/shard_map/all_to_all | solution.py:515
  106.8 1.2 shard_map.245
  108.1 19.9 %all_to_all.25.values = s16[32,8,8,128]{3,2,1,0:T(8,128)(2,1)S(1)} all-to-all(s16[32,8,8,128]{3,2,1,0:T(8,128)(2,1)S(1)} %shard_map.245), channel_id=1, replica_groups=mesh['row'=16,'col'=32] {'col'}, dimensions={0} | all-to-all | bytes 1048576 | tf_op jit(solution)/shard_map/all_to_all | solution.py:515
  128.0 2.3 %shard_map.246 = (f32[3,16,8,256]{3,2,1,0:T(8,128)}, f32[3,32,128]{2,1,0:T(8,128)}) custom-call(s32[32]{0:T(128)S(1)} %bitcast.12, s32[32]{0:T(128)S(1)} %get-tuple-element.11.slots, bf16[2,256,256]{2,1,0:T(8,128)(2,1)S(1)} %copy-done.7, s16[32,8,8,128]{3,2,1,0:T(8,128)(2,1)S(1)} %all_to_all.25.values, bf16[32,3,8,128]{3,2,1,0:T(8,128)(2,1)S(1)} %copy-done.4), custom_call_target="tpu_custom_call" | custom-call | tf_op jit(solution)/shard_map/pallas_call | solution.py:561
  (60 shorter events, 2.1 us)
Async XLA Ops:
  7.8 26.8 %copy-start.1 = (f32[3,16,8,256]{3,2,1,0:T(8,128)S(1)}, f32[3,16,8,256]{3,2,1,0:T(8,128)}, u32[]{:S(2)}) copy-start(f32[3,16,8,256]{3,2,1,0:T(8,128)} %velocity.3) | copy-start | bytes 1179652
  7.8 26.8 %copy-start.2 = (bf16[2,256,256]{2,1,0:T(8,128)(2,1)S(1)}, bf16[2,256,256]{2,1,0:T(8,128)(2,1)}, u32[]{:S(2)}) copy-start(bf16[2,256,256]{2,1,0:T(8,128)(2,1)} %constant.110.clone.table) | copy-start | bytes 786436
  7.8 27.4 %all-to-all-start = ((s16[32,5,8,128]{3,2,1,0:T(8,128)(2,1)}), s16[32,5,8,128]{3,2,1,0:T(8,128)(2,1)S(1)}, u32[]{:S(2)}, u32[]{:S(2)}) async-start(s16[32,5,8,128]{3,2,1,0:T(8,128)(2,1)} %get-tuple-element.12), calls=%async_computation | async-start | bytes 655360 | tf_op jit(solution)/shard_map/all_to_all | solution.py:515
  18.4 15.7 %collective-permute-start = (f32[3,1,8,256]{3,2,1,0:T(8,128)S(1)}, f32[3,1,8,256]{3,2,1,0:T(8,128)S(1)}, u32[]{:S(2)}, u32[]{:S(2)}) collective-permute-start(f32[3,1,8,256]{3,2,1,0:T(8,128)S(1)} %get-tuple-element.13), channel_id=1, source_target_pairs={{0,32},{32,64},{64,96},{96,128},{128,160},{160,192},{192,224},{224... | collective-permute-start | bytes 73736 | tf_op jit(solution)/shard_map/ppermute | solution.py:520
  20.3 13.8 %collective-permute-start.1 = (f32[3,1,8,256]{3,2,1,0:T(8,128)S(1)}, f32[3,1,8,256]{3,2,1,0:T(8,128)S(1)}, u32[]{:S(2)}, u32[]{:S(2)}) collective-permute-start(f32[3,1,8,256]{3,2,1,0:T(8,128)S(1)} %get-tuple-element.14), channel_id=1, source_target_pairs={{0,480},{32,0},{64,32},{96,64},{128,96},{160,128},{192,160},{224,1... | collective-permute-start | bytes 73736 | tf_op jit(solution)/shard_map/ppermute | solution.py:520
  29.6 5.0 %collective-permute-start.2 = (f32[3,16,1,256]{3,2,1,0:T(1,128)S(1)}, f32[3,16,1,256]{3,2,1,0:T(1,128)S(1)}, u32[]{:S(2)}, u32[]{:S(2)}) collective-permute-start(f32[3,16,1,256]{3,2,1,0:T(1,128)S(1)} %get-tuple-element.15), channel_id=1, source_target_pairs={{0,1},{1,2},{2,3},{3,4},{4,5},{5,6},{6,7},{7,8},{8,9},{9,10},{10,1... | collective-permute-start | bytes 147464 | tf_op jit(solution)/shard_map/ppermute | solution.py:520
  39.0 8.3 %copy-start.24 = (s32[320]{0:T(512)S(1)}, s32[320]{0:T(512)}, u32[]{:S(2)}) copy-start(s32[320]{0:T(512)} %constant.109.clone) | copy-start | bytes 3844
  39.0 17.8 %copy-start.9 = (bf16[2,256,256]{2,1,0:T(8,128)(2,1)S(1)}, bf16[2,256,256]{2,1,0:T(8,128)(2,1)}, u32[]{:S(2)}) copy-start(bf16[2,256,256]{2,1,0:T(8,128)(2,1)} %constant.111.clone.left) | copy-start | bytes 786436
  39.0 17.8 %copy-start.12 = (bf16[2,128,256]{2,1,0:T(8,128)(2,1)S(1)}, bf16[2,128,256]{2,1,0:T(8,128)(2,1)}, u32[]{:S(2)}) copy-start(bf16[2,128,256]{2,1,0:T(8,128)(2,1)} %constant.112.clone.lanes) | copy-start | bytes 393220
  39.0 17.8 %copy-start.13 = (f32[2,32,1,128]{3,2,1,0:T(1,128)S(1)}, f32[2,32,1,128]{3,2,1,0:T(1,128)}, u32[]{:S(2)}) copy-start(f32[2,32,1,128]{3,2,1,0:T(1,128)} %constant.113.clone.twiddle) | copy-start | bytes 98308
  39.0 17.8 %all-to-all-start.1 = ((s16[32,5,8,128]{3,2,1,0:T(8,128)(2,1)}), s16[32,5,8,128]{3,2,1,0:T(8,128)(2,1)S(1)}, u32[]{:S(2)}, u32[]{:S(2)}) async-start(s16[32,5,8,128]{3,2,1,0:T(8,128)(2,1)} %shard_map.241), calls=%async_computation.1 | async-start | bytes 655360 | tf_op jit(solution)/shard_map/all_to_all | solution.py:515
  58.4 22.1 %all-to-all-start.2 = ((s16[16,7,8,128]{3,2,1,0:T(8,128)(2,1)}), s16[16,7,8,128]{3,2,1,0:T(8,128)(2,1)S(1)}, u32[]{:S(2)}, u32[]{:S(2)}) async-start(s16[16,7,8,128]{3,2,1,0:T(8,128)(2,1)} %shard_map.242), calls=%async_computation.2 | async-start | bytes 458752 | tf_op jit(solution)/shard_map/all_to_all | solution.py:515
  67.8 12.7 %copy-start.15 = (bf16[2,128,256]{2,1,0:T(8,128)(2,1)S(1)}, bf16[2,128,256]{2,1,0:T(8,128)(2,1)}, u32[]{:S(2)}) copy-start(bf16[2,128,256]{2,1,0:T(8,128)(2,1)} %constant.117.clone.lanes) | copy-start | bytes 393220
  67.8 12.7 %copy-start.16 = (bf16[128,256]{1,0:T(8,128)(2,1)S(1)}, bf16[128,256]{1,0:T(8,128)(2,1)}, u32[]{:S(2)}) copy-start(bf16[128,256]{1,0:T(8,128)(2,1)} %constant.120.clone.flips) | copy-start | bytes 196612
  67.8 12.7 %copy-start.17 = (bf16[2,64,256]{2,1,0:T(8,128)(2,1)S(1)}, bf16[2,64,256]{2,1,0:T(8,128)(2,1)}, u32[]{:S(2)}) copy-start(bf16[2,64,256]{2,1,0:T(8,128)(2,1)} %constant.115.clone.left_extra) | copy-start | bytes 196612
  68.1 12.3 %copy-start.5 = (bf16[2,256,320]{2,1,0:T(8,128)(2,1)S(1)}, bf16[2,256,320]{2,1,0:T(8,128)(2,1)}, u32[]{:S(2)}) copy-start(bf16[2,256,320]{2,1,0:T(8,128)(2,1)} %constant.116.clone.back) | copy-start | bytes 983044
  68.1 12.3 %copy-start.6 = (f32[2,40,8,128]{3,2,1,0:T(8,128)S(1)}, f32[2,40,8,128]{3,2,1,0:T(8,128)}, u32[]{:S(2)}) copy-start(f32[2,40,8,128]{3,2,1,0:T(8,128)} %constant.119.clone.twiddle) | copy-start | bytes 983044
  68.1 12.3 %copy-start.10 = (bf16[2,256,256]{2,1,0:T(8,128)(2,1)S(1)}, bf16[2,256,256]{2,1,0:T(8,128)(2,1)}, u32[]{:S(2)}) copy-start(bf16[2,256,256]{2,1,0:T(8,128)(2,1)} %constant.114.clone.left) | copy-start | bytes 786436
  68.2 12.3 %copy-start.14 = (bf16[2,128,256]{2,1,0:T(8,128)(2,1)S(1)}, bf16[2,128,256]{2,1,0:T(8,128)(2,1)}, u32[]{:S(2)}) copy-start(bf16[2,128,256]{2,1,0:T(8,128)(2,1)} %constant.118.clone.lanes_back) | copy-start | bytes 393220
  84.3 22.6 %all-to-all-start.3 = ((s16[16,7,8,128]{3,2,1,0:T(8,128)(2,1)}), s16[16,7,8,128]{3,2,1,0:T(8,128)(2,1)S(1)}, u32[]{:S(2)}, u32[]{:S(2)}) async-start(s16[16,7,8,128]{3,2,1,0:T(8,128)(2,1)} %shard_map.243), calls=%async_computation.3 | async-start | bytes 458752 | tf_op jit(solution)/shard_map/all_to_all | solution.py:515
  93.7 13.2 %copy-start.8 = (bf16[2,256,256]{2,1,0:T(8,128)(2,1)S(1)}, bf16[2,256,256]{2,1,0:T(8,128)(2,1)}, u32[]{:S(2)}) copy-start(bf16[2,256,256]{2,1,0:T(8,128)(2,1)} %constant.121.clone.back) | copy-start | bytes 786436
  93.7 13.2 %copy-start.11 = (bf16[2,128,256]{2,1,0:T(8,128)(2,1)S(1)}, bf16[2,128,256]{2,1,0:T(8,128)(2,1)}, u32[]{:S(2)}) copy-start(bf16[2,128,256]{2,1,0:T(8,128)(2,1)} %constant.122.clone.lanes) | copy-start | bytes 393220
  108.1 19.9 %copy-start.4 = (bf16[32,3,8,128]{3,2,1,0:T(8,128)(2,1)S(1)}, bf16[32,3,8,128]{3,2,1,0:T(8,128)(2,1)}, u32[]{:S(2)}) copy-start(bf16[32,3,8,128]{3,2,1,0:T(8,128)(2,1)} %weights.1) | copy-start | bytes 589828
  108.1 19.9 %copy-start.7 = (bf16[2,256,256]{2,1,0:T(8,128)(2,1)S(1)}, bf16[2,256,256]{2,1,0:T(8,128)(2,1)}, u32[]{:S(2)}) copy-start(bf16[2,256,256]{2,1,0:T(8,128)(2,1)} %constant.123.clone.back) | copy-start | bytes 786436
  (9 other events, 6.7 us)

commit v4 on v3

--- a/solution.py
+++ b/solution.py
@@ -98,7 +98,7 @@
     first = np.concatenate([k_main, k_extra])
     wide[0] = np.cos(phase)[first]
     wide[1] = np.sin(phase)[first]
-    marks = (first, np.concatenate([p_main, p_extra]), np.concatenate([j_main, np.zeros(64, int)]))
+    marks = (first, np.concatenate([p_main, p_extra]), np.concatenate([j_main, np.full(64, -1)]))
     reverse = np.kron(np.eye(16), np.eye(8)[(7 - np.arange(8))])
     negate = np.kron(np.eye(16), np.eye(8)[(-np.arange(8)) % 8])
     flips = np.concatenate([reverse, negate], 1).astype(BF16)
@@ -231,8 +231,7 @@
     return jnp.sum(jnp.where(same, row, 0.0), axis=1, keepdims=True)
 
 
-def spread_kernel(owner_in, brick_in, stiffness_in, rest_in, positions_in, weights_in, velocity,
-                  out, slots, x_first, x_last, y_last, owner, brick, stiffness, rest_sq, positions, weights, count, cubes, marks, total, arrived):
+def spread_kernel(owner_in, brick_in, stiffness_in, rest_in, positions_in, weights_in, out, slots, owner, brick, stiffness, rest_sq, positions, weights, count, cubes, marks, total, arrived):
     pairs = ((weights_in, weights), (positions_in, positions), (rest_in, rest_sq),
              (stiffness_in, stiffness), (owner_in, owner), (brick_in, brick))
     copies = [pltpu.make_async_copy(a, b, arrived.at[i]) for i, (a, b) in enumerate(pairs)]
@@ -241,10 +240,6 @@
     total[...] = jnp.zeros(total.shape, F32)
     for d in range(32):
         count[d] = 0
-    for c in range(3):
-        x_first[c] = velocity[c, 0:1]
-        x_last[c] = velocity[c, 15:16]
-        y_last[c] = velocity[c, :, 7:8, :]
     for copy in copies:
         copy.wait()
     place = [positions[c].astype(F32) for c in range(3)]
@@ -295,7 +290,42 @@
     out[...] = narrow(total[...])
 
 
-def advect_kernel(table, velocity, x_low, x_high, y_low, spectrum, turned):
+def planes_kernel(_, velocity, x_first, x_last, y_last):
+    for c in range(3):
+        x_first[c] = velocity[c, 0:1]
+        x_last[c] = velocity[c, 15:16]
+        y_last[c] = velocity[c, :, 7:8, :]
+
+
+def add_up_kernel(ids, pushes, field0, field1, field2, other0, other1, other2):
+    sums = ((field0, field1, field2), (other0, other1, other2))
+    for group in sums:
+        for field in group:
+            field[...] = jnp.zeros(field.shape, F32)
+    half = lane_half()
+
+    @pl.loop(0, 16, unroll=2)
+    def _(pair):
+        for odd in range(2):
+            src = 2 * pair + odd
+            tiles = [wide(pushes[src, t]) for t in range(5)]
+            turned = [pltpu.roll(tile, 64, 1) for tile in tiles]
+            steps = step(tiles[4])
+            for slot in range(3):
+                brick = ids[src, slot]
+                x_half, z_block = brick >> 5, brick & 31
+                for c in range(3):
+                    at = 3 * slot + c
+                    tile, side = tile_place(slot, c)
+                    codes = jnp.where(half == side, tiles[tile], turned[tile])
+                    cube = codes * jnp.broadcast_to(steps[:, 64 + at:65 + at], (8, 128))
+                    sums[odd][c][z_block] += jnp.where(half == x_half, cube, 0.0)
+
+    for c in range(3):
+        sums[0][c][...] = sums[0][c][...] + sums[1][c][...]
+
+
+def star_kernel(table, velocity, x_low, x_high, y_low, field0, field1, field2, out, turned):
     u = [velocity[c].reshape(128, 256) for c in range(3)]
     sub = lax.broadcasted_iota(jnp.int32, (16, 8, 256), 1)
     rows = []
@@ -314,31 +344,8 @@
         rows.append(u[c] - (0.5 * DT_STEP) * total)
     beyond = (-0.5 * DT_STEP) * y_low[1] * beyond
     star = jnp.concatenate(rows + [beyond.reshape(128, 256)], 0)
-    spectrum[...] = table_left(table, star, ((1,), (1,)))
-
-
-def gather_kernel(ids, table, pushes, spectrum, out, force0, force1, force2):
-    forces = (force0, force1, force2)
-    for force in forces:
-        force[...] = jnp.zeros(force.shape, F32)
-    half = lane_half()
-
-    @pl.loop(0, 32, unroll=4)
-    def _(src):
-        tiles = [wide(pushes[src, t]) for t in range(5)]
-        turned = [pltpu.roll(tile, 64, 1) for tile in tiles]
-        steps = step(tiles[4])
-        for slot in range(3):
-            brick = ids[src, slot]
-            x_half, z_block = brick >> 5, brick & 31
-            for c in range(3):
-                at = 3 * slot + c
-                tile, side = tile_place(slot, c)
-                codes = jnp.where(half == side, tiles[tile], turned[tile])
-                cube = codes * jnp.broadcast_to(steps[:, 64 + at:65 + at], (8, 128))
-                forces[c][z_block] += jnp.where(half == x_half, cube, 0.0)
-
-    field = jnp.concatenate([force[...].reshape(256, 128) for force in forces], 1)
+    spectrum = table_left(table, star, ((1,), (1,)))
+    field = jnp.concatenate([field[...].reshape(256, 128) for field in (field0, field1, field2)], 1)
     total = spectrum[:, :384] + table_left(table, DT_STEP * field)
     total = jnp.concatenate([stacked(total), spectrum[:, 384:]], 0)
     codes, exponent = encoded(total.reshape(4, 32, 8, 128))
@@ -347,7 +354,10 @@
     out[:, 4] = narrow(exponent)
 
 
-def reply_kernel(ids, turned, out):
+def reply_kernel(ids, turned, weights, out, cells_high, cells_low):
+    for n in range(32):
+        w0, w1 = (weights[n, a].astype(F32) for a in range(2))
+        cells_high[n], cells_low[n] = halves((w0[:, None, :] * w1[None, :, :]).reshape(64, 128))
     half = lane_half()
     lane = lax.broadcasted_iota(jnp.int32, (8, 128), 1)
 
@@ -374,7 +384,7 @@
             out[src, t] = narrow(jnp.where(half == 0, codes[2 * t], codes[2 * t + 1]))
 
 
-def interpolate(owner, slots, replies, weights, out):
+def interpolate(owner, slots, replies, weights, cells_high, cells_low, out):
     half = lane_half()
     lane = lax.broadcasted_iota(jnp.int32, (8, 128), 1)
     for n in range(32):
@@ -388,9 +398,9 @@
             own = jnp.sum(jnp.where(lane == 64 + 3 * s + c, steps, 0.0), axis=1, keepdims=True)
             parts.append(cube * own)
         cube_high, cube_low = halves(jnp.concatenate(parts, 0)[:, :64])
-        w0, w1, w2 = (weights[n, a].astype(F32) for a in range(3))
-        cells_high, cells_low = halves((w0[:, None, :] * w1[None, :, :]).reshape(64, 128))
-        partial = dot(cube_high, cells_high) + dot(cube_low, cells_high) + dot(cube_high, cells_low)
+        w2 = weights[n, 2].astype(F32)
+        high = cells_high[n]
+        partial = dot(cube_high, high) + dot(cube_low, high) + dot(cube_high, cells_low[n])
         for c in range(3):
             out[c, n:n + 1] = jnp.sum(partial[8 * c:8 * c + 8] * w2, axis=0, keepdims=True)
 
@@ -454,8 +464,8 @@
     out[:, 7] = narrow(jnp.where(lane == 76, exponent, wide(replies[:, 4])))
 
 
-def last_kernel(owner, slots, back, values, weights, out, markers):
-    interpolate(owner, slots, values, weights, markers)
+def last_kernel(owner, slots, back, values, weights, cells_high, cells_low, out, markers):
+    interpolate(owner, slots, values, weights, cells_high, cells_low, markers)
     steps = step(wide(values[:, 7])[:, :, 76:77])
     spectrum = [(wide(values[:, c]) * steps).reshape(256, 128) for c in range(3)]
     field = table_right(jnp.transpose(jnp.concatenate(spectrum, 1)), back)
@@ -491,13 +501,12 @@
 
 
 def wave_tables(marks, row, col):
-    first, pair, slot = (jnp.asarray(m, jnp.int32)[:, None] for m in marks)
+    first, pair, slot = (m[:, None] for m in marks)
     lane = jnp.arange(128, dtype=jnp.int32)[None, :]
-    nyquist = jnp.arange(320, dtype=jnp.int32)[:, None] >= 256
     second = jnp.where(row == 0, 16, 32 - row)
     index_x = first + 16 * (lane // 8)
     index_y = jnp.where(pair == 0, row, second) + 32 * (lane % 8)
-    index_z = jnp.where(nyquist, N // 2, 4 * col + slot) + 0 * lane
+    index_z = jnp.where(slot < 0, N // 2, 4 * col + slot) + 0 * lane
     scale = 2.0 * jnp.pi / N
     full_sq, waves = 0.0, []
     for index in (index_x, index_y, index_z):
@@ -526,41 +535,45 @@
     y_fore, y_back, y_lanes, y_lanes_back, y_twiddle = y_tables()
     x_fore, x_extra, x_back, x_lanes, x_lanes_back, x_twiddle, marks, flips = x_tables()
     flags = jnp.stack([row == 0, col == 0]).astype(jnp.int32)
-    units, damping = wave_tables(marks, row, col)
 
     owner = owner_column.reshape(32)
-    spread_outs = (codes_of(32, 5), jax.ShapeDtypeStruct((32,), jnp.int32), [3, 1, 8, 256], [3, 1, 8, 256], [3, 16, 1, 256])
-    pushes, slots, x_first, x_last, y_last = call(
-        spread_kernel, [HBM] * 6 + [VMEM], spread_outs,
+    spread_outs = (codes_of(32, 5), jax.ShapeDtypeStruct((32,), jnp.int32))
+    pushes, slots = call(
+        spread_kernel, [HBM] * 6, spread_outs,
         [pltpu.SMEM((32,), jnp.int32), pltpu.SMEM((32,), jnp.int32), pltpu.VMEM((1, 32), BF16),
          pltpu.VMEM((1, 32), BF16), pltpu.VMEM((3, 32, 128), BF16), pltpu.VMEM((32, 3, 8, 128), BF16),
          pltpu.SMEM((32,), jnp.int32), pltpu.VMEM((32, 24, 128), F32), pltpu.VMEM((96, 128), F32),
-         pltpu.VMEM((32, 5, 8, 128), F32), pltpu.SemaphoreType.DMA((6,))], [VMEM, SMEM, VMEM, VMEM, VMEM],
-    )(owner, brick_index, stiffness.reshape(1, 32), rest_sq.reshape(1, 32), positions.transpose(1, 0, 2), weights,
-      velocity)
+         pltpu.VMEM((32, 5, 8, 128), F32), pltpu.SemaphoreType.DMA((6,))], [VMEM, SMEM],
+    )(owner, brick_index, stiffness.reshape(1, 32), rest_sq.reshape(1, 32), positions.transpose(1, 0, 2), weights)
+    x_first, x_last, y_last = call(
+        planes_kernel, [SMEM, VMEM], ([3, 1, 8, 256], [3, 1, 8, 256], [3, 16, 1, 256]))(slots, velocity)
     y_low = shifted(y_last, "col", 1)
     x_low = shifted(x_last, "row", 1)
     x_high = shifted(x_first, "row", -1)
     pushes = moved(pushes, "col")
     ids = pushes[:, 4, 0, 73:76].astype(jnp.int32)
 
-    spectrum, turned = call(advect_kernel, [VMEM] * 5, ([256, 512], [3, 32, 8, 128]))(
-        z_fore, velocity, x_low, x_high, y_low)
-    spectrum = call(gather_kernel, [SMEM, VMEM, VMEM, VMEM], codes_of(32, 5),
-                    [pltpu.VMEM((32, 8, 128), F32)] * 3)(ids, z_fore, pushes, spectrum)
+    field = call(add_up_kernel, [SMEM, VMEM], ([32, 8, 128],) * 3, [pltpu.VMEM((32, 8, 128), F32)] * 3)(ids, pushes)
+    spectrum, turned = call(star_kernel, [VMEM] * 8, (codes_of(32, 5), [3, 32, 8, 128]))(
+        z_fore, velocity, x_low, x_high, y_low, *field)
     spectrum = moved(spectrum, "col")
     spectrum = call(y_kernel, [VMEM] * 4, codes_of(16, 7))(y_fore, y_lanes, y_twiddle, spectrum)
+    marks = [jnp.asarray(m, jnp.int32) for m in marks]
+    spectrum, marks = lax.optimization_barrier((spectrum, marks))
     spectrum = moved(spectrum, "row")
+    units, damping = wave_tables(marks, row, col)
     spectrum = call(x_kernel, [SMEM] + [VMEM] * 10, codes_of(16, 7))(
         flags, x_fore, x_extra, x_back, x_lanes, x_lanes_back, x_twiddle, flips, units, damping, spectrum)
     spectrum = moved(spectrum, "row")
-    replies = call(reply_kernel, [SMEM, VMEM], codes_of(32, 5))(ids, turned)
+    cells = jax.ShapeDtypeStruct((32, 64, 128), BF16)
+    replies, cells_high, cells_low = call(reply_kernel, [SMEM, VMEM, VMEM], (codes_of(32, 5), cells, cells))(
+        ids, turned, weights)
     spectrum = call(y_back_kernel, [VMEM] * 5, codes_of(32, 8))(
         y_back, y_lanes_back, y_twiddle, spectrum, replies)
     spectrum = moved(spectrum, "col")
     new_velocity, marker_velocity = call(
-        last_kernel, [SMEM, SMEM, VMEM, VMEM, VMEM], ([3, 16, 8, 256], [3, 32, 128]))(
-        owner, slots, z_back, spectrum, weights)
+        last_kernel, [SMEM, SMEM] + [VMEM] * 5, ([3, 16, 8, 256], [3, 32, 128]))(
+        owner, slots, z_back, spectrum, weights, cells_high, cells_low)
     return new_velocity, marker_velocity.transpose(1, 0, 2)
 
 

time: 131 us -> 128 us (0.977)
  waiting for transfers between devices: 32.2 us -> 30.7 us
    unnamed x52 -> x50, local copies, waits for them, and re-layouts: 4.75 us -> 3.77 us
    pallas_call x5 -> x6, Pallas kernels: 13.2 us -> 13.7 us  [the longest x1 3.82 us: local(): call(spread_kernel, [HBM] * 6, spread_outs, [pltpu.SMEM((32,), jnp.int32)...]
  transfers between devices with their start and end apart: 7 -> 7, of which waited for: 4 -> 3; matrix products, arithmetic and copies ran while one was open for 1% -> 1% of each run, Pallas kernels for 3% -> 5%
where the time goes in v4:
time: 128 us; the launch traced here: 127 us
  starting transfers between devices  50.8 us (40%)
  waiting for transfers between devices  30.7 us (24%)
  Pallas kernels  20.3 us (16%)
  blocking collectives  19.9 us (16%)
  local copies, waits for them, and re-layouts  3.77 us (3%)
    all_to_all x4, starting transfers between devices, moved(): return lax.all_to_all(x, axis, split_axis=0, concat_axis=0, tiled=True)  35.6 us
    all_to_all x4, waiting for transfers between devices, moved(): return lax.all_to_all(x, axis, split_axis=0, concat_axis=0, tiled=True)  30.7 us
    all_to_all x1, blocking collectives, moved(): return lax.all_to_all(x, axis, split_axis=0, concat_axis=0, tiled=True)  19.9 us
    ppermute x3, starting transfers between devices, shifted(): lax.ppermute(plane, axis, [(i, (i + by) % count) for i in range(count)])  15.2 us
    pallas_call x1, Pallas kernels, local(): call(spread_kernel, [HBM] * 6, spread_outs, [pltpu.SMEM((32,), jnp.int32)...  3.82 us
    pallas_call x1, Pallas kernels, local(): call(x_kernel, [SMEM] + [VMEM] * 10, codes_of(16, 7))  3.79 us
    unnamed x50, local copies, waits for them, and re-layouts  3.77 us
    pallas_call x1, Pallas kernels, local(): call(reply_kernel, [SMEM, VMEM, VMEM], (codes_of(32, 5), cells, cells))  3.1 us
  transfers between devices with their start and end apart: 7, of which 3 were waited for; matrix products, arithmetic and copies ran while one was open for 1% of the time, Pallas kernels for 5%

profile of v4, /device:TPU:1, one launch (start us, length us, event | category | flops | bytes accessed | tf_op | source)
XLA Modules:
  0.0 127.3 jit_solution(10327421679477190976)
XLA Ops:
  0.7 0.6 copy-done.21
  1.3 0.9 copy-done
  2.3 0.7 copy-done.17
  3.0 3.8 %shard_map.239 = (s16[32,5,8,128]{3,2,1,0:T(8,128)(2,1)}, s32[32]{0:T(128)S(1)}) custom-call(s32[32]{0:T(128)S(1)} %bitcast.11, s32[32]{0:T(128)S(1)} %copy-done.19, bf16[1,32]{1,0:T(2,128)(2,1)S(1)} %bitcast.13, bf16[1,32]{1,0:T(2,128)(2,1)S(1)} %bitcast.14, bf16[3,32,128]{2,1,0:T(8,128)(2,1)S(1)} %bitcast.10, bf16[32,3,8,128]{3,2,1,0:T(8,128)(2,1)S(1)} %copy-done), custom_call_target="tpu_custom_call" | custom-call | tf_op jit(solution)/shard_map/pallas_call | solution.py:541
  6.8 10.4 %all-to-all-start = ((s16[32,5,8,128]{3,2,1,0:T(8,128)(2,1)}), s16[32,5,8,128]{3,2,1,0:T(8,128)(2,1)S(1)}, u32[]{:S(2)}, u32[]{:S(2)}) async-start(s16[32,5,8,128]{3,2,1,0:T(8,128)(2,1)} %get-tuple-element.25), calls=%async_computation | async-start | bytes 655360 | tf_op jit(solution)/shard_map/all_to_all | solution.py:524
  17.9 2.1 %collective-permute-start = (f32[3,1,8,256]{3,2,1,0:T(8,128)S(1)}, f32[3,1,8,256]{3,2,1,0:T(8,128)S(1)}, u32[]{:S(2)}, u32[]{:S(2)}) collective-permute-start(f32[3,1,8,256]{3,2,1,0:T(8,128)S(1)} %get-tuple-element.22), channel_id=1, source_target_pairs={{0,32},{32,64},{64,96},{96,128},{128,160},{160,192},{192,224},{224... | collective-permute-start | bytes 73736 | tf_op jit(solution)/shard_map/ppermute | solution.py:529
  19.9 9.3 %collective-permute-start.1 = (f32[3,1,8,256]{3,2,1,0:T(8,128)S(1)}, f32[3,1,8,256]{3,2,1,0:T(8,128)S(1)}, u32[]{:S(2)}, u32[]{:S(2)}) collective-permute-start(f32[3,1,8,256]{3,2,1,0:T(8,128)S(1)} %get-tuple-element.23), channel_id=1, source_target_pairs={{0,480},{32,0},{64,32},{96,64},{128,96},{160,128},{192,160},{224,1... | collective-permute-start | bytes 73736 | tf_op jit(solution)/shard_map/ppermute | solution.py:529
  29.2 3.8 %collective-permute-start.2 = (f32[3,16,1,256]{3,2,1,0:T(1,128)S(1)}, f32[3,16,1,256]{3,2,1,0:T(1,128)S(1)}, u32[]{:S(2)}, u32[]{:S(2)}) collective-permute-start(f32[3,16,1,256]{3,2,1,0:T(1,128)S(1)} %get-tuple-element.24), channel_id=1, source_target_pairs={{0,1},{1,2},{2,3},{3,4},{4,5},{5,6},{6,7},{7,8},{8,9},{9,10},{10,1... | collective-permute-start | bytes 147464 | tf_op jit(solution)/shard_map/ppermute | solution.py:529
  33.2 2.3 %shard_map.241 = (f32[32,8,128]{2,1,0:T(8,128)S(1)}, f32[32,8,128]{2,1,0:T(8,128)S(1)}, f32[32,8,128]{2,1,0:T(8,128)S(1)}) custom-call(s32[32,3]{1,0:T(8,128)S(1)} %bitcast.8, s16[32,5,8,128]{3,2,1,0:T(8,128)(2,1)S(1)} %all-to-all-done.pushes), custom_call_target="tpu_custom_call" | custom-call | tf_op jit(solution)/shard_map/pallas_call | solution.py:556
  35.5 1.7 %shard_map.242 = (s16[32,5,8,128]{3,2,1,0:T(8,128)(2,1)}, f32[3,32,8,128]{3,2,1,0:T(8,128)S(1)}) custom-call(bf16[2,256,256]{2,1,0:T(8,128)(2,1)S(1)} %copy-done.8, f32[3,16,8,256]{3,2,1,0:T(8,128)S(1)} %copy-done.2, f32[3,1,8,256]{3,2,1,0:T(8,128)S(1)} %collective-permute-done.x_low, f32[3,1,8,256]{3,2,1,0:T(8,128)S(1)} %collective-permute-done.1.x_high, ...), custom_call_target="tpu_custom_call" | custom-call | tf_op jit(solution)/shard_map/pallas_call | solution.py:557
  37.2 6.9 %all-to-all-start.1 = ((s16[32,5,8,128]{3,2,1,0:T(8,128)(2,1)}), s16[32,5,8,128]{3,2,1,0:T(8,128)(2,1)S(1)}, u32[]{:S(2)}, u32[]{:S(2)}) async-start(s16[32,5,8,128]{3,2,1,0:T(8,128)(2,1)} %get-tuple-element.29), calls=%async_computation.1 | async-start | bytes 655360 | tf_op jit(solution)/shard_map/all_to_all | solution.py:524
  44.3 9.4 %all-to-all-done.1.values = s16[32,5,8,128]{3,2,1,0:T(8,128)(2,1)S(1)} async-done(((s16[32,5,8,128]{3,2,1,0:T(8,128)(2,1)}), s16[32,5,8,128]{3,2,1,0:T(8,128)(2,1)S(1)}, u32[]{:S(2)}, u32[]{:S(2)}) %all-to-all-start.1) | async-done | bytes 327712 | tf_op jit(solution)/shard_map/all_to_all | solution.py:524
  53.7 1.6 %shard_map.243 = s16[16,7,8,128]{3,2,1,0:T(8,128)(2,1)} custom-call(bf16[2,256,256]{2,1,0:T(8,128)(2,1)S(1)} %copy-done.7, bf16[2,128,256]{2,1,0:T(8,128)(2,1)S(1)} %copy-done.11, f32[2,32,1,128]{3,2,1,0:T(1,128)S(1)} %copy-done.12, s16[32,5,8,128]{3,2,1,0:T(8,128)(2,1)S(1)} %all-to-all-done.1.values), custom_call_target="tpu_custom_call" | custom-call | tf_op jit(solution)/shard_map/pallas_call | solution.py:560
  55.3 8.8 %all-to-all-start.2 = ((s16[16,7,8,128]{3,2,1,0:T(8,128)(2,1)}), s16[16,7,8,128]{3,2,1,0:T(8,128)(2,1)S(1)}, u32[]{:S(2)}, u32[]{:S(2)}) async-start(s16[16,7,8,128]{3,2,1,0:T(8,128)(2,1)} %shard_map.243), calls=%async_computation.2 | async-start | bytes 458752 | tf_op jit(solution)/shard_map/all_to_all | solution.py:524
  64.1 0.7 copy-done.24
  64.8 0.7 copy-done.22
  66.2 11.3 %all-to-all-done.2.values = s16[16,7,8,128]{3,2,1,0:T(8,128)(2,1)S(1)} async-done(((s16[16,7,8,128]{3,2,1,0:T(8,128)(2,1)}), s16[16,7,8,128]{3,2,1,0:T(8,128)(2,1)S(1)}, u32[]{:S(2)}, u32[]{:S(2)}) %all-to-all-start.2) | async-done | bytes 229408 | tf_op jit(solution)/shard_map/all_to_all | solution.py:524
  77.6 3.8 %shard_map.244 = s16[16,7,8,128]{3,2,1,0:T(8,128)(2,1)} custom-call(s32[2]{0:T(128)S(1)} %add_convert_fusion.flags, bf16[2,256,256]{2,1,0:T(8,128)(2,1)S(1)} %copy-done.9, bf16[2,64,256]{2,1,0:T(8,128)(2,1)S(1)} %copy-done.16, bf16[2,256,320]{2,1,0:T(8,128)(2,1)S(1)} %copy-done.3, bf16[2,128,256]{2,1,0:T(8,128)(2,1)S(1)} %copy-done.14, ...), custom_call_target="tpu_custom_call" | custom-call | tf_op jit(solution)/shard_map/pallas_call | solution.py:565
  81.4 9.5 %all-to-all-start.3 = ((s16[16,7,8,128]{3,2,1,0:T(8,128)(2,1)}), s16[16,7,8,128]{3,2,1,0:T(8,128)(2,1)S(1)}, u32[]{:S(2)}, u32[]{:S(2)}) async-start(s16[16,7,8,128]{3,2,1,0:T(8,128)(2,1)} %shard_map.244), calls=%async_computation.3 | async-start | bytes 458752 | tf_op jit(solution)/shard_map/all_to_all | solution.py:524
  90.9 3.1 %shard_map.245 = (s16[32,5,8,128]{3,2,1,0:T(8,128)(2,1)S(1)}, bf16[32,64,128]{2,1,0:T(8,128)(2,1)S(1)}, bf16[32,64,128]{2,1,0:T(8,128)(2,1)S(1)}) custom-call(s32[32,3]{1,0:T(8,128)S(1)} %bitcast.9, f32[3,32,8,128]{3,2,1,0:T(8,128)S(1)} %get-tuple-element.34.turned, bf16[32,3,8,128]{3,2,1,0:T(8,128)(2,1)S(1)} %copy-done.1), custom_call_target="tpu_custom_call" | custom-call | tf_op jit(solution)/shard_map/pallas_call | solution.py:569
  94.0 10.0 %all-to-all-done.3.values = s16[16,7,8,128]{3,2,1,0:T(8,128)(2,1)S(1)} async-done(((s16[16,7,8,128]{3,2,1,0:T(8,128)(2,1)}), s16[16,7,8,128]{3,2,1,0:T(8,128)(2,1)S(1)}, u32[]{:S(2)}, u32[]{:S(2)}) %all-to-all-start.3) | async-done | bytes 229408 | tf_op jit(solution)/shard_map/all_to_all | solution.py:524
  104.0 1.2 shard_map.246
  105.3 19.9 %all_to_all.25.values = s16[32,8,8,128]{3,2,1,0:T(8,128)(2,1)S(1)} all-to-all(s16[32,8,8,128]{3,2,1,0:T(8,128)(2,1)S(1)} %shard_map.246), channel_id=1, replica_groups=mesh['row'=16,'col'=32] {'col'}, dimensions={0} | all-to-all | bytes 1048576 | tf_op jit(solution)/shard_map/all_to_all | solution.py:524
  125.1 2.2 %shard_map.247 = (f32[3,16,8,256]{3,2,1,0:T(8,128)}, f32[3,32,128]{2,1,0:T(8,128)}) custom-call(s32[32]{0:T(128)S(1)} %bitcast.12, s32[32]{0:T(128)S(1)} %get-tuple-element.21._.slots, bf16[2,256,256]{2,1,0:T(8,128)(2,1)S(1)} %copy-done.5, s16[32,8,8,128]{3,2,1,0:T(8,128)(2,1)S(1)} %all_to_all.25.values, bf16[32,3,8,128]{3,2,1,0:T(8,128)(2,1)S(1)} %copy-done.1, ...), custom_call_target="tpu_custom_call" | custom-call | tf_op jit(solution)/shard_map/pallas_call | solution.py:574
  (59 shorter events, 1.6 us)
Async XLA Ops:
  3.0 14.3 %copy-start.2 = (f32[3,16,8,256]{3,2,1,0:T(8,128)S(1)}, f32[3,16,8,256]{3,2,1,0:T(8,128)}, u32[]{:S(2)}) copy-start(f32[3,16,8,256]{3,2,1,0:T(8,128)} %velocity.3) | copy-start | bytes 1179652
  6.8 26.2 %all-to-all-start = ((s16[32,5,8,128]{3,2,1,0:T(8,128)(2,1)}), s16[32,5,8,128]{3,2,1,0:T(8,128)(2,1)S(1)}, u32[]{:S(2)}, u32[]{:S(2)}) async-start(s16[32,5,8,128]{3,2,1,0:T(8,128)(2,1)} %get-tuple-element.25), calls=%async_computation | async-start | bytes 655360 | tf_op jit(solution)/shard_map/all_to_all | solution.py:524
  17.8 17.6 %copy-start.8 = (bf16[2,256,256]{2,1,0:T(8,128)(2,1)S(1)}, bf16[2,256,256]{2,1,0:T(8,128)(2,1)}, u32[]{:S(2)}) copy-start(bf16[2,256,256]{2,1,0:T(8,128)(2,1)} %constant.106.clone.table) | copy-start | bytes 786436
  17.9 17.6 %collective-permute-start = (f32[3,1,8,256]{3,2,1,0:T(8,128)S(1)}, f32[3,1,8,256]{3,2,1,0:T(8,128)S(1)}, u32[]{:S(2)}, u32[]{:S(2)}) collective-permute-start(f32[3,1,8,256]{3,2,1,0:T(8,128)S(1)} %get-tuple-element.22), channel_id=1, source_target_pairs={{0,32},{32,64},{64,96},{96,128},{128,160},{160,192},{192,224},{224... | collective-permute-start | bytes 73736 | tf_op jit(solution)/shard_map/ppermute | solution.py:529
  19.9 15.6 %collective-permute-start.1 = (f32[3,1,8,256]{3,2,1,0:T(8,128)S(1)}, f32[3,1,8,256]{3,2,1,0:T(8,128)S(1)}, u32[]{:S(2)}, u32[]{:S(2)}) collective-permute-start(f32[3,1,8,256]{3,2,1,0:T(8,128)S(1)} %get-tuple-element.23), channel_id=1, source_target_pairs={{0,480},{32,0},{64,32},{96,64},{128,96},{160,128},{192,160},{224,1... | collective-permute-start | bytes 73736 | tf_op jit(solution)/shard_map/ppermute | solution.py:529
  29.2 6.3 %collective-permute-start.2 = (f32[3,16,1,256]{3,2,1,0:T(1,128)S(1)}, f32[3,16,1,256]{3,2,1,0:T(1,128)S(1)}, u32[]{:S(2)}, u32[]{:S(2)}) collective-permute-start(f32[3,16,1,256]{3,2,1,0:T(1,128)S(1)} %get-tuple-element.24), channel_id=1, source_target_pairs={{0,1},{1,2},{2,3},{3,4},{4,5},{5,6},{6,7},{7,8},{8,9},{9,10},{10,1... | collective-permute-start | bytes 147464 | tf_op jit(solution)/shard_map/ppermute | solution.py:529
  37.2 16.5 %copy-start.7 = (bf16[2,256,256]{2,1,0:T(8,128)(2,1)S(1)}, bf16[2,256,256]{2,1,0:T(8,128)(2,1)}, u32[]{:S(2)}) copy-start(bf16[2,256,256]{2,1,0:T(8,128)(2,1)} %constant.107.clone.left) | copy-start | bytes 786436
  37.2 16.5 %copy-start.11 = (bf16[2,128,256]{2,1,0:T(8,128)(2,1)S(1)}, bf16[2,128,256]{2,1,0:T(8,128)(2,1)}, u32[]{:S(2)}) copy-start(bf16[2,128,256]{2,1,0:T(8,128)(2,1)} %constant.108.clone.lanes) | copy-start | bytes 393220
  37.2 16.5 %copy-start.12 = (f32[2,32,1,128]{3,2,1,0:T(1,128)S(1)}, f32[2,32,1,128]{3,2,1,0:T(1,128)}, u32[]{:S(2)}) copy-start(f32[2,32,1,128]{3,2,1,0:T(1,128)} %constant.109.clone.twiddle) | copy-start | bytes 98308
  37.2 16.5 %all-to-all-start.1 = ((s16[32,5,8,128]{3,2,1,0:T(8,128)(2,1)}), s16[32,5,8,128]{3,2,1,0:T(8,128)(2,1)S(1)}, u32[]{:S(2)}, u32[]{:S(2)}) async-start(s16[32,5,8,128]{3,2,1,0:T(8,128)(2,1)} %get-tuple-element.29), calls=%async_computation.1 | async-start | bytes 655360 | tf_op jit(solution)/shard_map/all_to_all | solution.py:524
  55.3 8.8 %copy-start.23 = (s32[320]{0:T(512)S(1)}, s32[320]{0:T(512)}, u32[]{:S(2)}) copy-start(s32[320]{0:T(512)} %constant.112.clone) | copy-start | bytes 3844
  55.3 22.2 %all-to-all-start.2 = ((s16[16,7,8,128]{3,2,1,0:T(8,128)(2,1)}), s16[16,7,8,128]{3,2,1,0:T(8,128)(2,1)S(1)}, u32[]{:S(2)}, u32[]{:S(2)}) async-start(s16[16,7,8,128]{3,2,1,0:T(8,128)(2,1)} %shard_map.243), calls=%async_computation.2 | async-start | bytes 458752 | tf_op jit(solution)/shard_map/all_to_all | solution.py:524
  65.5 12.0 %copy-start.14 = (bf16[2,128,256]{2,1,0:T(8,128)(2,1)S(1)}, bf16[2,128,256]{2,1,0:T(8,128)(2,1)}, u32[]{:S(2)}) copy-start(bf16[2,128,256]{2,1,0:T(8,128)(2,1)} %constant.116.clone.lanes) | copy-start | bytes 393220
  65.5 12.0 %copy-start.15 = (bf16[128,256]{1,0:T(8,128)(2,1)S(1)}, bf16[128,256]{1,0:T(8,128)(2,1)}, u32[]{:S(2)}) copy-start(bf16[128,256]{1,0:T(8,128)(2,1)} %constant.119.clone.flips) | copy-start | bytes 196612
  65.5 12.0 %copy-start.16 = (bf16[2,64,256]{2,1,0:T(8,128)(2,1)S(1)}, bf16[2,64,256]{2,1,0:T(8,128)(2,1)}, u32[]{:S(2)}) copy-start(bf16[2,64,256]{2,1,0:T(8,128)(2,1)} %constant.114.clone.left_extra) | copy-start | bytes 196612
  65.8 11.7 %copy-start.3 = (bf16[2,256,320]{2,1,0:T(8,128)(2,1)S(1)}, bf16[2,256,320]{2,1,0:T(8,128)(2,1)}, u32[]{:S(2)}) copy-start(bf16[2,256,320]{2,1,0:T(8,128)(2,1)} %constant.115.clone.back) | copy-start | bytes 983044
  65.8 11.7 %copy-start.4 = (f32[2,40,8,128]{3,2,1,0:T(8,128)S(1)}, f32[2,40,8,128]{3,2,1,0:T(8,128)}, u32[]{:S(2)}) copy-start(f32[2,40,8,128]{3,2,1,0:T(8,128)} %constant.118.clone.twiddle) | copy-start | bytes 983044
  65.9 11.7 %copy-start.9 = (bf16[2,256,256]{2,1,0:T(8,128)(2,1)S(1)}, bf16[2,256,256]{2,1,0:T(8,128)(2,1)}, u32[]{:S(2)}) copy-start(bf16[2,256,256]{2,1,0:T(8,128)(2,1)} %constant.113.clone.left) | copy-start | bytes 786436
  65.9 11.6 %copy-start.13 = (bf16[2,128,256]{2,1,0:T(8,128)(2,1)S(1)}, bf16[2,128,256]{2,1,0:T(8,128)(2,1)}, u32[]{:S(2)}) copy-start(bf16[2,128,256]{2,1,0:T(8,128)(2,1)} %constant.117.clone.lanes_back) | copy-start | bytes 393220
  81.4 9.5 %copy-start.1 = (bf16[32,3,8,128]{3,2,1,0:T(8,128)(2,1)S(1)}, bf16[32,3,8,128]{3,2,1,0:T(8,128)(2,1)}, u32[]{:S(2)}) copy-start(bf16[32,3,8,128]{3,2,1,0:T(8,128)(2,1)} %weights.3) | copy-start | bytes 589828
  81.4 22.7 %all-to-all-start.3 = ((s16[16,7,8,128]{3,2,1,0:T(8,128)(2,1)}), s16[16,7,8,128]{3,2,1,0:T(8,128)(2,1)S(1)}, u32[]{:S(2)}, u32[]{:S(2)}) async-start(s16[16,7,8,128]{3,2,1,0:T(8,128)(2,1)} %shard_map.244), calls=%async_computation.3 | async-start | bytes 458752 | tf_op jit(solution)/shard_map/all_to_all | solution.py:524
  90.9 13.1 %copy-start.6 = (bf16[2,256,256]{2,1,0:T(8,128)(2,1)S(1)}, bf16[2,256,256]{2,1,0:T(8,128)(2,1)}, u32[]{:S(2)}) copy-start(bf16[2,256,256]{2,1,0:T(8,128)(2,1)} %constant.120.clone.back) | copy-start | bytes 786436
  90.9 13.1 %copy-start.10 = (bf16[2,128,256]{2,1,0:T(8,128)(2,1)S(1)}, bf16[2,128,256]{2,1,0:T(8,128)(2,1)}, u32[]{:S(2)}) copy-start(bf16[2,128,256]{2,1,0:T(8,128)(2,1)} %constant.121.clone.lanes) | copy-start | bytes 393220
  105.2 19.9 %copy-start.5 = (bf16[2,256,256]{2,1,0:T(8,128)(2,1)S(1)}, bf16[2,256,256]{2,1,0:T(8,128)(2,1)}, u32[]{:S(2)}) copy-start(bf16[2,256,256]{2,1,0:T(8,128)(2,1)} %constant.122.clone.back) | copy-start | bytes 786436
  (8 other events, 5.7 us)

commit v5 on v4

--- a/solution.py
+++ b/solution.py
@@ -274,7 +274,7 @@
     half = lane_half()
     lane = lax.broadcasted_iota(jnp.int32, (8, 128), 1)
 
-    @pl.loop(0, 32)
+    @pl.loop(0, 32, unroll=4)
     def _(n):
         d = owner[n]
         s = count[d]
@@ -283,9 +283,10 @@
         last = jnp.where(lane == 73 + s, brick[n].astype(F32), 0.0)
         for c in range(3):
             tile, side = tile_place(s, c)
-            total[d, tile] += jnp.where(half == side, cubes[n, 8 * c:8 * c + 8, :], 0.0)
+            pltpu.store(total.at[d, tile], cubes[n, 8 * c:8 * c + 8, :], mask=half == side)
             last = jnp.where(lane == 64 + 3 * s + c, marks[pl.ds(3 * n + c, 1), :], last)
-        total[d, 4] += last
+        own = (lane == 73 + s) | ((lane >= 64 + 3 * s) & (lane < 67 + 3 * s))
+        pltpu.store(total.at[d, 4], last, mask=own)
 
     out[...] = narrow(total[...])
 
@@ -304,7 +305,7 @@
             field[...] = jnp.zeros(field.shape, F32)
     half = lane_half()
 
-    @pl.loop(0, 16, unroll=2)
+    @pl.loop(0, 16, unroll=4)
     def _(pair):
         for odd in range(2):
             src = 2 * pair + odd
@@ -349,9 +350,10 @@
     total = spectrum[:, :384] + table_left(table, DT_STEP * field)
     total = jnp.concatenate([stacked(total), spectrum[:, 384:]], 0)
     codes, exponent = encoded(total.reshape(4, 32, 8, 128))
-    for t in range(4):
+    for t in range(3):
         out[:, t] = narrow(codes[t])
-    out[:, 4] = narrow(exponent)
+    lane = lax.broadcasted_iota(jnp.int32, (1, 8, 128), 2)
+    out[:, 3] = narrow(jnp.where(lane == 3, exponent, codes[3]))
 
 
 def reply_kernel(ids, turned, weights, out, cells_high, cells_low):
@@ -406,8 +408,9 @@
 
 
 def y_kernel(left, lanes, twiddle, values, out):
-    steps = step(wide(values[:, 4]))
-    beyond = wide(values[:, 3]) * steps
+    beyond = wide(values[:, 3])
+    steps = jnp.broadcast_to(step(beyond[:, :, 3:4]), (32, 8, 128))
+    beyond = beyond * steps
     beyond = jnp.concatenate([beyond[1:], beyond[:1]], 0)
     last = lax.broadcasted_iota(jnp.int32, (1, 8, 128), 2) % 8 == 7
     spectrum = []
@@ -544,7 +547,8 @@
          pltpu.VMEM((1, 32), BF16), pltpu.VMEM((3, 32, 128), BF16), pltpu.VMEM((32, 3, 8, 128), BF16),
          pltpu.SMEM((32,), jnp.int32), pltpu.VMEM((32, 24, 128), F32), pltpu.VMEM((96, 128), F32),
          pltpu.VMEM((32, 5, 8, 128), F32), pltpu.SemaphoreType.DMA((6,))], [VMEM, SMEM],
-    )(owner, brick_index, stiffness.reshape(1, 32), rest_sq.reshape(1, 32), positions.transpose(1, 0, 2), weights)
+    )(*(pltpu.with_memory_space_constraint(x, pltpu.HBM) for x in (
+        owner, brick_index, stiffness.reshape(1, 32), rest_sq.reshape(1, 32), positions.transpose(1, 0, 2), weights)))
     x_first, x_last, y_last = call(
         planes_kernel, [SMEM, VMEM], ([3, 1, 8, 256], [3, 1, 8, 256], [3, 16, 1, 256]))(slots, velocity)
     y_low = shifted(y_last, "col", 1)
@@ -554,7 +558,7 @@
     ids = pushes[:, 4, 0, 73:76].astype(jnp.int32)
 
     field = call(add_up_kernel, [SMEM, VMEM], ([32, 8, 128],) * 3, [pltpu.VMEM((32, 8, 128), F32)] * 3)(ids, pushes)
-    spectrum, turned = call(star_kernel, [VMEM] * 8, (codes_of(32, 5), [3, 32, 8, 128]))(
+    spectrum, turned = call(star_kernel, [VMEM] * 8, (codes_of(32, 4), [3, 32, 8, 128]))(
         z_fore, velocity, x_low, x_high, y_low, *field)
     spectrum = moved(spectrum, "col")
     spectrum = call(y_kernel, [VMEM] * 4, codes_of(16, 7))(y_fore, y_lanes, y_twiddle, spectrum)

time: 128 us -> 126 us (0.984)
  local copies, waits for them, and re-layouts: 3.77 us -> 2.08 us
    unnamed x50 -> x40, local copies, waits for them, and re-layouts: 3.77 us -> 2.08 us
where the time goes in v5:
time: 126 us; the launch traced here: 125 us
  starting transfers between devices  51 us (40%)
  waiting for transfers between devices  30.3 us (24%)
  Pallas kernels  19.9 us (16%)
  blocking collectives  19.9 us (16%)
  local copies, waits for them, and re-layouts  2.08 us (2%)
    all_to_all x4, starting transfers between devices, moved(): return lax.all_to_all(x, axis, split_axis=0, concat_axis=0, tiled=True)  35.9 us
    all_to_all x4, waiting for transfers between devices, moved(): return lax.all_to_all(x, axis, split_axis=0, concat_axis=0, tiled=True)  30.3 us
    all_to_all x1, blocking collectives, moved(): return lax.all_to_all(x, axis, split_axis=0, concat_axis=0, tiled=True)  19.9 us
    ppermute x3, starting transfers between devices, shifted(): lax.ppermute(plane, axis, [(i, (i + by) % count) for i in range(count)])  15.2 us
    pallas_call x1, Pallas kernels, local(): call(x_kernel, [SMEM] + [VMEM] * 10, codes_of(16, 7))  3.79 us
    pallas_call x1, Pallas kernels, local(): call(spread_kernel, [HBM] * 6, spread_outs, [pltpu.SMEM((32,), jnp.int32)...  3.64 us
    pallas_call x1, Pallas kernels, local(): call(reply_kernel, [SMEM, VMEM, VMEM], (codes_of(32, 5), cells, cells))  3.1 us
  transfers between devices with their start and end apart: 7, of which 3 were waited for; matrix products, arithmetic and copies ran while one was open for 1% of the time, Pallas kernels for 5%

profile of v5, /device:TPU:1, one launch (start us, length us, event | category | flops | bytes accessed | tf_op | source)
XLA Modules:
  0.0 125.0 jit_solution(929301496850409564)
XLA Ops:
  0.6 3.6 %shard_map.239 = (s16[32,5,8,128]{3,2,1,0:T(8,128)(2,1)}, s32[32]{0:T(128)S(1)}) custom-call(s32[32]{0:T(128)} %bitcast.10, s32[32]{0:T(128)} %brick_in.1, bf16[1,32]{1,0:T(2,128)(2,1)} %bitcast.13, bf16[1,32]{1,0:T(2,128)(2,1)} %bitcast.14, bf16[3,32,128]{2,1,0:T(8,128)(2,1)} %bitcast.12, bf16[32,3,8,128]{3,2,1,0:T(8,128)(2,1)} %weights.3), custom_call_target="tpu_custom_call" | custom-call | tf_op jit(solution)/shard_map/pallas_call | solution.py:544
  4.3 10.4 %all-to-all-start = ((s16[32,5,8,128]{3,2,1,0:T(8,128)(2,1)}), s16[32,5,8,128]{3,2,1,0:T(8,128)(2,1)S(1)}, u32[]{:S(2)}, u32[]{:S(2)}) async-start(s16[32,5,8,128]{3,2,1,0:T(8,128)(2,1)} %get-tuple-element.25), calls=%async_computation | async-start | bytes 655360 | tf_op jit(solution)/shard_map/all_to_all | solution.py:527
  14.7 0.6 shard_map.240
  15.3 2.1 %collective-permute-start = (f32[3,1,8,256]{3,2,1,0:T(8,128)S(1)}, f32[3,1,8,256]{3,2,1,0:T(8,128)S(1)}, u32[]{:S(2)}, u32[]{:S(2)}) collective-permute-start(f32[3,1,8,256]{3,2,1,0:T(8,128)S(1)} %get-tuple-element.22), channel_id=1, source_target_pairs={{0,32},{32,64},{64,96},{96,128},{128,160},{160,192},{192,224},{224... | collective-permute-start | bytes 73736 | tf_op jit(solution)/shard_map/ppermute | solution.py:532
  17.4 9.3 %collective-permute-start.1 = (f32[3,1,8,256]{3,2,1,0:T(8,128)S(1)}, f32[3,1,8,256]{3,2,1,0:T(8,128)S(1)}, u32[]{:S(2)}, u32[]{:S(2)}) collective-permute-start(f32[3,1,8,256]{3,2,1,0:T(8,128)S(1)} %get-tuple-element.23), channel_id=1, source_target_pairs={{0,480},{32,0},{64,32},{96,64},{128,96},{160,128},{192,160},{224,1... | collective-permute-start | bytes 73736 | tf_op jit(solution)/shard_map/ppermute | solution.py:532
  26.7 3.8 %collective-permute-start.2 = (f32[3,16,1,256]{3,2,1,0:T(1,128)S(1)}, f32[3,16,1,256]{3,2,1,0:T(1,128)S(1)}, u32[]{:S(2)}, u32[]{:S(2)}) collective-permute-start(f32[3,16,1,256]{3,2,1,0:T(1,128)S(1)} %get-tuple-element.24), channel_id=1, source_target_pairs={{0,1},{1,2},{2,3},{3,4},{4,5},{5,6},{6,7},{7,8},{8,9},{9,10},{10,1... | collective-permute-start | bytes 147464 | tf_op jit(solution)/shard_map/ppermute | solution.py:532
  30.6 2.0 %shard_map.241 = (f32[32,8,128]{2,1,0:T(8,128)S(1)}, f32[32,8,128]{2,1,0:T(8,128)S(1)}, f32[32,8,128]{2,1,0:T(8,128)S(1)}) custom-call(s32[32,3]{1,0:T(8,128)S(1)} %bitcast.8, s16[32,5,8,128]{3,2,1,0:T(8,128)(2,1)S(1)} %all-to-all-done.pushes), custom_call_target="tpu_custom_call" | custom-call | tf_op jit(solution)/shard_map/pallas_call | solution.py:560
  32.7 1.7 %shard_map.242 = (s16[32,4,8,128]{3,2,1,0:T(8,128)(2,1)}, f32[3,32,8,128]{3,2,1,0:T(8,128)S(1)}) custom-call(bf16[2,256,256]{2,1,0:T(8,128)(2,1)S(1)} %copy-done.7, f32[3,16,8,256]{3,2,1,0:T(8,128)S(1)} %copy-done.1, f32[3,1,8,256]{3,2,1,0:T(8,128)S(1)} %collective-permute-done.x_low, f32[3,1,8,256]{3,2,1,0:T(8,128)S(1)} %collective-permute-done.1.x_high, ...), custom_call_target="tpu_custom_call" | custom-call | tf_op jit(solution)/shard_map/pallas_call | solution.py:561
  34.4 7.2 %all-to-all-start.1 = ((s16[32,4,8,128]{3,2,1,0:T(8,128)(2,1)}), s16[32,4,8,128]{3,2,1,0:T(8,128)(2,1)S(1)}, u32[]{:S(2)}, u32[]{:S(2)}) async-start(s16[32,4,8,128]{3,2,1,0:T(8,128)(2,1)} %get-tuple-element.29), calls=%async_computation.1 | async-start | bytes 524288 | tf_op jit(solution)/shard_map/all_to_all | solution.py:527
  41.7 8.8 %all-to-all-done.1.values = s16[32,4,8,128]{3,2,1,0:T(8,128)(2,1)S(1)} async-done(((s16[32,4,8,128]{3,2,1,0:T(8,128)(2,1)}), s16[32,4,8,128]{3,2,1,0:T(8,128)(2,1)S(1)}, u32[]{:S(2)}, u32[]{:S(2)}) %all-to-all-start.1) | async-done | bytes 262176 | tf_op jit(solution)/shard_map/all_to_all | solution.py:527
  50.5 1.7 %shard_map.243 = s16[16,7,8,128]{3,2,1,0:T(8,128)(2,1)} custom-call(bf16[2,256,256]{2,1,0:T(8,128)(2,1)S(1)} %copy-done.5, bf16[2,128,256]{2,1,0:T(8,128)(2,1)S(1)} %copy-done.10, f32[2,32,1,128]{3,2,1,0:T(1,128)S(1)} %copy-done.11, s16[32,4,8,128]{3,2,1,0:T(8,128)(2,1)S(1)} %all-to-all-done.1.values), custom_call_target="tpu_custom_call" | custom-call | tf_op jit(solution)/shard_map/pallas_call | solution.py:564
  52.2 8.8 %all-to-all-start.2 = ((s16[16,7,8,128]{3,2,1,0:T(8,128)(2,1)}), s16[16,7,8,128]{3,2,1,0:T(8,128)(2,1)S(1)}, u32[]{:S(2)}, u32[]{:S(2)}) async-start(s16[16,7,8,128]{3,2,1,0:T(8,128)(2,1)} %shard_map.243), calls=%async_computation.2 | async-start | bytes 458752 | tf_op jit(solution)/shard_map/all_to_all | solution.py:527
  61.0 0.7 copy-done.19
  61.7 0.7 copy-done.17
  62.4 0.3 fusion.22
  63.1 11.4 %all-to-all-done.2.values = s16[16,7,8,128]{3,2,1,0:T(8,128)(2,1)S(1)} async-done(((s16[16,7,8,128]{3,2,1,0:T(8,128)(2,1)}), s16[16,7,8,128]{3,2,1,0:T(8,128)(2,1)S(1)}, u32[]{:S(2)}, u32[]{:S(2)}) %all-to-all-start.2) | async-done | bytes 229408 | tf_op jit(solution)/shard_map/all_to_all | solution.py:527
  74.6 3.8 %shard_map.244 = s16[16,7,8,128]{3,2,1,0:T(8,128)(2,1)} custom-call(s32[2]{0:T(128)S(1)} %add_convert_fusion.flags, bf16[2,256,256]{2,1,0:T(8,128)(2,1)S(1)} %copy-done.8, bf16[2,64,256]{2,1,0:T(8,128)(2,1)S(1)} %copy-done.15, bf16[2,256,320]{2,1,0:T(8,128)(2,1)S(1)} %copy-done.2, bf16[2,128,256]{2,1,0:T(8,128)(2,1)S(1)} %copy-done.13, ...), custom_call_target="tpu_custom_call" | custom-call | tf_op jit(solution)/shard_map/pallas_call | solution.py:569
  78.3 9.4 %all-to-all-start.3 = ((s16[16,7,8,128]{3,2,1,0:T(8,128)(2,1)}), s16[16,7,8,128]{3,2,1,0:T(8,128)(2,1)S(1)}, u32[]{:S(2)}, u32[]{:S(2)}) async-start(s16[16,7,8,128]{3,2,1,0:T(8,128)(2,1)} %shard_map.244), calls=%async_computation.3 | async-start | bytes 458752 | tf_op jit(solution)/shard_map/all_to_all | solution.py:527
  87.8 3.1 %shard_map.245 = (s16[32,5,8,128]{3,2,1,0:T(8,128)(2,1)S(1)}, bf16[32,64,128]{2,1,0:T(8,128)(2,1)S(1)}, bf16[32,64,128]{2,1,0:T(8,128)(2,1)S(1)}) custom-call(s32[32,3]{1,0:T(8,128)S(1)} %bitcast.9, f32[3,32,8,128]{3,2,1,0:T(8,128)S(1)} %get-tuple-element.34.turned, bf16[32,3,8,128]{3,2,1,0:T(8,128)(2,1)S(1)} %copy-done), custom_call_target="tpu_custom_call" | custom-call | tf_op jit(solution)/shard_map/pallas_call | solution.py:573
  90.9 10.0 %all-to-all-done.3.values = s16[16,7,8,128]{3,2,1,0:T(8,128)(2,1)S(1)} async-done(((s16[16,7,8,128]{3,2,1,0:T(8,128)(2,1)}), s16[16,7,8,128]{3,2,1,0:T(8,128)(2,1)S(1)}, u32[]{:S(2)}, u32[]{:S(2)}) %all-to-all-start.3) | async-done | bytes 229408 | tf_op jit(solution)/shard_map/all_to_all | solution.py:527
  101.0 1.2 shard_map.246
  102.2 19.9 %all_to_all.25.values = s16[32,8,8,128]{3,2,1,0:T(8,128)(2,1)S(1)} all-to-all(s16[32,8,8,128]{3,2,1,0:T(8,128)(2,1)S(1)} %shard_map.246), channel_id=1, replica_groups=mesh['row'=16,'col'=32] {'col'}, dimensions={0} | all-to-all | bytes 1048576 | tf_op jit(solution)/shard_map/all_to_all | solution.py:527
  122.1 0.7 copy-done.16
  122.8 2.2 %shard_map.247 = (f32[3,16,8,256]{3,2,1,0:T(8,128)}, f32[3,32,128]{2,1,0:T(8,128)}) custom-call(s32[32]{0:T(128)S(1)} %bitcast.11, s32[32]{0:T(128)S(1)} %get-tuple-element.21._.slots, bf16[2,256,256]{2,1,0:T(8,128)(2,1)S(1)} %copy-done.4, s16[32,8,8,128]{3,2,1,0:T(8,128)(2,1)S(1)} %all_to_all.25.values, bf16[32,3,8,128]{3,2,1,0:T(8,128)(2,1)S(1)} %copy-done, ...), custom_call_target="tpu_custom_call" | custom-call | tf_op jit(solution)/shard_map/pallas_call | solution.py:578
  (49 shorter events, 0.6 us)
Async XLA Ops:
  0.6 14.1 %copy-start.1 = (f32[3,16,8,256]{3,2,1,0:T(8,128)S(1)}, f32[3,16,8,256]{3,2,1,0:T(8,128)}, u32[]{:S(2)}) copy-start(f32[3,16,8,256]{3,2,1,0:T(8,128)} %velocity.3) | copy-start | bytes 1179652
  4.3 26.2 %all-to-all-start = ((s16[32,5,8,128]{3,2,1,0:T(8,128)(2,1)}), s16[32,5,8,128]{3,2,1,0:T(8,128)(2,1)S(1)}, u32[]{:S(2)}, u32[]{:S(2)}) async-start(s16[32,5,8,128]{3,2,1,0:T(8,128)(2,1)} %get-tuple-element.25), calls=%async_computation | async-start | bytes 655360 | tf_op jit(solution)/shard_map/all_to_all | solution.py:527
  15.3 17.3 %copy-start.7 = (bf16[2,256,256]{2,1,0:T(8,128)(2,1)S(1)}, bf16[2,256,256]{2,1,0:T(8,128)(2,1)}, u32[]{:S(2)}) copy-start(bf16[2,256,256]{2,1,0:T(8,128)(2,1)} %constant.106.clone.table) | copy-start | bytes 786436
  15.3 17.3 %collective-permute-start = (f32[3,1,8,256]{3,2,1,0:T(8,128)S(1)}, f32[3,1,8,256]{3,2,1,0:T(8,128)S(1)}, u32[]{:S(2)}, u32[]{:S(2)}) collective-permute-start(f32[3,1,8,256]{3,2,1,0:T(8,128)S(1)} %get-tuple-element.22), channel_id=1, source_target_pairs={{0,32},{32,64},{64,96},{96,128},{128,160},{160,192},{192,224},{224... | collective-permute-start | bytes 73736 | tf_op jit(solution)/shard_map/ppermute | solution.py:532
  17.4 15.3 %collective-permute-start.1 = (f32[3,1,8,256]{3,2,1,0:T(8,128)S(1)}, f32[3,1,8,256]{3,2,1,0:T(8,128)S(1)}, u32[]{:S(2)}, u32[]{:S(2)}) collective-permute-start(f32[3,1,8,256]{3,2,1,0:T(8,128)S(1)} %get-tuple-element.23), channel_id=1, source_target_pairs={{0,480},{32,0},{64,32},{96,64},{128,96},{160,128},{192,160},{224,1... | collective-permute-start | bytes 73736 | tf_op jit(solution)/shard_map/ppermute | solution.py:532
  26.7 6.0 %collective-permute-start.2 = (f32[3,16,1,256]{3,2,1,0:T(1,128)S(1)}, f32[3,16,1,256]{3,2,1,0:T(1,128)S(1)}, u32[]{:S(2)}, u32[]{:S(2)}) collective-permute-start(f32[3,16,1,256]{3,2,1,0:T(1,128)S(1)} %get-tuple-element.24), channel_id=1, source_target_pairs={{0,1},{1,2},{2,3},{3,4},{4,5},{5,6},{6,7},{7,8},{8,9},{9,10},{10,1... | collective-permute-start | bytes 147464 | tf_op jit(solution)/shard_map/ppermute | solution.py:532
  34.3 16.2 %copy-start.5 = (bf16[2,256,256]{2,1,0:T(8,128)(2,1)S(1)}, bf16[2,256,256]{2,1,0:T(8,128)(2,1)}, u32[]{:S(2)}) copy-start(bf16[2,256,256]{2,1,0:T(8,128)(2,1)} %constant.107.clone.left) | copy-start | bytes 786436
  34.4 16.2 %copy-start.10 = (bf16[2,128,256]{2,1,0:T(8,128)(2,1)S(1)}, bf16[2,128,256]{2,1,0:T(8,128)(2,1)}, u32[]{:S(2)}) copy-start(bf16[2,128,256]{2,1,0:T(8,128)(2,1)} %constant.108.clone.lanes) | copy-start | bytes 393220
  34.4 16.2 %copy-start.11 = (f32[2,32,1,128]{3,2,1,0:T(1,128)S(1)}, f32[2,32,1,128]{3,2,1,0:T(1,128)}, u32[]{:S(2)}) copy-start(f32[2,32,1,128]{3,2,1,0:T(1,128)} %constant.109.clone.twiddle) | copy-start | bytes 98308
  34.4 16.1 %all-to-all-start.1 = ((s16[32,4,8,128]{3,2,1,0:T(8,128)(2,1)}), s16[32,4,8,128]{3,2,1,0:T(8,128)(2,1)S(1)}, u32[]{:S(2)}, u32[]{:S(2)}) async-start(s16[32,4,8,128]{3,2,1,0:T(8,128)(2,1)} %get-tuple-element.29), calls=%async_computation.1 | async-start | bytes 524288 | tf_op jit(solution)/shard_map/all_to_all | solution.py:527
  52.2 8.8 %copy-start.18 = (s32[320]{0:T(512)S(1)}, s32[320]{0:T(512)}, u32[]{:S(2)}) copy-start(s32[320]{0:T(512)} %constant.112.clone) | copy-start | bytes 3844
  52.2 22.3 %all-to-all-start.2 = ((s16[16,7,8,128]{3,2,1,0:T(8,128)(2,1)}), s16[16,7,8,128]{3,2,1,0:T(8,128)(2,1)S(1)}, u32[]{:S(2)}, u32[]{:S(2)}) async-start(s16[16,7,8,128]{3,2,1,0:T(8,128)(2,1)} %shard_map.243), calls=%async_computation.2 | async-start | bytes 458752 | tf_op jit(solution)/shard_map/all_to_all | solution.py:527
  62.4 12.2 %copy-start.13 = (bf16[2,128,256]{2,1,0:T(8,128)(2,1)S(1)}, bf16[2,128,256]{2,1,0:T(8,128)(2,1)}, u32[]{:S(2)}) copy-start(bf16[2,128,256]{2,1,0:T(8,128)(2,1)} %constant.116.clone.lanes) | copy-start | bytes 393220
  62.4 12.2 %copy-start.14 = (bf16[128,256]{1,0:T(8,128)(2,1)S(1)}, bf16[128,256]{1,0:T(8,128)(2,1)}, u32[]{:S(2)}) copy-start(bf16[128,256]{1,0:T(8,128)(2,1)} %constant.119.clone.flips) | copy-start | bytes 196612
  62.4 12.2 %copy-start.15 = (bf16[2,64,256]{2,1,0:T(8,128)(2,1)S(1)}, bf16[2,64,256]{2,1,0:T(8,128)(2,1)}, u32[]{:S(2)}) copy-start(bf16[2,64,256]{2,1,0:T(8,128)(2,1)} %constant.114.clone.left_extra) | copy-start | bytes 196612
  62.7 11.8 %copy-start.2 = (bf16[2,256,320]{2,1,0:T(8,128)(2,1)S(1)}, bf16[2,256,320]{2,1,0:T(8,128)(2,1)}, u32[]{:S(2)}) copy-start(bf16[2,256,320]{2,1,0:T(8,128)(2,1)} %constant.115.clone.back) | copy-start | bytes 983044
  62.7 11.8 %copy-start.3 = (f32[2,40,8,128]{3,2,1,0:T(8,128)S(1)}, f32[2,40,8,128]{3,2,1,0:T(8,128)}, u32[]{:S(2)}) copy-start(f32[2,40,8,128]{3,2,1,0:T(8,128)} %constant.118.clone.twiddle) | copy-start | bytes 983044
  62.7 11.8 %copy-start.8 = (bf16[2,256,256]{2,1,0:T(8,128)(2,1)S(1)}, bf16[2,256,256]{2,1,0:T(8,128)(2,1)}, u32[]{:S(2)}) copy-start(bf16[2,256,256]{2,1,0:T(8,128)(2,1)} %constant.113.clone.left) | copy-start | bytes 786436
  62.8 11.8 %copy-start.12 = (bf16[2,128,256]{2,1,0:T(8,128)(2,1)S(1)}, bf16[2,128,256]{2,1,0:T(8,128)(2,1)}, u32[]{:S(2)}) copy-start(bf16[2,128,256]{2,1,0:T(8,128)(2,1)} %constant.117.clone.lanes_back) | copy-start | bytes 393220
  78.3 9.5 %copy-start = (bf16[32,3,8,128]{3,2,1,0:T(8,128)(2,1)S(1)}, bf16[32,3,8,128]{3,2,1,0:T(8,128)(2,1)}, u32[]{:S(2)}) copy-start(bf16[32,3,8,128]{3,2,1,0:T(8,128)(2,1)} %weights.3) | copy-start | bytes 589828
  78.3 22.6 %all-to-all-start.3 = ((s16[16,7,8,128]{3,2,1,0:T(8,128)(2,1)}), s16[16,7,8,128]{3,2,1,0:T(8,128)(2,1)S(1)}, u32[]{:S(2)}, u32[]{:S(2)}) async-start(s16[16,7,8,128]{3,2,1,0:T(8,128)(2,1)} %shard_map.244), calls=%async_computation.3 | async-start | bytes 458752 | tf_op jit(solution)/shard_map/all_to_all | solution.py:527
  87.8 13.2 %copy-start.6 = (bf16[2,256,256]{2,1,0:T(8,128)(2,1)S(1)}, bf16[2,256,256]{2,1,0:T(8,128)(2,1)}, u32[]{:S(2)}) copy-start(bf16[2,256,256]{2,1,0:T(8,128)(2,1)} %constant.120.clone.back) | copy-start | bytes 786436
  87.8 13.2 %copy-start.9 = (bf16[2,128,256]{2,1,0:T(8,128)(2,1)S(1)}, bf16[2,128,256]{2,1,0:T(8,128)(2,1)}, u32[]{:S(2)}) copy-start(bf16[2,128,256]{2,1,0:T(8,128)(2,1)} %constant.121.clone.lanes) | copy-start | bytes 393220
  102.2 19.9 %copy-start.4 = (bf16[2,256,256]{2,1,0:T(8,128)(2,1)S(1)}, bf16[2,256,256]{2,1,0:T(8,128)(2,1)}, u32[]{:S(2)}) copy-start(bf16[2,256,256]{2,1,0:T(8,128)(2,1)} %constant.122.clone.back) | copy-start | bytes 786436
  (3 other events, 2.0 us)

commit v6 on v5

--- a/solution.py
+++ b/solution.py
@@ -59,7 +59,14 @@
     lanes_back = split_table(np.concatenate([cosine, -sine], 1))
     phase = TURN / N * np.outer(FIRST, np.tile(np.arange(8), 16))
     twiddle = np.stack([np.cos(phase), np.sin(phase)]).astype(np.float32)[:, :, None, :]
-    return fore, back, lanes_fore, lanes_back, twiddle
+    phase = TURN / N * np.outer(FIRST, np.arange(128) // 8 % 8)
+    side_twiddle = np.stack([np.cos(phase), np.sin(phase)]).astype(np.float32)[:, :, None, :]
+    side = np.zeros((128, 2, 128))
+    for c in range(3):
+        for y in range(8):
+            side[8 * y + 4 + c, 0, 8 * c:8 * c + 8] = np.cos(small[y])
+            side[8 * y + 4 + c, 1, 8 * c:8 * c + 8] = np.sin(small[y])
+    return fore, back, lanes_fore, lanes_back, twiddle, split_table(side.reshape(128, 256)), side_twiddle
 
 
 def x_tables():
@@ -201,25 +208,34 @@
     return jnp.round(x * steps_per_unit(exponent)[None]), exponent
 
 
-def put_pairs(out, spectrum):
+def put_pairs(out, spectrum, side=None):
+    if side is not None:
+        spectrum = jnp.concatenate([spectrum, side[None]], 0)
     codes, exponent = encoded(spectrum)
-    codes = narrow(codes).reshape(3, 16, 2, 8, 128)
+    codes = codes.reshape(-1, 16, 2, 8, 128)
     exponent = exponent.reshape(16, 2, 8, 128)
     for p in range(2):
         for c in range(3):
-            out[:, 3 * p + c] = codes[c, :, p]
-    half = lane_half((1, 8, 128))
-    out[:, 6] = narrow(jnp.where(half == 0, exponent[:, 0], exponent[:, 1]))
-
-
-def take_pairs(values):
-    half = lane_half((1, 8, 128))
-    steps = step(wide(values[:, 6]))
-    turned = pltpu.roll(steps, 64, 2)
-    steps = (jnp.where(half == 0, steps, turned), jnp.where(half == 0, turned, steps))
+            out[:, 3 * p + c] = narrow(codes[c, :, p])
+    lane = lax.broadcasted_iota(jnp.int32, (1, 8, 128), 2)
+    rest = 0.0 if side is None else codes[3, :, 0] + pltpu.roll(codes[3, :, 1], 32, 2)
+    out[:, 6] = narrow(jnp.where(lane == 64, exponent[:, 0], jnp.where(lane == 65, exponent[:, 1], rest)))
+
+
+def take_pairs(values, sides=False):
+    rest = wide(values[:, 6])
+    steps = [jnp.broadcast_to(step(rest[:, :, 64 + p:65 + p]), (16, 8, 128)) for p in range(2)]
+    top = lax.broadcasted_iota(jnp.int32, (1, 8, 128), 2) >= 120
     parts = []
     for c in range(3):
-        pair = [wide(values[:, 3 * p + c]) * steps[p] for p in range(2)]
+        pair = []
+        for p in range(2):
+            part = wide(values[:, 3 * p + c]) * steps[p]
+            if sides:
+                side = rest * steps[p]
+                side = jnp.concatenate([side[1:], side[:1]], 0)
+                part = part + jnp.where(top, pltpu.roll(side, 120 - 32 * p - 8 * c, 2), 0.0)
+            pair.append(part)
         parts.append(jnp.stack(pair, 1).reshape(256, 128))
     return jnp.concatenate(parts, 0)
 
@@ -280,6 +296,7 @@
         s = count[d]
         count[d] = s + 1
         slots[n] = s
+        slots[32 + n] = d
         last = jnp.where(lane == 73 + s, brick[n].astype(F32), 0.0)
         for c in range(3):
             tile, side = tile_place(s, c)
@@ -291,9 +308,8 @@
     out[...] = narrow(total[...])
 
 
-def planes_kernel(_, velocity, x_first, x_last, y_last):
-    for c in range(3):
-        x_first[c] = velocity[c, 0:1]
+def planes_kernel(_, velocity, x_last, y_last):
+    for c in range(3):
         x_last[c] = velocity[c, 15:16]
         y_last[c] = velocity[c, :, 7:8, :]
 
@@ -326,7 +342,7 @@
         sums[0][c][...] = sums[0][c][...] + sums[1][c][...]
 
 
-def star_kernel(table, velocity, x_low, x_high, y_low, field0, field1, field2, out, turned):
+def star_kernel(table, velocity, x_low, y_low, field0, field1, field2, out, turned):
     u = [velocity[c].reshape(128, 256) for c in range(3)]
     sub = lax.broadcasted_iota(jnp.int32, (16, 8, 256), 1)
     rows = []
@@ -335,7 +351,7 @@
         v = velocity[c]
         beyond = jnp.where(sub == c, v[:, 0:1, :], beyond)
         turned[c] = jnp.transpose(u[c]).reshape(32, 8, 128)
-        ahead = jnp.concatenate([v[1:], x_high[c]], 0)
+        ahead = jnp.concatenate([v[1:], jnp.zeros((1, 8, 256), F32)], 0)
         behind = jnp.concatenate([x_low[c], v[:-1]], 0)
         total = u[0] * (ahead - behind).reshape(128, 256)
         ahead = jnp.where(sub == 7, 0.0, pltpu.roll(v, 7, 1))
@@ -343,7 +359,11 @@
         total = total + u[1] * (ahead - behind).reshape(128, 256)
         total = total + u[2] * (pltpu.roll(u[c], 255, 1) - pltpu.roll(u[c], 1, 1))
         rows.append(u[c] - (0.5 * DT_STEP) * total)
-    beyond = (-0.5 * DT_STEP) * y_low[1] * beyond
+    beyond = y_low[1] * beyond
+    side = jnp.zeros((8, 8, 256), F32)
+    for c in range(3):
+        side = jnp.where(sub[:8] == 4 + c, (x_low[0, 0] * velocity[c, 0]).reshape(8, 1, 256), side)
+    beyond = (-0.5 * DT_STEP) * (beyond + jnp.concatenate([side, jnp.zeros((8, 8, 256), F32)], 0))
     star = jnp.concatenate(rows + [beyond.reshape(128, 256)], 0)
     spectrum = table_left(table, star, ((1,), (1,)))
     field = jnp.concatenate([field[...].reshape(256, 128) for field in (field0, field1, field2)], 1)
@@ -386,11 +406,11 @@
             out[src, t] = narrow(jnp.where(half == 0, codes[2 * t], codes[2 * t + 1]))
 
 
-def interpolate(owner, slots, replies, weights, cells_high, cells_low, out):
+def interpolate(slots, replies, weights, cells_high, cells_low, out):
     half = lane_half()
     lane = lax.broadcasted_iota(jnp.int32, (8, 128), 1)
     for n in range(32):
-        d, s = owner[n], slots[n]
+        d, s = slots[32 + n], slots[n]
         steps = step(wide(replies[d, 7]))
         parts = []
         for c in range(3):
@@ -407,25 +427,30 @@
             out[c, n:n + 1] = jnp.sum(partial[8 * c:8 * c + 8] * w2, axis=0, keepdims=True)
 
 
-def y_kernel(left, lanes, twiddle, values, out):
+def y_kernel(left, lanes, twiddle, side_lanes, side_twiddle, values, out):
     beyond = wide(values[:, 3])
     steps = jnp.broadcast_to(step(beyond[:, :, 3:4]), (32, 8, 128))
     beyond = beyond * steps
+    lane = lax.broadcasted_iota(jnp.int32, (1, 8, 128), 2) % 8
+    last = lane == 7
+    side = jnp.where(lane >= 4, beyond, 0.0).reshape(256, 128)
     beyond = jnp.concatenate([beyond[1:], beyond[:1]], 0)
-    last = lax.broadcasted_iota(jnp.int32, (1, 8, 128), 2) % 8 == 7
     spectrum = []
     for c in range(3):
         part = wide(values[:, c]) * steps + jnp.where(last, pltpu.roll(beyond, 7 - c, 2), 0.0)
         spectrum.append(part.reshape(256, 128))
-    spectrum = table_left(left, jnp.concatenate(spectrum, 1))
+    spectrum = table_left(left, jnp.concatenate(spectrum + [side], 1))
+    side = spectrum[:, 384:].reshape(32, 8, 128)
+    side = side * side_twiddle[0] + swapped(side) * side_twiddle[1]
     spectrum = stacked(spectrum).reshape(96, 8, 128)
     spectrum = twiddled(spectrum, twiddle[0], twiddle[1])
     spectrum = lane_pass(spectrum.reshape(768, 128), lanes)
-    put_pairs(out, spectrum.reshape(3, 32, 8, 128))
+    side = lane_pass(side.reshape(256, 128), side_lanes)
+    put_pairs(out, spectrum.reshape(3, 32, 8, 128), side)
 
 
 def x_kernel(flags, left, left_extra, back, lanes, lanes_back, twiddle, flips, waves, damping, values, out):
-    packed = take_pairs(values)
+    packed = take_pairs(values, True)
     high, low = halves(packed)
     flipped = dot(jnp.concatenate([high, low], 1), jnp.concatenate([flips[...], flips[...]], 0))
     by_pair = (3, 16, 2, 8, 128)
@@ -467,8 +492,8 @@
     out[:, 7] = narrow(jnp.where(lane == 76, exponent, wide(replies[:, 4])))
 
 
-def last_kernel(owner, slots, back, values, weights, cells_high, cells_low, out, markers):
-    interpolate(owner, slots, values, weights, cells_high, cells_low, markers)
+def last_kernel(slots, back, values, weights, cells_high, cells_low, out, markers):
+    interpolate(slots, values, weights, cells_high, cells_low, markers)
     steps = step(wide(values[:, 7])[:, :, 76:77])
     spectrum = [(wide(values[:, c]) * steps).reshape(256, 128) for c in range(3)]
     field = table_right(jnp.transpose(jnp.concatenate(spectrum, 1)), back)
@@ -535,12 +560,12 @@
 def local(velocity, positions, weights, stiffness, rest_sq, owner_column, brick_index):
     row, col = lax.axis_index("row"), lax.axis_index("col")
     z_fore, z_back = z_tables()
-    y_fore, y_back, y_lanes, y_lanes_back, y_twiddle = y_tables()
+    y_fore, y_back, y_lanes, y_lanes_back, y_twiddle, side_lanes, side_twiddle = y_tables()
     x_fore, x_extra, x_back, x_lanes, x_lanes_back, x_twiddle, marks, flips = x_tables()
     flags = jnp.stack([row == 0, col == 0]).astype(jnp.int32)
 
     owner = owner_column.reshape(32)
-    spread_outs = (codes_of(32, 5), jax.ShapeDtypeStruct((32,), jnp.int32))
+    spread_outs = (codes_of(32, 5), jax.ShapeDtypeStruct((64,), jnp.int32))
     pushes, slots = call(
         spread_kernel, [HBM] * 6, spread_outs,
         [pltpu.SMEM((32,), jnp.int32), pltpu.SMEM((32,), jnp.int32), pltpu.VMEM((1, 32), BF16),
@@ -549,19 +574,18 @@
          pltpu.VMEM((32, 5, 8, 128), F32), pltpu.SemaphoreType.DMA((6,))], [VMEM, SMEM],
     )(*(pltpu.with_memory_space_constraint(x, pltpu.HBM) for x in (
         owner, brick_index, stiffness.reshape(1, 32), rest_sq.reshape(1, 32), positions.transpose(1, 0, 2), weights)))
-    x_first, x_last, y_last = call(
-        planes_kernel, [SMEM, VMEM], ([3, 1, 8, 256], [3, 1, 8, 256], [3, 16, 1, 256]))(slots, velocity)
+    x_last, y_last = call(planes_kernel, [SMEM, VMEM], ([3, 1, 8, 256], [3, 16, 1, 256]))(slots, velocity)
     y_low = shifted(y_last, "col", 1)
     x_low = shifted(x_last, "row", 1)
-    x_high = shifted(x_first, "row", -1)
     pushes = moved(pushes, "col")
     ids = pushes[:, 4, 0, 73:76].astype(jnp.int32)
 
     field = call(add_up_kernel, [SMEM, VMEM], ([32, 8, 128],) * 3, [pltpu.VMEM((32, 8, 128), F32)] * 3)(ids, pushes)
-    spectrum, turned = call(star_kernel, [VMEM] * 8, (codes_of(32, 4), [3, 32, 8, 128]))(
-        z_fore, velocity, x_low, x_high, y_low, *field)
+    spectrum, turned = call(star_kernel, [VMEM] * 7, (codes_of(32, 4), [3, 32, 8, 128]))(
+        z_fore, velocity, x_low, y_low, *field)
     spectrum = moved(spectrum, "col")
-    spectrum = call(y_kernel, [VMEM] * 4, codes_of(16, 7))(y_fore, y_lanes, y_twiddle, spectrum)
+    spectrum = call(y_kernel, [VMEM] * 6, codes_of(16, 7))(
+        y_fore, y_lanes, y_twiddle, side_lanes, side_twiddle, spectrum)
     marks = [jnp.asarray(m, jnp.int32) for m in marks]
     spectrum, marks = lax.optimization_barrier((spectrum, marks))
     spectrum = moved(spectrum, "row")
@@ -576,8 +600,8 @@
         y_back, y_lanes_back, y_twiddle, spectrum, replies)
     spectrum = moved(spectrum, "col")
     new_velocity, marker_velocity = call(
-        last_kernel, [SMEM, SMEM] + [VMEM] * 5, ([3, 16, 8, 256], [3, 32, 128]))(
-        owner, slots, z_back, spectrum, weights, cells_high, cells_low)
+        last_kernel, [SMEM] + [VMEM] * 5, ([3, 16, 8, 256], [3, 32, 128]))(
+        slots, z_back, spectrum, weights, cells_high, cells_low)
     return new_velocity, marker_velocity.transpose(1, 0, 2)
 
 

time: 126 us -> 121 us (0.960)
  starting transfers between devices: 51 us -> 43.6 us
  waiting for transfers between devices: 30.3 us -> 33.6 us
    ppermute x3 -> x2, starting transfers between devices: 15.2 us -> 5.68 us  [shifted(): lax.ppermute(plane, axis, [(i, (i + by) % count) for i in range(count)])]
    all_to_all x4, waiting for transfers between devices: 30.3 us -> 33.6 us  [moved(): return lax.all_to_all(x, axis, split_axis=0, concat_axis=0, tiled=True)]
    all_to_all x4, starting transfers between devices: 35.9 us -> 37.9 us  [moved(): return lax.all_to_all(x, axis, split_axis=0, concat_axis=0, tiled=True)]
  transfers between devices with their start and end apart: 7 -> 6, of which waited for: 3 -> 4; matrix products, arithmetic and copies ran while one was open for 1% -> 1% of each run, Pallas kernels for 5% -> 5%
where the time goes in v6:
time: 121 us; the launch traced here: 120 us
  starting transfers between devices  43.6 us (36%)
  waiting for transfers between devices  33.6 us (28%)
  Pallas kernels  20.1 us (17%)
  blocking collectives  19.9 us (16%)
  local copies, waits for them, and re-layouts  1.45 us (1%)
    all_to_all x4, starting transfers between devices, moved(): return lax.all_to_all(x, axis, split_axis=0, concat_axis=0, tiled=True)  37.9 us
    all_to_all x4, waiting for transfers between devices, moved(): return lax.all_to_all(x, axis, split_axis=0, concat_axis=0, tiled=True)  33.6 us
    all_to_all x1, blocking collectives, moved(): return lax.all_to_all(x, axis, split_axis=0, concat_axis=0, tiled=True)  19.9 us
    ppermute x2, starting transfers between devices, shifted(): lax.ppermute(plane, axis, [(i, (i + by) % count) for i in range(count)])  5.68 us
    pallas_call x1, Pallas kernels, local(): call(x_kernel, [SMEM] + [VMEM] * 10, codes_of(16, 7))  3.87 us
    pallas_call x1, Pallas kernels, local(): call(spread_kernel, [HBM] * 6, spread_outs, [pltpu.SMEM((32,), jnp.int32)...  3.67 us
    pallas_call x1, Pallas kernels, local(): call(reply_kernel, [SMEM, VMEM, VMEM], (codes_of(32, 5), cells, cells))  3.1 us
  transfers between devices with their start and end apart: 6, of which 4 were waited for; matrix products, arithmetic and copies ran while one was open for 1% of the time, Pallas kernels for 5%

profile of v6, /device:TPU:1, one launch (start us, length us, event | category | flops | bytes accessed | tf_op | source)
XLA Modules:
  0.0 120.5 jit_solution(17095846216543074622)
XLA Ops:
  0.6 3.7 %shard_map.257 = (s16[32,5,8,128]{3,2,1,0:T(8,128)(2,1)}, s32[64]{0:T(128)S(1)}) custom-call(s32[32]{0:T(128)} %bitcast.11, s32[32]{0:T(128)} %brick_in.1, bf16[1,32]{1,0:T(2,128)(2,1)} %bitcast.12, bf16[1,32]{1,0:T(2,128)(2,1)} %bitcast.13, bf16[3,32,128]{2,1,0:T(8,128)(2,1)} %bitcast.10, bf16[32,3,8,128]{3,2,1,0:T(8,128)(2,1)} %weights.3), custom_call_target="tpu_custom_call" | custom-call | tf_op jit(solution)/shard_map/pallas_call | solution.py:569
  4.3 10.4 %all-to-all-start = ((s16[32,5,8,128]{3,2,1,0:T(8,128)(2,1)}), s16[32,5,8,128]{3,2,1,0:T(8,128)(2,1)S(1)}, u32[]{:S(2)}, u32[]{:S(2)}) async-start(s16[32,5,8,128]{3,2,1,0:T(8,128)(2,1)} %get-tuple-element.23), calls=%async_computation | async-start | bytes 655360 | tf_op jit(solution)/shard_map/all_to_all | solution.py:552
  14.8 0.6 shard_map.258
  15.3 2.1 %collective-permute-start = (f32[3,1,8,256]{3,2,1,0:T(8,128)S(1)}, f32[3,1,8,256]{3,2,1,0:T(8,128)S(1)}, u32[]{:S(2)}, u32[]{:S(2)}) collective-permute-start(f32[3,1,8,256]{3,2,1,0:T(8,128)S(1)} %get-tuple-element.21), channel_id=1, source_target_pairs={{0,32},{32,64},{64,96},{96,128},{128,160},{160,192},{192,224},{224... | collective-permute-start | bytes 73736 | tf_op jit(solution)/shard_map/ppermute | solution.py:557
  17.4 3.6 %collective-permute-start.1 = (f32[3,16,1,256]{3,2,1,0:T(1,128)S(1)}, f32[3,16,1,256]{3,2,1,0:T(1,128)S(1)}, u32[]{:S(2)}, u32[]{:S(2)}) collective-permute-start(f32[3,16,1,256]{3,2,1,0:T(1,128)S(1)} %get-tuple-element.22), channel_id=1, source_target_pairs={{0,1},{1,2},{2,3},{3,4},{4,5},{5,6},{6,7},{7,8},{8,9},{9,10},{10,1... | collective-permute-start | bytes 147464 | tf_op jit(solution)/shard_map/ppermute | solution.py:557
  21.0 3.4 %all-to-all-done.pushes = s16[32,5,8,128]{3,2,1,0:T(8,128)(2,1)S(1)} async-done(((s16[32,5,8,128]{3,2,1,0:T(8,128)(2,1)}), s16[32,5,8,128]{3,2,1,0:T(8,128)(2,1)S(1)}, u32[]{:S(2)}, u32[]{:S(2)}) %all-to-all-start) | async-done | bytes 327712 | tf_op jit(solution)/shard_map/all_to_all | solution.py:552
  24.5 2.0 %shard_map.259 = (f32[32,8,128]{2,1,0:T(8,128)S(1)}, f32[32,8,128]{2,1,0:T(8,128)S(1)}, f32[32,8,128]{2,1,0:T(8,128)S(1)}) custom-call(s32[32,3]{1,0:T(8,128)S(1)} %bitcast.8, s16[32,5,8,128]{3,2,1,0:T(8,128)(2,1)S(1)} %all-to-all-done.pushes), custom_call_target="tpu_custom_call" | custom-call | tf_op jit(solution)/shard_map/pallas_call | solution.py:583
  26.5 1.7 %shard_map.260 = (s16[32,4,8,128]{3,2,1,0:T(8,128)(2,1)}, f32[3,32,8,128]{3,2,1,0:T(8,128)S(1)}) custom-call(bf16[2,256,256]{2,1,0:T(8,128)(2,1)S(1)} %copy-done.5, f32[3,16,8,256]{3,2,1,0:T(8,128)S(1)} %copy-done.1, f32[3,1,8,256]{3,2,1,0:T(8,128)S(1)} %collective-permute-done.x_low, f32[3,16,1,256]{3,2,1,0:T(1,128)S(1)} %collective-permute-done.1.y_low, ...), custom_call_target="tpu_custom_call" | custom-call | tf_op jit(solution)/shard_map/pallas_call | solution.py:584
  28.3 7.9 %all-to-all-start.1 = ((s16[32,4,8,128]{3,2,1,0:T(8,128)(2,1)}), s16[32,4,8,128]{3,2,1,0:T(8,128)(2,1)S(1)}, u32[]{:S(2)}, u32[]{:S(2)}) async-start(s16[32,4,8,128]{3,2,1,0:T(8,128)(2,1)} %get-tuple-element.27), calls=%async_computation.1 | async-start | bytes 524288 | tf_op jit(solution)/shard_map/all_to_all | solution.py:552
  36.2 8.8 %all-to-all-done.1.values = s16[32,4,8,128]{3,2,1,0:T(8,128)(2,1)S(1)} async-done(((s16[32,4,8,128]{3,2,1,0:T(8,128)(2,1)}), s16[32,4,8,128]{3,2,1,0:T(8,128)(2,1)S(1)}, u32[]{:S(2)}, u32[]{:S(2)}) %all-to-all-start.1) | async-done | bytes 262176 | tf_op jit(solution)/shard_map/all_to_all | solution.py:552
  45.0 1.8 %shard_map.261 = s16[16,7,8,128]{3,2,1,0:T(8,128)(2,1)} custom-call(bf16[2,256,256]{2,1,0:T(8,128)(2,1)S(1)} %copy-done.7, bf16[2,128,256]{2,1,0:T(8,128)(2,1)S(1)} %copy-done.11, f32[2,32,1,128]{3,2,1,0:T(1,128)S(1)} %copy-done.12, bf16[2,128,256]{2,1,0:T(8,128)(2,1)S(1)} %copy-done.10, f32[2,32,1,128]{3,2,1,0:T(1,128)S(1)} %copy-done.17, ...), custom_call_target="tpu_custom_call" | custom-call | tf_op jit(solution)/shard_map/pallas_call | solution.py:587
  46.9 10.2 %all-to-all-start.2 = ((s16[16,7,8,128]{3,2,1,0:T(8,128)(2,1)}), s16[16,7,8,128]{3,2,1,0:T(8,128)(2,1)S(1)}, u32[]{:S(2)}, u32[]{:S(2)}) async-start(s16[16,7,8,128]{3,2,1,0:T(8,128)(2,1)} %shard_map.261), calls=%async_computation.2 | async-start | bytes 458752 | tf_op jit(solution)/shard_map/all_to_all | solution.py:552
  57.1 0.7 copy-done.20
  57.8 0.7 copy-done.18
  58.4 0.3 fusion.22
  58.9 0.3 fusion.16.damping
  59.2 11.4 %all-to-all-done.2.values = s16[16,7,8,128]{3,2,1,0:T(8,128)(2,1)S(1)} async-done(((s16[16,7,8,128]{3,2,1,0:T(8,128)(2,1)}), s16[16,7,8,128]{3,2,1,0:T(8,128)(2,1)S(1)}, u32[]{:S(2)}, u32[]{:S(2)}) %all-to-all-start.2) | async-done | bytes 229408 | tf_op jit(solution)/shard_map/all_to_all | solution.py:552
  70.6 3.9 %shard_map.262 = s16[16,7,8,128]{3,2,1,0:T(8,128)(2,1)} custom-call(s32[2]{0:T(128)S(1)} %add_convert_fusion.flags, bf16[2,256,256]{2,1,0:T(8,128)(2,1)S(1)} %copy-done.8, bf16[2,64,256]{2,1,0:T(8,128)(2,1)S(1)} %copy-done.16, bf16[2,256,320]{2,1,0:T(8,128)(2,1)S(1)} %copy-done.2, bf16[2,128,256]{2,1,0:T(8,128)(2,1)S(1)} %copy-done.14, ...), custom_call_target="tpu_custom_call" | custom-call | tf_op jit(solution)/shard_map/pallas_call | solution.py:593
  74.5 9.4 %all-to-all-start.3 = ((s16[16,7,8,128]{3,2,1,0:T(8,128)(2,1)}), s16[16,7,8,128]{3,2,1,0:T(8,128)(2,1)S(1)}, u32[]{:S(2)}, u32[]{:S(2)}) async-start(s16[16,7,8,128]{3,2,1,0:T(8,128)(2,1)} %shard_map.262), calls=%async_computation.3 | async-start | bytes 458752 | tf_op jit(solution)/shard_map/all_to_all | solution.py:552
  84.0 3.1 %shard_map.263 = (s16[32,5,8,128]{3,2,1,0:T(8,128)(2,1)S(1)}, bf16[32,64,128]{2,1,0:T(8,128)(2,1)S(1)}, bf16[32,64,128]{2,1,0:T(8,128)(2,1)S(1)}) custom-call(s32[32,3]{1,0:T(8,128)S(1)} %bitcast.9, f32[3,32,8,128]{3,2,1,0:T(8,128)S(1)} %get-tuple-element.32.turned, bf16[32,3,8,128]{3,2,1,0:T(8,128)(2,1)S(1)} %copy-done), custom_call_target="tpu_custom_call" | custom-call | tf_op jit(solution)/shard_map/pallas_call | solution.py:597
  87.1 10.0 %all-to-all-done.3.values = s16[16,7,8,128]{3,2,1,0:T(8,128)(2,1)S(1)} async-done(((s16[16,7,8,128]{3,2,1,0:T(8,128)(2,1)}), s16[16,7,8,128]{3,2,1,0:T(8,128)(2,1)S(1)}, u32[]{:S(2)}, u32[]{:S(2)}) %all-to-all-start.3) | async-done | bytes 229408 | tf_op jit(solution)/shard_map/all_to_all | solution.py:552
  97.1 1.2 %shard_map.264 = s16[32,8,8,128]{3,2,1,0:T(8,128)(2,1)S(1)} custom-call(bf16[2,256,256]{2,1,0:T(8,128)(2,1)S(1)} %copy-done.6, bf16[2,128,256]{2,1,0:T(8,128)(2,1)S(1)} %copy-done.9, f32[2,32,1,128]{3,2,1,0:T(1,128)S(1)} %copy-done.12, s16[16,7,8,128]{3,2,1,0:T(8,128)(2,1)S(1)} %all-to-all-done.3.values, s16[32,5,8,128]{3,2,1,0:T(8,128)(2,1)S(1)} %get-tuple-element.33.replies), custom_call_target="tpu_custom_call" | custom-call | tf_op jit(solution)/shard_map/pallas_call | solution.py:599
  98.4 19.9 %all_to_all.25.values = s16[32,8,8,128]{3,2,1,0:T(8,128)(2,1)S(1)} all-to-all(s16[32,8,8,128]{3,2,1,0:T(8,128)(2,1)S(1)} %shard_map.264), channel_id=1, replica_groups=mesh['row'=16,'col'=32] {'col'}, dimensions={0} | all-to-all | bytes 1048576 | tf_op jit(solution)/shard_map/all_to_all | solution.py:552
  118.3 2.2 %shard_map.265 = (f32[3,16,8,256]{3,2,1,0:T(8,128)}, f32[3,32,128]{2,1,0:T(8,128)}) custom-call(s32[64]{0:T(128)S(1)} %get-tuple-element.20._.slots, bf16[2,256,256]{2,1,0:T(8,128)(2,1)S(1)} %copy-done.4, s16[32,8,8,128]{3,2,1,0:T(8,128)(2,1)S(1)} %all_to_all.25.values, bf16[32,3,8,128]{3,2,1,0:T(8,128)(2,1)S(1)} %copy-done, ...), custom_call_target="tpu_custom_call" | custom-call | tf_op jit(solution)/shard_map/pallas_call | solution.py:602
  (49 shorter events, 0.4 us)
Async XLA Ops:
  0.6 14.1 %copy-start.1 = (f32[3,16,8,256]{3,2,1,0:T(8,128)S(1)}, f32[3,16,8,256]{3,2,1,0:T(8,128)}, u32[]{:S(2)}) copy-start(f32[3,16,8,256]{3,2,1,0:T(8,128)} %velocity.3) | copy-start | bytes 1179652
  4.3 20.1 %all-to-all-start = ((s16[32,5,8,128]{3,2,1,0:T(8,128)(2,1)}), s16[32,5,8,128]{3,2,1,0:T(8,128)(2,1)S(1)}, u32[]{:S(2)}, u32[]{:S(2)}) async-start(s16[32,5,8,128]{3,2,1,0:T(8,128)(2,1)} %get-tuple-element.23), calls=%async_computation | async-start | bytes 655360 | tf_op jit(solution)/shard_map/all_to_all | solution.py:552
  15.3 11.2 %copy-start.5 = (bf16[2,256,256]{2,1,0:T(8,128)(2,1)S(1)}, bf16[2,256,256]{2,1,0:T(8,128)(2,1)}, u32[]{:S(2)}) copy-start(bf16[2,256,256]{2,1,0:T(8,128)(2,1)} %constant.110.clone.table) | copy-start | bytes 786436
  15.3 11.1 %collective-permute-start = (f32[3,1,8,256]{3,2,1,0:T(8,128)S(1)}, f32[3,1,8,256]{3,2,1,0:T(8,128)S(1)}, u32[]{:S(2)}, u32[]{:S(2)}) collective-permute-start(f32[3,1,8,256]{3,2,1,0:T(8,128)S(1)} %get-tuple-element.21), channel_id=1, source_target_pairs={{0,32},{32,64},{64,96},{96,128},{128,160},{160,192},{192,224},{224... | collective-permute-start | bytes 73736 | tf_op jit(solution)/shard_map/ppermute | solution.py:557
  17.4 9.1 %collective-permute-start.1 = (f32[3,16,1,256]{3,2,1,0:T(1,128)S(1)}, f32[3,16,1,256]{3,2,1,0:T(1,128)S(1)}, u32[]{:S(2)}, u32[]{:S(2)}) collective-permute-start(f32[3,16,1,256]{3,2,1,0:T(1,128)S(1)} %get-tuple-element.22), channel_id=1, source_target_pairs={{0,1},{1,2},{2,3},{3,4},{4,5},{5,6},{6,7},{7,8},{8,9},{9,10},{10,1... | collective-permute-start | bytes 147464 | tf_op jit(solution)/shard_map/ppermute | solution.py:557
  26.5 18.5 %copy-start.12 = (f32[2,32,1,128]{3,2,1,0:T(1,128)S(1)}, f32[2,32,1,128]{3,2,1,0:T(1,128)}, u32[]{:S(2)}) copy-start(f32[2,32,1,128]{3,2,1,0:T(1,128)} %constant.113.clone.twiddle) | copy-start | bytes 98308
  26.5 18.5 %copy-start.17 = (f32[2,32,1,128]{3,2,1,0:T(1,128)S(1)}, f32[2,32,1,128]{3,2,1,0:T(1,128)}, u32[]{:S(2)}) copy-start(f32[2,32,1,128]{3,2,1,0:T(1,128)} %constant.115.clone.side_twiddle) | copy-start | bytes 98308
  28.2 16.8 %copy-start.7 = (bf16[2,256,256]{2,1,0:T(8,128)(2,1)S(1)}, bf16[2,256,256]{2,1,0:T(8,128)(2,1)}, u32[]{:S(2)}) copy-start(bf16[2,256,256]{2,1,0:T(8,128)(2,1)} %constant.111.clone.left) | copy-start | bytes 786436
  28.2 16.8 %copy-start.10 = (bf16[2,128,256]{2,1,0:T(8,128)(2,1)S(1)}, bf16[2,128,256]{2,1,0:T(8,128)(2,1)}, u32[]{:S(2)}) copy-start(bf16[2,128,256]{2,1,0:T(8,128)(2,1)} %constant.114.clone.side_lanes) | copy-start | bytes 393220
  28.2 16.8 %copy-start.11 = (bf16[2,128,256]{2,1,0:T(8,128)(2,1)S(1)}, bf16[2,128,256]{2,1,0:T(8,128)(2,1)}, u32[]{:S(2)}) copy-start(bf16[2,128,256]{2,1,0:T(8,128)(2,1)} %constant.112.clone.lanes) | copy-start | bytes 393220
  28.3 16.8 %all-to-all-start.1 = ((s16[32,4,8,128]{3,2,1,0:T(8,128)(2,1)}), s16[32,4,8,128]{3,2,1,0:T(8,128)(2,1)S(1)}, u32[]{:S(2)}, u32[]{:S(2)}) async-start(s16[32,4,8,128]{3,2,1,0:T(8,128)(2,1)} %get-tuple-element.27), calls=%async_computation.1 | async-start | bytes 524288 | tf_op jit(solution)/shard_map/all_to_all | solution.py:552
  46.9 10.2 %copy-start.19 = (s32[320]{0:T(512)S(1)}, s32[320]{0:T(512)}, u32[]{:S(2)}) copy-start(s32[320]{0:T(512)} %constant.118.clone) | copy-start | bytes 3844
  46.9 23.7 %all-to-all-start.2 = ((s16[16,7,8,128]{3,2,1,0:T(8,128)(2,1)}), s16[16,7,8,128]{3,2,1,0:T(8,128)(2,1)S(1)}, u32[]{:S(2)}, u32[]{:S(2)}) async-start(s16[16,7,8,128]{3,2,1,0:T(8,128)(2,1)} %shard_map.261), calls=%async_computation.2 | async-start | bytes 458752 | tf_op jit(solution)/shard_map/all_to_all | solution.py:552
  58.4 12.2 %copy-start.14 = (bf16[2,128,256]{2,1,0:T(8,128)(2,1)S(1)}, bf16[2,128,256]{2,1,0:T(8,128)(2,1)}, u32[]{:S(2)}) copy-start(bf16[2,128,256]{2,1,0:T(8,128)(2,1)} %constant.122.clone.lanes) | copy-start | bytes 393220
  58.4 12.2 %copy-start.15 = (bf16[128,256]{1,0:T(8,128)(2,1)S(1)}, bf16[128,256]{1,0:T(8,128)(2,1)}, u32[]{:S(2)}) copy-start(bf16[128,256]{1,0:T(8,128)(2,1)} %constant.125.clone.flips) | copy-start | bytes 196612
  58.4 12.2 %copy-start.16 = (bf16[2,64,256]{2,1,0:T(8,128)(2,1)S(1)}, bf16[2,64,256]{2,1,0:T(8,128)(2,1)}, u32[]{:S(2)}) copy-start(bf16[2,64,256]{2,1,0:T(8,128)(2,1)} %constant.120.clone.left_extra) | copy-start | bytes 196612
  58.8 11.8 %copy-start.2 = (bf16[2,256,320]{2,1,0:T(8,128)(2,1)S(1)}, bf16[2,256,320]{2,1,0:T(8,128)(2,1)}, u32[]{:S(2)}) copy-start(bf16[2,256,320]{2,1,0:T(8,128)(2,1)} %constant.121.clone.back) | copy-start | bytes 983044
  58.8 11.8 %copy-start.3 = (f32[2,40,8,128]{3,2,1,0:T(8,128)S(1)}, f32[2,40,8,128]{3,2,1,0:T(8,128)}, u32[]{:S(2)}) copy-start(f32[2,40,8,128]{3,2,1,0:T(8,128)} %constant.124.clone.twiddle) | copy-start | bytes 983044
  58.8 11.8 %copy-start.8 = (bf16[2,256,256]{2,1,0:T(8,128)(2,1)S(1)}, bf16[2,256,256]{2,1,0:T(8,128)(2,1)}, u32[]{:S(2)}) copy-start(bf16[2,256,256]{2,1,0:T(8,128)(2,1)} %constant.119.clone.left) | copy-start | bytes 786436
  58.9 11.8 %copy-start.13 = (bf16[2,128,256]{2,1,0:T(8,128)(2,1)S(1)}, bf16[2,128,256]{2,1,0:T(8,128)(2,1)}, u32[]{:S(2)}) copy-start(bf16[2,128,256]{2,1,0:T(8,128)(2,1)} %constant.123.clone.lanes_back) | copy-start | bytes 393220
  74.5 22.6 %all-to-all-start.3 = ((s16[16,7,8,128]{3,2,1,0:T(8,128)(2,1)}), s16[16,7,8,128]{3,2,1,0:T(8,128)(2,1)S(1)}, u32[]{:S(2)}, u32[]{:S(2)}) async-start(s16[16,7,8,128]{3,2,1,0:T(8,128)(2,1)} %shard_map.262), calls=%async_computation.3 | async-start | bytes 458752 | tf_op jit(solution)/shard_map/all_to_all | solution.py:552
  84.0 13.2 %copy-start.6 = (bf16[2,256,256]{2,1,0:T(8,128)(2,1)S(1)}, bf16[2,256,256]{2,1,0:T(8,128)(2,1)}, u32[]{:S(2)}) copy-start(bf16[2,256,256]{2,1,0:T(8,128)(2,1)} %constant.126.clone.back) | copy-start | bytes 786436
  84.0 13.2 %copy-start.9 = (bf16[2,128,256]{2,1,0:T(8,128)(2,1)S(1)}, bf16[2,128,256]{2,1,0:T(8,128)(2,1)}, u32[]{:S(2)}) copy-start(bf16[2,128,256]{2,1,0:T(8,128)(2,1)} %constant.127.clone.lanes) | copy-start | bytes 393220
  98.4 19.9 %copy-start.4 = (bf16[2,256,256]{2,1,0:T(8,128)(2,1)S(1)}, bf16[2,256,256]{2,1,0:T(8,128)(2,1)}, u32[]{:S(2)}) copy-start(bf16[2,256,256]{2,1,0:T(8,128)(2,1)} %constant.128.clone.back) | copy-start | bytes 786436
  (3 other events, 10.8 us)

commit v7 on v6

--- a/solution.py
+++ b/solution.py
@@ -308,10 +308,14 @@
     out[...] = narrow(total[...])
 
 
-def planes_kernel(_, velocity, x_last, y_last):
+def y_plane_kernel(_, velocity, y_last):
+    for c in range(3):
+        y_last[c] = velocity[c, :, 7:8, :]
+
+
+def x_plane_kernel(_, velocity, x_last):
     for c in range(3):
         x_last[c] = velocity[c, 15:16]
-        y_last[c] = velocity[c, :, 7:8, :]
 
 
 def add_up_kernel(ids, pushes, field0, field1, field2, other0, other1, other2):
@@ -422,7 +426,8 @@
         cube_high, cube_low = halves(jnp.concatenate(parts, 0)[:, :64])
         w2 = weights[n, 2].astype(F32)
         high = cells_high[n]
-        partial = dot(cube_high, high) + dot(cube_low, high) + dot(cube_high, cells_low[n])
+        partial = dot(jnp.concatenate([cube_high, cube_low], 1), jnp.concatenate([high, high], 0))
+        partial = partial + dot(cube_high, cells_low[n])
         for c in range(3):
             out[c, n:n + 1] = jnp.sum(partial[8 * c:8 * c + 8] * w2, axis=0, keepdims=True)
 
@@ -574,7 +579,8 @@
          pltpu.VMEM((32, 5, 8, 128), F32), pltpu.SemaphoreType.DMA((6,))], [VMEM, SMEM],
     )(*(pltpu.with_memory_space_constraint(x, pltpu.HBM) for x in (
         owner, brick_index, stiffness.reshape(1, 32), rest_sq.reshape(1, 32), positions.transpose(1, 0, 2), weights)))
-    x_last, y_last = call(planes_kernel, [SMEM, VMEM], ([3, 1, 8, 256], [3, 16, 1, 256]))(slots, velocity)
+    y_last = call(y_plane_kernel, [SMEM, VMEM], [3, 16, 1, 256])(slots, velocity)
+    x_last = call(x_plane_kernel, [VMEM, VMEM], [3, 1, 8, 256])(y_last, velocity)
     y_low = shifted(y_last, "col", 1)
     x_low = shifted(x_last, "row", 1)
     pushes = moved(pushes, "col")

time: 121 us -> 124 us (1.025)
  waiting for transfers between devices: 33.6 us -> 36.7 us
  Pallas kernels: 20.1 us -> 22.6 us
  starting transfers between devices: 43.6 us -> 41.2 us
    ppermute x2, waiting for transfers between devices: 0.01 us -> 2.66 us  [shifted(): lax.ppermute(plane, axis, [(i, (i + by) % count) for i in range(count)])]
    pallas_call x1, Pallas kernels: 2.19 us -> 4.63 us  [local(): call(last_kernel, [SMEM] + [VMEM] * 5, ([3, 16, 8, 256], [3, 32, 128]))]
    all_to_all x4, starting transfers between devices: 37.9 us -> 35.6 us  [moved(): return lax.all_to_all(x, axis, split_axis=0, concat_axis=0, tiled=True)]
  transfers between devices with their start and end apart: 6 -> 6, of which waited for: 4 -> 5; matrix products, arithmetic and copies ran while one was open for 1% -> 1% of each run, Pallas kernels for 5% -> 5%
where the time goes in v7:
time: 124 us
  starting transfers between devices  41.2 us (33%)
  waiting for transfers between devices  36.7 us (30%)
  Pallas kernels  22.6 us (18%)
  blocking collectives  19.9 us (16%)
  local copies, waits for them, and re-layouts  1.44 us (1%)
    all_to_all x4, starting transfers between devices, moved(): return lax.all_to_all(x, axis, split_axis=0, concat_axis=0, tiled=True)  35.6 us
    all_to_all x4, waiting for transfers between devices, moved(): return lax.all_to_all(x, axis, split_axis=0, concat_axis=0, tiled=True)  34.1 us
    all_to_all x1, blocking collectives, moved(): return lax.all_to_all(x, axis, split_axis=0, concat_axis=0, tiled=True)  19.9 us
    ppermute x2, starting transfers between devices, shifted(): lax.ppermute(plane, axis, [(i, (i + by) % count) for i in range(count)])  5.6 us
    pallas_call x1, Pallas kernels, local(): call(last_kernel, [SMEM] + [VMEM] * 5, ([3, 16, 8, 256], [3, 32, 128]))  4.63 us
    pallas_call x1, Pallas kernels, local(): call(x_kernel, [SMEM] + [VMEM] * 10, codes_of(16, 7))  3.87 us
    pallas_call x1, Pallas kernels, local(): call(spread_kernel, [HBM] * 6, spread_outs, [pltpu.SMEM((32,), jnp.int32)...  3.67 us
    pallas_call x1, Pallas kernels, local(): call(reply_kernel, [SMEM, VMEM, VMEM], (codes_of(32, 5), cells, cells))  3.1 us
  transfers between devices with their start and end apart: 6, of which 5 were waited for; matrix products, arithmetic and copies ran while one was open for 1% of the time, Pallas kernels for 5%

profile of v7, /device:TPU:1, one launch (start us, length us, event | category | flops | bytes accessed | tf_op | source)
XLA Modules:
  0.0 123.7 jit_solution(10413362104574171624)
XLA Ops:
  0.6 3.7 %shard_map.257 = (s16[32,5,8,128]{3,2,1,0:T(8,128)(2,1)}, s32[64]{0:T(128)S(1)}) custom-call(s32[32]{0:T(128)} %bitcast.11, s32[32]{0:T(128)} %brick_in.1, bf16[1,32]{1,0:T(2,128)(2,1)} %bitcast.12, bf16[1,32]{1,0:T(2,128)(2,1)} %bitcast.13, bf16[3,32,128]{2,1,0:T(8,128)(2,1)} %bitcast.10, bf16[32,3,8,128]{3,2,1,0:T(8,128)(2,1)} %weights.3), custom_call_target="tpu_custom_call" | custom-call | tf_op jit(solution)/shard_map/pallas_call | solution.py:574
  4.3 10.4 %all-to-all-start = ((s16[32,5,8,128]{3,2,1,0:T(8,128)(2,1)}), s16[32,5,8,128]{3,2,1,0:T(8,128)(2,1)S(1)}, u32[]{:S(2)}, u32[]{:S(2)}) async-start(s16[32,5,8,128]{3,2,1,0:T(8,128)(2,1)} %get-tuple-element.19), calls=%async_computation | async-start | bytes 655360 | tf_op jit(solution)/shard_map/all_to_all | solution.py:557
  14.8 0.6 shard_map.258._
  15.3 3.5 %collective-permute-start.1 = (f32[3,16,1,256]{3,2,1,0:T(1,128)S(1)}, f32[3,16,1,256]{3,2,1,0:T(1,128)S(1)}, u32[]{:S(2)}, u32[]{:S(2)}) collective-permute-start(f32[3,16,1,256]{3,2,1,0:T(1,128)S(1)} %shard_map.258._), channel_id=1, source_target_pairs={{0,1},{1,2},{2,3},{3,4},{4,5},{5,6},{6,7},{7,8},{8,9},{9,10},{10,1... | collective-permute-start | bytes 147464 | tf_op jit(solution)/shard_map/ppermute | solution.py:562
  18.9 2.1 %collective-permute-start = (f32[3,1,8,256]{3,2,1,0:T(8,128)S(1)}, f32[3,1,8,256]{3,2,1,0:T(8,128)S(1)}, u32[]{:S(2)}, u32[]{:S(2)}) collective-permute-start(f32[3,1,8,256]{3,2,1,0:T(8,128)S(1)} %shard_map.259), channel_id=1, source_target_pairs={{0,32},{32,64},{64,96},{96,128},{128,160},{160,192},{192,224},{224... | collective-permute-start | bytes 73736 | tf_op jit(solution)/shard_map/ppermute | solution.py:562
  21.0 3.8 %all-to-all-done.pushes = s16[32,5,8,128]{3,2,1,0:T(8,128)(2,1)S(1)} async-done(((s16[32,5,8,128]{3,2,1,0:T(8,128)(2,1)}), s16[32,5,8,128]{3,2,1,0:T(8,128)(2,1)S(1)}, u32[]{:S(2)}, u32[]{:S(2)}) %all-to-all-start) | async-done | bytes 327712 | tf_op jit(solution)/shard_map/all_to_all | solution.py:557
  24.9 2.0 %shard_map.260 = (f32[32,8,128]{2,1,0:T(8,128)S(1)}, f32[32,8,128]{2,1,0:T(8,128)S(1)}, f32[32,8,128]{2,1,0:T(8,128)S(1)}) custom-call(s32[32,3]{1,0:T(8,128)S(1)} %bitcast.8, s16[32,5,8,128]{3,2,1,0:T(8,128)(2,1)S(1)} %all-to-all-done.pushes), custom_call_target="tpu_custom_call" | custom-call | tf_op jit(solution)/shard_map/pallas_call | solution.py:589
  26.9 2.7 %collective-permute-done.x_low = f32[3,1,8,256]{3,2,1,0:T(8,128)S(1)} collective-permute-done((f32[3,1,8,256]{3,2,1,0:T(8,128)S(1)}, f32[3,1,8,256]{3,2,1,0:T(8,128)S(1)}, u32[]{:S(2)}, u32[]{:S(2)}) %collective-permute-start) | collective-permute-done | bytes 24608 | tf_op jit(solution)/shard_map/ppermute | solution.py:562
  29.6 1.7 %shard_map.261 = (s16[32,4,8,128]{3,2,1,0:T(8,128)(2,1)}, f32[3,32,8,128]{3,2,1,0:T(8,128)S(1)}) custom-call(bf16[2,256,256]{2,1,0:T(8,128)(2,1)S(1)} %copy-done.5, f32[3,16,8,256]{3,2,1,0:T(8,128)S(1)} %copy-done, f32[3,1,8,256]{3,2,1,0:T(8,128)S(1)} %collective-permute-done.x_low, f32[3,16,1,256]{3,2,1,0:T(1,128)S(1)} %collective-permute-done.1.y_low, ...), custom_call_target="tpu_custom_call" | custom-call | tf_op jit(solution)/shard_map/pallas_call | solution.py:590
  31.3 6.9 %all-to-all-start.1 = ((s16[32,4,8,128]{3,2,1,0:T(8,128)(2,1)}), s16[32,4,8,128]{3,2,1,0:T(8,128)(2,1)S(1)}, u32[]{:S(2)}, u32[]{:S(2)}) async-start(s16[32,4,8,128]{3,2,1,0:T(8,128)(2,1)} %get-tuple-element.23), calls=%async_computation.1 | async-start | bytes 524288 | tf_op jit(solution)/shard_map/all_to_all | solution.py:557
  38.3 8.8 %all-to-all-done.1.values = s16[32,4,8,128]{3,2,1,0:T(8,128)(2,1)S(1)} async-done(((s16[32,4,8,128]{3,2,1,0:T(8,128)(2,1)}), s16[32,4,8,128]{3,2,1,0:T(8,128)(2,1)S(1)}, u32[]{:S(2)}, u32[]{:S(2)}) %all-to-all-start.1) | async-done | bytes 262176 | tf_op jit(solution)/shard_map/all_to_all | solution.py:557
  47.1 1.8 %shard_map.262 = s16[16,7,8,128]{3,2,1,0:T(8,128)(2,1)} custom-call(bf16[2,256,256]{2,1,0:T(8,128)(2,1)S(1)} %copy-done.7, bf16[2,128,256]{2,1,0:T(8,128)(2,1)S(1)} %copy-done.11, f32[2,32,1,128]{3,2,1,0:T(1,128)S(1)} %copy-done.12, bf16[2,128,256]{2,1,0:T(8,128)(2,1)S(1)} %copy-done.10, f32[2,32,1,128]{3,2,1,0:T(1,128)S(1)} %copy-done.17, ...), custom_call_target="tpu_custom_call" | custom-call | tf_op jit(solution)/shard_map/pallas_call | solution.py:593
  48.9 8.9 %all-to-all-start.2 = ((s16[16,7,8,128]{3,2,1,0:T(8,128)(2,1)}), s16[16,7,8,128]{3,2,1,0:T(8,128)(2,1)S(1)}, u32[]{:S(2)}, u32[]{:S(2)}) async-start(s16[16,7,8,128]{3,2,1,0:T(8,128)(2,1)} %shard_map.262), calls=%async_computation.2 | async-start | bytes 458752 | tf_op jit(solution)/shard_map/all_to_all | solution.py:557
  57.9 0.7 copy-done.20
  58.5 0.7 copy-done.18
  59.2 0.3 fusion.22
  59.9 11.4 %all-to-all-done.2.values = s16[16,7,8,128]{3,2,1,0:T(8,128)(2,1)S(1)} async-done(((s16[16,7,8,128]{3,2,1,0:T(8,128)(2,1)}), s16[16,7,8,128]{3,2,1,0:T(8,128)(2,1)S(1)}, u32[]{:S(2)}, u32[]{:S(2)}) %all-to-all-start.2) | async-done | bytes 229408 | tf_op jit(solution)/shard_map/all_to_all | solution.py:557
  71.4 3.9 %shard_map.263 = s16[16,7,8,128]{3,2,1,0:T(8,128)(2,1)} custom-call(s32[2]{0:T(128)S(1)} %add_convert_fusion.flags, bf16[2,256,256]{2,1,0:T(8,128)(2,1)S(1)} %copy-done.8, bf16[2,64,256]{2,1,0:T(8,128)(2,1)S(1)} %copy-done.16, bf16[2,256,320]{2,1,0:T(8,128)(2,1)S(1)} %copy-done.2, bf16[2,128,256]{2,1,0:T(8,128)(2,1)S(1)} %copy-done.14, ...), custom_call_target="tpu_custom_call" | custom-call | tf_op jit(solution)/shard_map/pallas_call | solution.py:599
  75.3 9.4 %all-to-all-start.3 = ((s16[16,7,8,128]{3,2,1,0:T(8,128)(2,1)}), s16[16,7,8,128]{3,2,1,0:T(8,128)(2,1)S(1)}, u32[]{:S(2)}, u32[]{:S(2)}) async-start(s16[16,7,8,128]{3,2,1,0:T(8,128)(2,1)} %shard_map.263), calls=%async_computation.3 | async-start | bytes 458752 | tf_op jit(solution)/shard_map/all_to_all | solution.py:557
  84.8 3.1 %shard_map.264 = (s16[32,5,8,128]{3,2,1,0:T(8,128)(2,1)S(1)}, bf16[32,64,128]{2,1,0:T(8,128)(2,1)S(1)}, bf16[32,64,128]{2,1,0:T(8,128)(2,1)S(1)}) custom-call(s32[32,3]{1,0:T(8,128)S(1)} %bitcast.9, f32[3,32,8,128]{3,2,1,0:T(8,128)S(1)} %get-tuple-element.28.turned, bf16[32,3,8,128]{3,2,1,0:T(8,128)(2,1)S(1)} %copy-done.1), custom_call_target="tpu_custom_call" | custom-call | tf_op jit(solution)/shard_map/pallas_call | solution.py:603
  87.9 10.0 %all-to-all-done.3.values = s16[16,7,8,128]{3,2,1,0:T(8,128)(2,1)S(1)} async-done(((s16[16,7,8,128]{3,2,1,0:T(8,128)(2,1)}), s16[16,7,8,128]{3,2,1,0:T(8,128)(2,1)S(1)}, u32[]{:S(2)}, u32[]{:S(2)}) %all-to-all-start.3) | async-done | bytes 229408 | tf_op jit(solution)/shard_map/all_to_all | solution.py:557
  97.9 1.2 shard_map.265
  99.2 19.9 %all_to_all.25.values = s16[32,8,8,128]{3,2,1,0:T(8,128)(2,1)S(1)} all-to-all(s16[32,8,8,128]{3,2,1,0:T(8,128)(2,1)S(1)} %shard_map.265), channel_id=1, replica_groups=mesh['row'=16,'col'=32] {'col'}, dimensions={0} | all-to-all | bytes 1048576 | tf_op jit(solution)/shard_map/all_to_all | solution.py:557
  119.0 4.6 %shard_map.266 = (f32[3,16,8,256]{3,2,1,0:T(8,128)}, f32[3,32,128]{2,1,0:T(8,128)}) custom-call(s32[64]{0:T(128)S(1)} %get-tuple-element.18._.slots, bf16[2,256,256]{2,1,0:T(8,128)(2,1)S(1)} %copy-done.4, s16[32,8,8,128]{3,2,1,0:T(8,128)(2,1)S(1)} %all_to_all.25.values, bf16[32,3,8,128]{3,2,1,0:T(8,128)(2,1)S(1)} %copy-done.1, ...), custom_call_target="tpu_custom_call" | custom-call | tf_op jit(solution)/shard_map/pallas_call | solution.py:608
  (50 shorter events, 0.6 us)
Async XLA Ops:
  0.6 14.1 %copy-start = (f32[3,16,8,256]{3,2,1,0:T(8,128)S(1)}, f32[3,16,8,256]{3,2,1,0:T(8,128)}, u32[]{:S(2)}) copy-start(f32[3,16,8,256]{3,2,1,0:T(8,128)} %velocity.5) | copy-start | bytes 1179652
  4.3 20.5 %all-to-all-start = ((s16[32,5,8,128]{3,2,1,0:T(8,128)(2,1)}), s16[32,5,8,128]{3,2,1,0:T(8,128)(2,1)S(1)}, u32[]{:S(2)}, u32[]{:S(2)}) async-start(s16[32,5,8,128]{3,2,1,0:T(8,128)(2,1)} %get-tuple-element.19), calls=%async_computation | async-start | bytes 655360 | tf_op jit(solution)/shard_map/all_to_all | solution.py:557
  15.3 14.2 %collective-permute-start.1 = (f32[3,16,1,256]{3,2,1,0:T(1,128)S(1)}, f32[3,16,1,256]{3,2,1,0:T(1,128)S(1)}, u32[]{:S(2)}, u32[]{:S(2)}) collective-permute-start(f32[3,16,1,256]{3,2,1,0:T(1,128)S(1)} %shard_map.258._), channel_id=1, source_target_pairs={{0,1},{1,2},{2,3},{3,4},{4,5},{5,6},{6,7},{7,8},{8,9},{9,10},{10,1... | collective-permute-start | bytes 147464 | tf_op jit(solution)/shard_map/ppermute | solution.py:562
  18.9 10.7 %copy-start.5 = (bf16[2,256,256]{2,1,0:T(8,128)(2,1)S(1)}, bf16[2,256,256]{2,1,0:T(8,128)(2,1)}, u32[]{:S(2)}) copy-start(bf16[2,256,256]{2,1,0:T(8,128)(2,1)} %constant.110.clone.table) | copy-start | bytes 786436
  18.9 10.6 %collective-permute-start = (f32[3,1,8,256]{3,2,1,0:T(8,128)S(1)}, f32[3,1,8,256]{3,2,1,0:T(8,128)S(1)}, u32[]{:S(2)}, u32[]{:S(2)}) collective-permute-start(f32[3,1,8,256]{3,2,1,0:T(8,128)S(1)} %shard_map.259), channel_id=1, source_target_pairs={{0,32},{32,64},{64,96},{96,128},{128,160},{160,192},{192,224},{224... | collective-permute-start | bytes 73736 | tf_op jit(solution)/shard_map/ppermute | solution.py:562
  29.6 17.5 %copy-start.12 = (f32[2,32,1,128]{3,2,1,0:T(1,128)S(1)}, f32[2,32,1,128]{3,2,1,0:T(1,128)}, u32[]{:S(2)}) copy-start(f32[2,32,1,128]{3,2,1,0:T(1,128)} %constant.113.clone.twiddle) | copy-start | bytes 98308
  29.6 17.5 %copy-start.17 = (f32[2,32,1,128]{3,2,1,0:T(1,128)S(1)}, f32[2,32,1,128]{3,2,1,0:T(1,128)}, u32[]{:S(2)}) copy-start(f32[2,32,1,128]{3,2,1,0:T(1,128)} %constant.115.clone.side_twiddle) | copy-start | bytes 98308
  31.3 15.8 %copy-start.7 = (bf16[2,256,256]{2,1,0:T(8,128)(2,1)S(1)}, bf16[2,256,256]{2,1,0:T(8,128)(2,1)}, u32[]{:S(2)}) copy-start(bf16[2,256,256]{2,1,0:T(8,128)(2,1)} %constant.111.clone.left) | copy-start | bytes 786436
  31.3 15.8 %copy-start.10 = (bf16[2,128,256]{2,1,0:T(8,128)(2,1)S(1)}, bf16[2,128,256]{2,1,0:T(8,128)(2,1)}, u32[]{:S(2)}) copy-start(bf16[2,128,256]{2,1,0:T(8,128)(2,1)} %constant.114.clone.side_lanes) | copy-start | bytes 393220
  31.3 15.8 %copy-start.11 = (bf16[2,128,256]{2,1,0:T(8,128)(2,1)S(1)}, bf16[2,128,256]{2,1,0:T(8,128)(2,1)}, u32[]{:S(2)}) copy-start(bf16[2,128,256]{2,1,0:T(8,128)(2,1)} %constant.112.clone.lanes) | copy-start | bytes 393220
  31.3 15.8 %all-to-all-start.1 = ((s16[32,4,8,128]{3,2,1,0:T(8,128)(2,1)}), s16[32,4,8,128]{3,2,1,0:T(8,128)(2,1)S(1)}, u32[]{:S(2)}, u32[]{:S(2)}) async-start(s16[32,4,8,128]{3,2,1,0:T(8,128)(2,1)} %get-tuple-element.23), calls=%async_computation.1 | async-start | bytes 524288 | tf_op jit(solution)/shard_map/all_to_all | solution.py:557
  48.9 22.4 %all-to-all-start.2 = ((s16[16,7,8,128]{3,2,1,0:T(8,128)(2,1)}), s16[16,7,8,128]{3,2,1,0:T(8,128)(2,1)S(1)}, u32[]{:S(2)}, u32[]{:S(2)}) async-start(s16[16,7,8,128]{3,2,1,0:T(8,128)(2,1)} %shard_map.262), calls=%async_computation.2 | async-start | bytes 458752 | tf_op jit(solution)/shard_map/all_to_all | solution.py:557
  59.2 12.2 %copy-start.14 = (bf16[2,128,256]{2,1,0:T(8,128)(2,1)S(1)}, bf16[2,128,256]{2,1,0:T(8,128)(2,1)}, u32[]{:S(2)}) copy-start(bf16[2,128,256]{2,1,0:T(8,128)(2,1)} %constant.122.clone.lanes) | copy-start | bytes 393220
  59.2 12.2 %copy-start.15 = (bf16[128,256]{1,0:T(8,128)(2,1)S(1)}, bf16[128,256]{1,0:T(8,128)(2,1)}, u32[]{:S(2)}) copy-start(bf16[128,256]{1,0:T(8,128)(2,1)} %constant.125.clone.flips) | copy-start | bytes 196612
  59.2 12.2 %copy-start.16 = (bf16[2,64,256]{2,1,0:T(8,128)(2,1)S(1)}, bf16[2,64,256]{2,1,0:T(8,128)(2,1)}, u32[]{:S(2)}) copy-start(bf16[2,64,256]{2,1,0:T(8,128)(2,1)} %constant.120.clone.left_extra) | copy-start | bytes 196612
  59.5 11.8 %copy-start.2 = (bf16[2,256,320]{2,1,0:T(8,128)(2,1)S(1)}, bf16[2,256,320]{2,1,0:T(8,128)(2,1)}, u32[]{:S(2)}) copy-start(bf16[2,256,320]{2,1,0:T(8,128)(2,1)} %constant.121.clone.back) | copy-start | bytes 983044
  59.6 11.8 %copy-start.3 = (f32[2,40,8,128]{3,2,1,0:T(8,128)S(1)}, f32[2,40,8,128]{3,2,1,0:T(8,128)}, u32[]{:S(2)}) copy-start(f32[2,40,8,128]{3,2,1,0:T(8,128)} %constant.124.clone.twiddle) | copy-start | bytes 983044
  59.6 11.8 %copy-start.8 = (bf16[2,256,256]{2,1,0:T(8,128)(2,1)S(1)}, bf16[2,256,256]{2,1,0:T(8,128)(2,1)}, u32[]{:S(2)}) copy-start(bf16[2,256,256]{2,1,0:T(8,128)(2,1)} %constant.119.clone.left) | copy-start | bytes 786436
  59.6 11.8 %copy-start.13 = (bf16[2,128,256]{2,1,0:T(8,128)(2,1)S(1)}, bf16[2,128,256]{2,1,0:T(8,128)(2,1)}, u32[]{:S(2)}) copy-start(bf16[2,128,256]{2,1,0:T(8,128)(2,1)} %constant.123.clone.lanes_back) | copy-start | bytes 393220
  75.3 9.5 %copy-start.1 = (bf16[32,3,8,128]{3,2,1,0:T(8,128)(2,1)S(1)}, bf16[32,3,8,128]{3,2,1,0:T(8,128)(2,1)}, u32[]{:S(2)}) copy-start(bf16[32,3,8,128]{3,2,1,0:T(8,128)(2,1)} %weights.3) | copy-start | bytes 589828
  75.3 22.6 %all-to-all-start.3 = ((s16[16,7,8,128]{3,2,1,0:T(8,128)(2,1)}), s16[16,7,8,128]{3,2,1,0:T(8,128)(2,1)S(1)}, u32[]{:S(2)}, u32[]{:S(2)}) async-start(s16[16,7,8,128]{3,2,1,0:T(8,128)(2,1)} %shard_map.263), calls=%async_computation.3 | async-start | bytes 458752 | tf_op jit(solution)/shard_map/all_to_all | solution.py:557
  84.7 13.2 %copy-start.6 = (bf16[2,256,256]{2,1,0:T(8,128)(2,1)S(1)}, bf16[2,256,256]{2,1,0:T(8,128)(2,1)}, u32[]{:S(2)}) copy-start(bf16[2,256,256]{2,1,0:T(8,128)(2,1)} %constant.126.clone.back) | copy-start | bytes 786436
  84.7 13.2 %copy-start.9 = (bf16[2,128,256]{2,1,0:T(8,128)(2,1)S(1)}, bf16[2,128,256]{2,1,0:T(8,128)(2,1)}, u32[]{:S(2)}) copy-start(bf16[2,128,256]{2,1,0:T(8,128)(2,1)} %constant.127.clone.lanes) | copy-start | bytes 393220
  99.1 19.9 %copy-start.4 = (bf16[2,256,256]{2,1,0:T(8,128)(2,1)S(1)}, bf16[2,256,256]{2,1,0:T(8,128)(2,1)}, u32[]{:S(2)}) copy-start(bf16[2,256,256]{2,1,0:T(8,128)(2,1)} %constant.128.clone.back) | copy-start | bytes 786436
  (3 other events, 10.2 us)

commit v8 on v6

--- a/solution.py
+++ b/solution.py
@@ -314,7 +314,7 @@
         y_last[c] = velocity[c, :, 7:8, :]
 
 
-def add_up_kernel(ids, pushes, field0, field1, field2, other0, other1, other2):
+def add_up_kernel(ids, pushes, table, velocity, out, turned_out, field0, field1, field2, other0, other1, other2):
     sums = ((field0, field1, field2), (other0, other1, other2))
     for group in sums:
         for field in group:
@@ -339,10 +339,12 @@
                     sums[odd][c][z_block] += jnp.where(half == x_half, cube, 0.0)
 
     for c in range(3):
-        sums[0][c][...] = sums[0][c][...] + sums[1][c][...]
-
-
-def star_kernel(table, velocity, x_low, y_low, field0, field1, field2, out, turned):
+        turned_out[c] = jnp.transpose(velocity[c].reshape(128, 256)).reshape(32, 8, 128)
+    field = jnp.concatenate([(sums[0][c][...] + sums[1][c][...]).reshape(256, 128) for c in range(3)], 1)
+    out[...] = table_left(table, DT_STEP * field)
+
+
+def star_kernel(table, velocity, x_low, y_low, field, out):
     u = [velocity[c].reshape(128, 256) for c in range(3)]
     sub = lax.broadcasted_iota(jnp.int32, (16, 8, 256), 1)
     rows = []
@@ -350,7 +352,6 @@
     for c in range(3):
         v = velocity[c]
         beyond = jnp.where(sub == c, v[:, 0:1, :], beyond)
-        turned[c] = jnp.transpose(u[c]).reshape(32, 8, 128)
         ahead = jnp.concatenate([v[1:], jnp.zeros((1, 8, 256), F32)], 0)
         behind = jnp.concatenate([x_low[c], v[:-1]], 0)
         total = u[0] * (ahead - behind).reshape(128, 256)
@@ -366,8 +367,7 @@
     beyond = (-0.5 * DT_STEP) * (beyond + jnp.concatenate([side, jnp.zeros((8, 8, 256), F32)], 0))
     star = jnp.concatenate(rows + [beyond.reshape(128, 256)], 0)
     spectrum = table_left(table, star, ((1,), (1,)))
-    field = jnp.concatenate([field[...].reshape(256, 128) for field in (field0, field1, field2)], 1)
-    total = spectrum[:, :384] + table_left(table, DT_STEP * field)
+    total = spectrum[:, :384] + field[...]
     total = jnp.concatenate([stacked(total), spectrum[:, 384:]], 0)
     codes, exponent = encoded(total.reshape(4, 32, 8, 128))
     for t in range(3):
@@ -580,9 +580,9 @@
     pushes = moved(pushes, "col")
     ids = pushes[:, 4, 0, 73:76].astype(jnp.int32)
 
-    field = call(add_up_kernel, [SMEM, VMEM], ([32, 8, 128],) * 3, [pltpu.VMEM((32, 8, 128), F32)] * 3)(ids, pushes)
-    spectrum, turned = call(star_kernel, [VMEM] * 7, (codes_of(32, 4), [3, 32, 8, 128]))(
-        z_fore, velocity, x_low, y_low, *field)
+    field, turned = call(add_up_kernel, [SMEM] + [VMEM] * 3, ([256, 384], [3, 32, 8, 128]),
+                         [pltpu.VMEM((32, 8, 128), F32)] * 6)(ids, pushes, z_fore, velocity)
+    spectrum = call(star_kernel, [VMEM] * 5, codes_of(32, 4))(z_fore, velocity, x_low, y_low, field)
     spectrum = moved(spectrum, "col")
     spectrum = call(y_kernel, [VMEM] * 6, codes_of(16, 7))(
         y_fore, y_lanes, y_twiddle, side_lanes, side_twiddle, spectrum)

time: 121 us -> 121 us (level)
  no operation moved by 1% of the time
where the time goes in v8:
time: 121 us; the launch traced here: 120 us
  starting transfers between devices  42.9 us (35%)
  waiting for transfers between devices  33.7 us (28%)
  Pallas kernels  20.3 us (17%)
  blocking collectives  19.9 us (16%)
  local copies, waits for them, and re-layouts  1.45 us (1%)
    all_to_all x4, starting transfers between devices, moved(): return lax.all_to_all(x, axis, split_axis=0, concat_axis=0, tiled=True)  37.4 us
    all_to_all x4, waiting for transfers between devices, moved(): return lax.all_to_all(x, axis, split_axis=0, concat_axis=0, tiled=True)  33.7 us
    all_to_all x1, blocking collectives, moved(): return lax.all_to_all(x, axis, split_axis=0, concat_axis=0, tiled=True)  19.9 us
    ppermute x2, starting transfers between devices, shifted(): lax.ppermute(plane, axis, [(i, (i + by) % count) for i in range(count)])  5.55 us
    pallas_call x1, Pallas kernels, local(): call(x_kernel, [SMEM] + [VMEM] * 10, codes_of(16, 7))  3.87 us
    pallas_call x1, Pallas kernels, local(): call(spread_kernel, [HBM] * 6, spread_outs, [pltpu.SMEM((32,), jnp.int32)...  3.67 us
    pallas_call x1, Pallas kernels, local(): call(reply_kernel, [SMEM, VMEM, VMEM], (codes_of(32, 5), cells, cells))  3.1 us
  transfers between devices with their start and end apart: 6, of which 4 were waited for; matrix products, arithmetic and copies ran while one was open for 1% of the time, Pallas kernels for 5%

profile of v8, /device:TPU:1, one launch (start us, length us, event | category | flops | bytes accessed | tf_op | source)
XLA Modules:
  0.0 120.1 jit_solution(13173908742259590266)
XLA Ops:
  0.6 3.7 %shard_map.257 = (s16[32,5,8,128]{3,2,1,0:T(8,128)(2,1)}, s32[64]{0:T(128)S(1)}) custom-call(s32[32]{0:T(128)} %bitcast.11, s32[32]{0:T(128)} %brick_in.1, bf16[1,32]{1,0:T(2,128)(2,1)} %bitcast.12, bf16[1,32]{1,0:T(2,128)(2,1)} %bitcast.13, bf16[3,32,128]{2,1,0:T(8,128)(2,1)} %bitcast.10, bf16[32,3,8,128]{3,2,1,0:T(8,128)(2,1)} %weights.3), custom_call_target="tpu_custom_call" | custom-call | tf_op jit(solution)/shard_map/pallas_call | solution.py:569
  4.3 10.4 %all-to-all-start = ((s16[32,5,8,128]{3,2,1,0:T(8,128)(2,1)}), s16[32,5,8,128]{3,2,1,0:T(8,128)(2,1)S(1)}, u32[]{:S(2)}, u32[]{:S(2)}) async-start(s16[32,5,8,128]{3,2,1,0:T(8,128)(2,1)} %get-tuple-element.20), calls=%async_computation | async-start | bytes 655360 | tf_op jit(solution)/shard_map/all_to_all | solution.py:552
  14.8 0.6 shard_map.258
  15.3 1.9 %collective-permute-start = (f32[3,1,8,256]{3,2,1,0:T(8,128)S(1)}, f32[3,1,8,256]{3,2,1,0:T(8,128)S(1)}, u32[]{:S(2)}, u32[]{:S(2)}) collective-permute-start(f32[3,1,8,256]{3,2,1,0:T(8,128)S(1)} %get-tuple-element.18), channel_id=1, source_target_pairs={{0,32},{32,64},{64,96},{96,128},{128,160},{160,192},{192,224},{224... | collective-permute-start | bytes 73736 | tf_op jit(solution)/shard_map/ppermute | solution.py:557
  17.3 3.6 %collective-permute-start.1 = (f32[3,16,1,256]{3,2,1,0:T(1,128)S(1)}, f32[3,16,1,256]{3,2,1,0:T(1,128)S(1)}, u32[]{:S(2)}, u32[]{:S(2)}) collective-permute-start(f32[3,16,1,256]{3,2,1,0:T(1,128)S(1)} %get-tuple-element.19), channel_id=1, source_target_pairs={{0,1},{1,2},{2,3},{3,4},{4,5},{5,6},{6,7},{7,8},{8,9},{9,10},{10,1... | collective-permute-start | bytes 147464 | tf_op jit(solution)/shard_map/ppermute | solution.py:557
  20.9 3.5 %all-to-all-done.pushes = s16[32,5,8,128]{3,2,1,0:T(8,128)(2,1)S(1)} async-done(((s16[32,5,8,128]{3,2,1,0:T(8,128)(2,1)}), s16[32,5,8,128]{3,2,1,0:T(8,128)(2,1)S(1)}, u32[]{:S(2)}, u32[]{:S(2)}) %all-to-all-start) | async-done | bytes 327712 | tf_op jit(solution)/shard_map/all_to_all | solution.py:552
  24.5 2.3 %shard_map.259 = (f32[256,384]{1,0:T(8,128)S(1)}, f32[3,32,8,128]{3,2,1,0:T(8,128)S(1)}) custom-call(s32[32,3]{1,0:T(8,128)S(1)} %bitcast.8, s16[32,5,8,128]{3,2,1,0:T(8,128)(2,1)S(1)} %all-to-all-done.pushes, bf16[2,256,256]{2,1,0:T(8,128)(2,1)S(1)} %copy-done.2, f32[3,16,8,256]{3,2,1,0:T(8,128)S(1)} %copy-done), custom_call_target="tpu_custom_call" | custom-call | tf_op jit(solution)/shard_map/pallas_call | solution.py:583
  26.9 1.5 %shard_map.260 = s16[32,4,8,128]{3,2,1,0:T(8,128)(2,1)} custom-call(bf16[2,256,256]{2,1,0:T(8,128)(2,1)S(1)} %copy-done.2, f32[3,16,8,256]{3,2,1,0:T(8,128)S(1)} %copy-done, f32[3,1,8,256]{3,2,1,0:T(8,128)S(1)} %collective-permute-done.x_low, f32[3,16,1,256]{3,2,1,0:T(1,128)S(1)} %collective-permute-done.1.y_low, f32[256,384]{1,0:T(8,128)S(1)} %get-tuple-element.21.field), custom_call_target="tpu_custom_call" | custom-call | tf_op jit(solution)/shard_map/pallas_call | solution.py:585
  28.4 7.3 %all-to-all-start.1 = ((s16[32,4,8,128]{3,2,1,0:T(8,128)(2,1)}), s16[32,4,8,128]{3,2,1,0:T(8,128)(2,1)S(1)}, u32[]{:S(2)}, u32[]{:S(2)}) async-start(s16[32,4,8,128]{3,2,1,0:T(8,128)(2,1)} %shard_map.260), calls=%async_computation.1 | async-start | bytes 524288 | tf_op jit(solution)/shard_map/all_to_all | solution.py:552
  35.9 8.8 %all-to-all-done.1.values = s16[32,4,8,128]{3,2,1,0:T(8,128)(2,1)S(1)} async-done(((s16[32,4,8,128]{3,2,1,0:T(8,128)(2,1)}), s16[32,4,8,128]{3,2,1,0:T(8,128)(2,1)S(1)}, u32[]{:S(2)}, u32[]{:S(2)}) %all-to-all-start.1) | async-done | bytes 262176 | tf_op jit(solution)/shard_map/all_to_all | solution.py:552
  44.7 1.8 %shard_map.261 = s16[16,7,8,128]{3,2,1,0:T(8,128)(2,1)} custom-call(bf16[2,256,256]{2,1,0:T(8,128)(2,1)S(1)} %copy-done.7, bf16[2,128,256]{2,1,0:T(8,128)(2,1)S(1)} %copy-done.11, f32[2,32,1,128]{3,2,1,0:T(1,128)S(1)} %copy-done.12, bf16[2,128,256]{2,1,0:T(8,128)(2,1)S(1)} %copy-done.10, f32[2,32,1,128]{3,2,1,0:T(1,128)S(1)} %copy-done.17, ...), custom_call_target="tpu_custom_call" | custom-call | tf_op jit(solution)/shard_map/pallas_call | solution.py:587
  46.5 10.2 %all-to-all-start.2 = ((s16[16,7,8,128]{3,2,1,0:T(8,128)(2,1)}), s16[16,7,8,128]{3,2,1,0:T(8,128)(2,1)S(1)}, u32[]{:S(2)}, u32[]{:S(2)}) async-start(s16[16,7,8,128]{3,2,1,0:T(8,128)(2,1)} %shard_map.261), calls=%async_computation.2 | async-start | bytes 458752 | tf_op jit(solution)/shard_map/all_to_all | solution.py:552
  56.8 0.7 copy-done.20
  57.4 0.7 copy-done.18
  58.1 0.3 fusion.22
  58.5 0.3 fusion.16.damping
  58.8 11.4 %all-to-all-done.2.values = s16[16,7,8,128]{3,2,1,0:T(8,128)(2,1)S(1)} async-done(((s16[16,7,8,128]{3,2,1,0:T(8,128)(2,1)}), s16[16,7,8,128]{3,2,1,0:T(8,128)(2,1)S(1)}, u32[]{:S(2)}, u32[]{:S(2)}) %all-to-all-start.2) | async-done | bytes 229408 | tf_op jit(solution)/shard_map/all_to_all | solution.py:552
  70.3 3.9 %shard_map.262 = s16[16,7,8,128]{3,2,1,0:T(8,128)(2,1)} custom-call(s32[2]{0:T(128)S(1)} %add_convert_fusion.flags, bf16[2,256,256]{2,1,0:T(8,128)(2,1)S(1)} %copy-done.8, bf16[2,64,256]{2,1,0:T(8,128)(2,1)S(1)} %copy-done.16, bf16[2,256,320]{2,1,0:T(8,128)(2,1)S(1)} %copy-done.3, bf16[2,128,256]{2,1,0:T(8,128)(2,1)S(1)} %copy-done.14, ...), custom_call_target="tpu_custom_call" | custom-call | tf_op jit(solution)/shard_map/pallas_call | solution.py:593
  74.2 9.4 %all-to-all-start.3 = ((s16[16,7,8,128]{3,2,1,0:T(8,128)(2,1)}), s16[16,7,8,128]{3,2,1,0:T(8,128)(2,1)S(1)}, u32[]{:S(2)}, u32[]{:S(2)}) async-start(s16[16,7,8,128]{3,2,1,0:T(8,128)(2,1)} %shard_map.262), calls=%async_computation.3 | async-start | bytes 458752 | tf_op jit(solution)/shard_map/all_to_all | solution.py:552
  83.7 3.1 %shard_map.263 = (s16[32,5,8,128]{3,2,1,0:T(8,128)(2,1)S(1)}, bf16[32,64,128]{2,1,0:T(8,128)(2,1)S(1)}, bf16[32,64,128]{2,1,0:T(8,128)(2,1)S(1)}) custom-call(s32[32,3]{1,0:T(8,128)S(1)} %bitcast.9, f32[3,32,8,128]{3,2,1,0:T(8,128)S(1)} %get-tuple-element.26.turned, bf16[32,3,8,128]{3,2,1,0:T(8,128)(2,1)S(1)} %copy-done.1), custom_call_target="tpu_custom_call" | custom-call | tf_op jit(solution)/shard_map/pallas_call | solution.py:597
  86.8 10.0 %all-to-all-done.3.values = s16[16,7,8,128]{3,2,1,0:T(8,128)(2,1)S(1)} async-done(((s16[16,7,8,128]{3,2,1,0:T(8,128)(2,1)}), s16[16,7,8,128]{3,2,1,0:T(8,128)(2,1)S(1)}, u32[]{:S(2)}, u32[]{:S(2)}) %all-to-all-start.3) | async-done | bytes 229408 | tf_op jit(solution)/shard_map/all_to_all | solution.py:552
  96.8 1.2 %shard_map.264 = s16[32,8,8,128]{3,2,1,0:T(8,128)(2,1)S(1)} custom-call(bf16[2,256,256]{2,1,0:T(8,128)(2,1)S(1)} %copy-done.6, bf16[2,128,256]{2,1,0:T(8,128)(2,1)S(1)} %copy-done.9, f32[2,32,1,128]{3,2,1,0:T(1,128)S(1)} %copy-done.12, s16[16,7,8,128]{3,2,1,0:T(8,128)(2,1)S(1)} %all-to-all-done.3.values, s16[32,5,8,128]{3,2,1,0:T(8,128)(2,1)S(1)} %get-tuple-element.27.replies), custom_call_target="tpu_custom_call" | custom-call | tf_op jit(solution)/shard_map/pallas_call | solution.py:599
  98.1 19.9 %all_to_all.25.values = s16[32,8,8,128]{3,2,1,0:T(8,128)(2,1)S(1)} all-to-all(s16[32,8,8,128]{3,2,1,0:T(8,128)(2,1)S(1)} %shard_map.264), channel_id=1, replica_groups=mesh['row'=16,'col'=32] {'col'}, dimensions={0} | all-to-all | bytes 1048576 | tf_op jit(solution)/shard_map/all_to_all | solution.py:552
  117.9 2.2 %shard_map.265 = (f32[3,16,8,256]{3,2,1,0:T(8,128)}, f32[3,32,128]{2,1,0:T(8,128)}) custom-call(s32[64]{0:T(128)S(1)} %get-tuple-element.17._.slots, bf16[2,256,256]{2,1,0:T(8,128)(2,1)S(1)} %copy-done.5, s16[32,8,8,128]{3,2,1,0:T(8,128)(2,1)S(1)} %all_to_all.25.values, bf16[32,3,8,128]{3,2,1,0:T(8,128)(2,1)S(1)} %copy-done.1, ...), custom_call_target="tpu_custom_call" | custom-call | tf_op jit(solution)/shard_map/pallas_call | solution.py:602
  (49 shorter events, 0.4 us)
Async XLA Ops:
  0.6 14.1 %copy-start = (f32[3,16,8,256]{3,2,1,0:T(8,128)S(1)}, f32[3,16,8,256]{3,2,1,0:T(8,128)}, u32[]{:S(2)}) copy-start(f32[3,16,8,256]{3,2,1,0:T(8,128)} %velocity.5) | copy-start | bytes 1179652
  4.3 20.1 %all-to-all-start = ((s16[32,5,8,128]{3,2,1,0:T(8,128)(2,1)}), s16[32,5,8,128]{3,2,1,0:T(8,128)(2,1)S(1)}, u32[]{:S(2)}, u32[]{:S(2)}) async-start(s16[32,5,8,128]{3,2,1,0:T(8,128)(2,1)} %get-tuple-element.20), calls=%async_computation | async-start | bytes 655360 | tf_op jit(solution)/shard_map/all_to_all | solution.py:552
  14.7 9.8 %copy-start.2 = (bf16[2,256,256]{2,1,0:T(8,128)(2,1)S(1)}, bf16[2,256,256]{2,1,0:T(8,128)(2,1)}, u32[]{:S(2)}) copy-start(bf16[2,256,256]{2,1,0:T(8,128)(2,1)} %constant.110.clone.table) | copy-start | bytes 786436
  15.3 11.5 %collective-permute-start = (f32[3,1,8,256]{3,2,1,0:T(8,128)S(1)}, f32[3,1,8,256]{3,2,1,0:T(8,128)S(1)}, u32[]{:S(2)}, u32[]{:S(2)}) collective-permute-start(f32[3,1,8,256]{3,2,1,0:T(8,128)S(1)} %get-tuple-element.18), channel_id=1, source_target_pairs={{0,32},{32,64},{64,96},{96,128},{128,160},{160,192},{192,224},{224... | collective-permute-start | bytes 73736 | tf_op jit(solution)/shard_map/ppermute | solution.py:557
  17.3 9.6 %collective-permute-start.1 = (f32[3,16,1,256]{3,2,1,0:T(1,128)S(1)}, f32[3,16,1,256]{3,2,1,0:T(1,128)S(1)}, u32[]{:S(2)}, u32[]{:S(2)}) collective-permute-start(f32[3,16,1,256]{3,2,1,0:T(1,128)S(1)} %get-tuple-element.19), channel_id=1, source_target_pairs={{0,1},{1,2},{2,3},{3,4},{4,5},{5,6},{6,7},{7,8},{8,9},{9,10},{10,1... | collective-permute-start | bytes 147464 | tf_op jit(solution)/shard_map/ppermute | solution.py:557
  26.9 17.8 %copy-start.12 = (f32[2,32,1,128]{3,2,1,0:T(1,128)S(1)}, f32[2,32,1,128]{3,2,1,0:T(1,128)}, u32[]{:S(2)}) copy-start(f32[2,32,1,128]{3,2,1,0:T(1,128)} %constant.113.clone.twiddle) | copy-start | bytes 98308
  26.9 17.8 %copy-start.17 = (f32[2,32,1,128]{3,2,1,0:T(1,128)S(1)}, f32[2,32,1,128]{3,2,1,0:T(1,128)}, u32[]{:S(2)}) copy-start(f32[2,32,1,128]{3,2,1,0:T(1,128)} %constant.115.clone.side_twiddle) | copy-start | bytes 98308
  28.4 16.3 %copy-start.7 = (bf16[2,256,256]{2,1,0:T(8,128)(2,1)S(1)}, bf16[2,256,256]{2,1,0:T(8,128)(2,1)}, u32[]{:S(2)}) copy-start(bf16[2,256,256]{2,1,0:T(8,128)(2,1)} %constant.111.clone.left) | copy-start | bytes 786436
  28.4 16.3 %copy-start.10 = (bf16[2,128,256]{2,1,0:T(8,128)(2,1)S(1)}, bf16[2,128,256]{2,1,0:T(8,128)(2,1)}, u32[]{:S(2)}) copy-start(bf16[2,128,256]{2,1,0:T(8,128)(2,1)} %constant.114.clone.side_lanes) | copy-start | bytes 393220
  28.4 16.3 %copy-start.11 = (bf16[2,128,256]{2,1,0:T(8,128)(2,1)S(1)}, bf16[2,128,256]{2,1,0:T(8,128)(2,1)}, u32[]{:S(2)}) copy-start(bf16[2,128,256]{2,1,0:T(8,128)(2,1)} %constant.112.clone.lanes) | copy-start | bytes 393220
  28.4 16.3 %all-to-all-start.1 = ((s16[32,4,8,128]{3,2,1,0:T(8,128)(2,1)}), s16[32,4,8,128]{3,2,1,0:T(8,128)(2,1)S(1)}, u32[]{:S(2)}, u32[]{:S(2)}) async-start(s16[32,4,8,128]{3,2,1,0:T(8,128)(2,1)} %shard_map.260), calls=%async_computation.1 | async-start | bytes 524288 | tf_op jit(solution)/shard_map/all_to_all | solution.py:552
  46.5 10.2 %copy-start.19 = (s32[320]{0:T(512)S(1)}, s32[320]{0:T(512)}, u32[]{:S(2)}) copy-start(s32[320]{0:T(512)} %constant.118.clone) | copy-start | bytes 3844
  46.5 23.7 %all-to-all-start.2 = ((s16[16,7,8,128]{3,2,1,0:T(8,128)(2,1)}), s16[16,7,8,128]{3,2,1,0:T(8,128)(2,1)S(1)}, u32[]{:S(2)}, u32[]{:S(2)}) async-start(s16[16,7,8,128]{3,2,1,0:T(8,128)(2,1)} %shard_map.261), calls=%async_computation.2 | async-start | bytes 458752 | tf_op jit(solution)/shard_map/all_to_all | solution.py:552
  58.1 12.2 %copy-start.14 = (bf16[2,128,256]{2,1,0:T(8,128)(2,1)S(1)}, bf16[2,128,256]{2,1,0:T(8,128)(2,1)}, u32[]{:S(2)}) copy-start(bf16[2,128,256]{2,1,0:T(8,128)(2,1)} %constant.122.clone.lanes) | copy-start | bytes 393220
  58.1 12.2 %copy-start.15 = (bf16[128,256]{1,0:T(8,128)(2,1)S(1)}, bf16[128,256]{1,0:T(8,128)(2,1)}, u32[]{:S(2)}) copy-start(bf16[128,256]{1,0:T(8,128)(2,1)} %constant.125.clone.flips) | copy-start | bytes 196612
  58.1 12.2 %copy-start.16 = (bf16[2,64,256]{2,1,0:T(8,128)(2,1)S(1)}, bf16[2,64,256]{2,1,0:T(8,128)(2,1)}, u32[]{:S(2)}) copy-start(bf16[2,64,256]{2,1,0:T(8,128)(2,1)} %constant.120.clone.left_extra) | copy-start | bytes 196612
  58.4 11.8 %copy-start.3 = (bf16[2,256,320]{2,1,0:T(8,128)(2,1)S(1)}, bf16[2,256,320]{2,1,0:T(8,128)(2,1)}, u32[]{:S(2)}) copy-start(bf16[2,256,320]{2,1,0:T(8,128)(2,1)} %constant.121.clone.back) | copy-start | bytes 983044
  58.5 11.8 %copy-start.4 = (f32[2,40,8,128]{3,2,1,0:T(8,128)S(1)}, f32[2,40,8,128]{3,2,1,0:T(8,128)}, u32[]{:S(2)}) copy-start(f32[2,40,8,128]{3,2,1,0:T(8,128)} %constant.124.clone.twiddle) | copy-start | bytes 983044
  58.5 11.8 %copy-start.8 = (bf16[2,256,256]{2,1,0:T(8,128)(2,1)S(1)}, bf16[2,256,256]{2,1,0:T(8,128)(2,1)}, u32[]{:S(2)}) copy-start(bf16[2,256,256]{2,1,0:T(8,128)(2,1)} %constant.119.clone.left) | copy-start | bytes 786436
  58.5 11.8 %copy-start.13 = (bf16[2,128,256]{2,1,0:T(8,128)(2,1)S(1)}, bf16[2,128,256]{2,1,0:T(8,128)(2,1)}, u32[]{:S(2)}) copy-start(bf16[2,128,256]{2,1,0:T(8,128)(2,1)} %constant.123.clone.lanes_back) | copy-start | bytes 393220
  74.2 22.6 %all-to-all-start.3 = ((s16[16,7,8,128]{3,2,1,0:T(8,128)(2,1)}), s16[16,7,8,128]{3,2,1,0:T(8,128)(2,1)S(1)}, u32[]{:S(2)}, u32[]{:S(2)}) async-start(s16[16,7,8,128]{3,2,1,0:T(8,128)(2,1)} %shard_map.262), calls=%async_computation.3 | async-start | bytes 458752 | tf_op jit(solution)/shard_map/all_to_all | solution.py:552
  83.6 13.2 %copy-start.6 = (bf16[2,256,256]{2,1,0:T(8,128)(2,1)S(1)}, bf16[2,256,256]{2,1,0:T(8,128)(2,1)}, u32[]{:S(2)}) copy-start(bf16[2,256,256]{2,1,0:T(8,128)(2,1)} %constant.126.clone.back) | copy-start | bytes 786436
  83.6 13.2 %copy-start.9 = (bf16[2,128,256]{2,1,0:T(8,128)(2,1)S(1)}, bf16[2,128,256]{2,1,0:T(8,128)(2,1)}, u32[]{:S(2)}) copy-start(bf16[2,128,256]{2,1,0:T(8,128)(2,1)} %constant.127.clone.lanes) | copy-start | bytes 393220
  98.0 19.9 %copy-start.5 = (bf16[2,256,256]{2,1,0:T(8,128)(2,1)S(1)}, bf16[2,256,256]{2,1,0:T(8,128)(2,1)}, u32[]{:S(2)}) copy-start(bf16[2,256,256]{2,1,0:T(8,128)(2,1)} %constant.128.clone.back) | copy-start | bytes 786436
  (3 other events, 10.8 us)
